TPU v7x, 256 devices: a whole 4x4x8 slice. The times are simulated.
256 devices in a mesh: feat: 16 (over z, core), dom: 16 (over x, y).
Axes of the slice: x: 4, y: 4, z: 8, core: 2. Of those that a mesh axis runs over, the one named last changes fastest.
Arguments:
- features: bfloat16 [16, 1024, 9216], P('dom', 'feat'), may hold values from -6 to 6
- w1_self: bfloat16 [1024, 256], P('feat'), may hold values from -0.1875 to 0.1875
- w1_neigh: bfloat16 [1024, 256], P('feat'), may hold values from -0.1875 to 0.1875
- w2_self: bfloat16 [256, 256], replicated, may hold values from -0.375 to 0.375
- w2_neigh: bfloat16 [256, 256], replicated, may hold values from -0.375 to 0.375
- neigh_one: int32 [16, 10, 4608], P('dom'), may hold values from 0 to 9215
- send_rows: int32 [16, 16, 16, 128], P('dom', 'feat'), may hold values from 0 to 287
- recv_count: int32 [16, 16, 16], P(None, 'feat', 'dom'), may hold values from 1 to 128, as said below
- neigh_two: int32 [16, 16, 256, 15], P('dom', 'feat'), may hold values from 0 to 2047, as said below
- seed_rows: int32 [16, 16, 256], P('dom', 'feat'), may hold values from 0 to 287, as said below
- d_out: bfloat16 [16, 16, 256, 256], P('dom', 'feat'), may hold values from -0.0625 to 0.0625
Outputs:
- layer_two: bfloat16 [16, 16, 256, 256], P('dom', 'feat')
- grad_w1_self: float32 [1024, 256], P('feat')
- grad_w1_neigh: float32 [1024, 256], P('feat')
- grad_w2_self: float32 [256, 256], replicated
- grad_w2_neigh: float32 [256, 256], replicated
Inputs may be any that keep to these rules, and one draw needn't show every extreme that they name: `neigh_one`: columns of the partition's 9216 input nodes. `send_rows`: rows among the sending device's 288 owned nodes. `recv_count`: the live slots of a buffer are its leading ones; every receiver gets a full buffer of 128 live rows from some source, and some receiver gets full buffers from every source. `neigh_two`: each is below the total of the receiving device's counts; on every device some seed names the last live row. `seed_rows`: distinct within one device.
All inputs are finite; a program needn't handle non-finite values.
Results may differ from a plain program's by a relative error of at most 0.0051.
Values may be sent and summed in bfloat16 or wider, within the bound.
No kernel may reach another device: no remote copies, remote signals or barrier semaphores. Data moves between devices by JAX's collectives and lax.ppermute only.
A program may use at most 64 MiB of HBM per device.

v0:
```python
import jax
import jax.numpy as jnp
from jax import lax
from jax.sharding import PartitionSpec as P


def rows_of(source_table, index_rows):
    return jnp.take(source_table, index_rows, axis=0)


def contract_rows(left_side, right_side):
    return lax.dot_general(
        left_side, right_side, (((0,), (0,)), ((), ())), preferred_element_type=jnp.float32
    )


def contract_cols(left_side, right_side):
    return lax.dot_general(
        left_side, right_side, (((1,), (1,)), ((), ())), preferred_element_type=jnp.float32
    )


def per_device(
    features,
    w1_self,
    w1_neigh,
    w2_self,
    w2_neigh,
    neigh_one,
    send_rows,
    recv_count,
    neigh_two,
    seed_rows,
    d_out,
):
    feature_table = features[0]
    neigh_lists = neigh_one[0]
    target_rows = neigh_lists.shape[1]
    fan_one = neigh_lists.shape[0]
    running = jnp.zeros((feature_table.shape[0], target_rows), jnp.float32)
    for column in range(fan_one):
        running = running + jnp.take(feature_table, neigh_lists[column], axis=1).astype(jnp.float32)
    mean_one = (running / fan_one).astype(jnp.bfloat16)
    own_self = feature_table[:, :target_rows]
    owned_rows = target_rows // lax.axis_size("feat")
    hidden_width = w1_self.shape[1]
    left_self = own_self
    left_mean = mean_one
    pre_one = lax.psum_scatter(
        contract_rows(left_self, w1_self) + contract_rows(left_mean, w1_neigh),
        "feat",
        scatter_dimension=0,
        tiled=True,
    )
    hidden = jax.nn.elu(pre_one).astype(jnp.bfloat16)
    send_index = send_rows[0, 0]
    peer_count = send_index.shape[0]
    slot_count = send_index.shape[1]
    outgoing = rows_of(hidden, send_index.reshape(-1)).reshape(peer_count, slot_count, hidden_width)
    incoming = lax.all_to_all(outgoing, "dom", split_axis=0, concat_axis=0, tiled=True)
    flat_in = incoming.reshape(peer_count * slot_count, hidden_width)
    counts = recv_count[:, 0, 0]
    starts = jnp.cumsum(counts) - counts
    positions = neigh_two[0, 0]
    source = jnp.sum((positions[:, :, None] >= starts[None, None, 1:]).astype(jnp.int32), axis=2)
    picked = (source[:, :, None] == jnp.arange(peer_count, dtype=jnp.int32)).astype(jnp.int32)
    offset_of = jnp.sum(picked * starts[None, None, :], axis=2)
    where_in = source * slot_count + positions - offset_of
    fan_two = positions.shape[1]
    seed_count = positions.shape[0]
    running_two = jnp.zeros((seed_count, hidden_width), jnp.float32)
    for column in range(fan_two):
        running_two = running_two + rows_of(flat_in, where_in[:, column]).astype(jnp.float32)
    mean_two = (running_two / fan_two).astype(jnp.bfloat16)
    seeds = seed_rows[0, 0]
    self_two = rows_of(hidden, seeds)
    grad_out = d_out[0, 0]
    layer_out = (
        jnp.dot(self_two, w2_self, preferred_element_type=jnp.float32)
        + jnp.dot(mean_two, w2_neigh, preferred_element_type=jnp.float32)
    ).astype(jnp.bfloat16)
    local_w2_self = contract_rows(self_two, grad_out)
    local_w2_neigh = contract_rows(mean_two, grad_out)
    d_self = contract_cols(grad_out, w2_self)
    d_mean = contract_cols(grad_out, w2_neigh) / fan_two
    slot_sum = jnp.zeros((peer_count * slot_count, hidden_width), jnp.float32)
    for column in range(fan_two):
        slot_sum = slot_sum.at[where_in[:, column]].add(d_mean)
    slot_grad = slot_sum.astype(jnp.bfloat16).reshape(peer_count, slot_count, hidden_width)
    returned = lax.all_to_all(slot_grad, "dom", split_axis=0, concat_axis=0, tiled=True)
    d_hidden = jnp.zeros((owned_rows, hidden_width), jnp.float32)
    d_hidden = d_hidden.at[send_index.reshape(-1)].add(
        returned.reshape(-1, hidden_width).astype(jnp.float32)
    )
    d_hidden = d_hidden.at[seeds].add(d_self)
    elu_slope = jnp.where(pre_one > 0, 1.0, jnp.exp(jnp.minimum(pre_one, 0.0)))
    d_pre = (d_hidden * elu_slope).astype(jnp.bfloat16)
    piece = lax.all_gather(d_pre, "feat", axis=0, tiled=True)
    left_self = own_self
    left_mean = mean_one
    first_self = jnp.dot(left_self, piece, preferred_element_type=jnp.float32)
    first_mean = jnp.dot(left_mean, piece, preferred_element_type=jnp.float32)
    first_self, first_mean = lax.psum((first_self, first_mean), "dom")
    second_self, second_mean = lax.psum((local_w2_self, local_w2_neigh), ("feat", "dom"))
    return (layer_out[None, None], first_self, first_mean, second_self, second_mean)


def solution(mesh):
    return jax.shard_map(
        per_device,
        mesh=mesh,
        in_specs=(
            P("dom", "feat", None),
            P("feat", None),
            P("feat", None),
            P(),
            P(),
            P("dom", None, None),
            P("dom", "feat", None, None),
            P(None, "feat", "dom"),
            P("dom", "feat", None, None),
            P("dom", "feat", None),
            P("dom", "feat", None, None),
        ),
        out_specs=(P("dom", "feat", None, None), P("feat", None), P("feat", None), P(), P()),
        check_vma=False,
    )
```

profile of v0, /device:TPU:1, one launch (start us, length us, event | category | flops | bytes accessed | tf_op | source)
XLA Modules:
  0.0 690.4 jit_solution(7600817708877585368)
XLA Ops:
  11.5 10.1 %gather_fusion.2 = bf16[4608,64]{1,0:T(8,128)(2,1)} fusion(bf16[64,9216]{0,1:T(8,128)(2,1)S(1)} %bitcast.99, s32[5120]{0:T(1024)S(1)} %pad_clamp_fusion.9), kind=kCustom, calls=%fused_computation.clone | custom fusion | bytes 1198080 | tf_op jit(solution)/shard_map/jit(_take)/gather | solution.py:42
  21.6 10.1 %gather_fusion.3 = bf16[4608,64]{1,0:T(8,128)(2,1)} fusion(bf16[64,9216]{0,1:T(8,128)(2,1)S(1)} %bitcast.100, s32[5120]{0:T(1024)S(1)} %pad_clamp_fusion.8), kind=kCustom, calls=%fused_computation.2.clone | custom fusion | bytes 1198080 | tf_op jit(solution)/shard_map/jit(_take)/gather | solution.py:42
  31.7 10.1 %gather_fusion.4 = bf16[4608,64]{1,0:T(8,128)(2,1)} fusion(bf16[64,9216]{0,1:T(8,128)(2,1)S(1)} %bitcast.101, s32[5120]{0:T(1024)S(1)} %pad_clamp_fusion.7), kind=kCustom, calls=%fused_computation.3.clone | custom fusion | bytes 1198080 | tf_op jit(solution)/shard_map/jit(_take)/gather | solution.py:42
  41.8 10.1 %gather_fusion.5 = bf16[4608,64]{1,0:T(8,128)(2,1)} fusion(bf16[64,9216]{0,1:T(8,128)(2,1)S(1)} %bitcast.102, s32[5120]{0:T(1024)S(1)} %pad_clamp_fusion.6), kind=kCustom, calls=%fused_computation.4.clone | custom fusion | bytes 1198080 | tf_op jit(solution)/shard_map/jit(_take)/gather | solution.py:42
  51.9 10.1 %gather_fusion.6 = bf16[4608,64]{1,0:T(8,128)(2,1)} fusion(bf16[64,9216]{0,1:T(8,128)(2,1)S(1)} %bitcast.103, s32[5120]{0:T(1024)S(1)} %pad_clamp_fusion.5), kind=kCustom, calls=%fused_computation.5.clone | custom fusion | bytes 1198080 | tf_op jit(solution)/shard_map/jit(_take)/gather | solution.py:42
  62.1 10.1 %gather_fusion.7 = bf16[4608,64]{1,0:T(8,128)(2,1)} fusion(bf16[64,9216]{0,1:T(8,128)(2,1)S(1)} %bitcast.104, s32[5120]{0:T(1024)S(1)} %pad_clamp_fusion.4), kind=kCustom, calls=%fused_computation.6.clone | custom fusion | bytes 1198080 | tf_op jit(solution)/shard_map/jit(_take)/gather | solution.py:42
  72.2 10.1 %gather_fusion.8 = bf16[4608,64]{1,0:T(8,128)(2,1)} fusion(bf16[64,9216]{0,1:T(8,128)(2,1)S(1)} %bitcast.105, s32[5120]{0:T(1024)S(1)} %pad_clamp_fusion.3), kind=kCustom, calls=%fused_computation.7.clone | custom fusion | bytes 1198080 | tf_op jit(solution)/shard_map/jit(_take)/gather | solution.py:42
  82.3 10.1 %gather_fusion.9 = bf16[4608,64]{1,0:T(8,128)(2,1)} fusion(bf16[64,9216]{0,1:T(8,128)(2,1)S(1)} %bitcast.106, s32[5120]{0:T(1024)S(1)} %pad_clamp_fusion.2), kind=kCustom, calls=%fused_computation.8.clone | custom fusion | bytes 1198080 | tf_op jit(solution)/shard_map/jit(_take)/gather | solution.py:42
  92.4 10.1 %gather_fusion.10 = bf16[4608,64]{1,0:T(8,128)(2,1)} fusion(bf16[64,9216]{0,1:T(8,128)(2,1)S(1)} %bitcast.107, s32[5120]{0:T(1024)S(1)} %pad_clamp_fusion.1), kind=kCustom, calls=%fused_computation.9.clone | custom fusion | bytes 1198080 | tf_op jit(solution)/shard_map/jit(_take)/gather | solution.py:42
  102.6 10.1 %gather_fusion.11 = bf16[4608,64]{1,0:T(8,128)(2,1)} fusion(bf16[64,9216]{0,1:T(8,128)(2,1)S(1)} %bitcast.108, s32[5120]{0:T(1024)S(1)} %pad_clamp_fusion), kind=kCustom, calls=%fused_computation.10.clone | custom fusion | bytes 1198080 | tf_op jit(solution)/shard_map/jit(_take)/gather | solution.py:42
  116.8 10.3 %multiply_convert_fusion = bf16[64,4608]{0,1:T(8,128)(2,1)S(1)} fusion(bf16[4608,64]{1,0:T(8,128)(2,1)} %gather_fusion.11, bf16[4608,64]{1,0:T(8,128)(2,1)S(1)} %copy-done.11, bf16[4608,64]{1,0:T(8,128)(2,1)S(1)} %copy-done.10, bf16[4608,64]{1,0:T(8,128)(2,1)S(1)} %copy-done.9, bf16[4608,64]{1,0:T(8,128)(2,1)S(1)} %copy-done.8, ...), kind=kLoop, calls=%fused_computation.45 | loop fusion | flops 9142272 | bytes 6534144 | tf_op jit(solution)/shard_map/convert_element_type | solution.py:43
  141.2 4.9 scatter_fusion.1
  146.0 4.8 scatter_fusion.2
  174.6 4.8 scatter_fusion.8
  179.3 4.8 scatter_fusion.9
  188.8 4.9 scatter_fusion.11
  193.8 4.8 scatter_fusion.12
  206.0 7.5 %all-to-all-start.1 = ((bf16[16,128,256]{2,1,0:T(8,128)(2,1)}), bf16[16,128,256]{2,1,0:T(8,128)(2,1)S(1)}, u32[]{:S(2)}, u32[]{:S(2)}) async-start(bf16[16,128,256]{2,1,0:T(8,128)(2,1)} %bitcast.53), calls=%async_computation.2 | async-start | bytes 2097152 | tf_op jit(solution)/shard_map/all_to_all | solution.py:90
  230.1 11.0 %scatter_custom_fusion.15 = f32[288,256]{1,0:T(8,128)S(1)} fusion(s32[2048]{0:T(1024)S(1)} %bitcast.115, bf16[2048,256]{1,0:T(8,128)(2,1)} %bitcast.111, f32[]{:T(128)} %constant.47.clone.1), kind=kCustom, calls=%fused_computation.46 | custom fusion | flops 1048576 | bytes 1343492 | tf_op jit(solution)/shard_map/scatter-add | solution.py:92
  250.3 9.0 %gather_fusion.1 = bf16[2048,256]{1,0:T(8,128)(2,1)} fusion(bf16[288,256]{1,0:T(8,128)(2,1)S(1)} %get-tuple-element.22, s32[2048]{0:T(1024)S(1)} %broadcast_clamp_fusion), kind=kCustom, calls=%fused_computation.26 | custom fusion | bytes 2105344 | tf_op jit(solution)/shard_map/jit(_take)/gather | solution.py:8
  261.5 5.8 all-to-all-start
  271.8 10.7 %all-to-all-done = bf16[16,128,256]{2,1,0:T(8,128)(2,1)} async-done(((bf16[16,128,256]{2,1,0:T(8,128)(2,1)}), bf16[16,128,256]{2,1,0:T(8,128)(2,1)}, u32[]{:S(2)}, u32[]{:S(2)}) %all-to-all-start) | async-done | bytes 1048608 | tf_op jit(solution)/shard_map/all_to_all | solution.py:60
  334.5 247.5 %all-reduce.5.cloned.1.call-done = (f32[256,256]{1,0:T(8,128)}, f32[256,256]{1,0:T(8,128)}) async-done(((f32[256,256]{1,0:T(8,128)}, f32[256,256]{1,0:T(8,128)}), (f32[256,256]{1,0:T(8,128)}, f32[256,256]{1,0:T(8,128)})) %all-reduce.5.cloned.1.call-update) | async-done | bytes 524304 | tf_op jit(solution)/shard_map/psum | solution.py:104
  582.1 95.1 %all-reduce.7.cloned.1.call-done = (f32[64,256]{1,0:T(8,128)}, f32[64,256]{1,0:T(8,128)}) async-done(((f32[64,256]{1,0:T(8,128)}, f32[64,256]{1,0:T(8,128)}), (f32[64,256]{1,0:T(8,128)}, f32[64,256]{1,0:T(8,128)})) %all-reduce.7.cloned.1.call-update) | async-done | bytes 131088 | tf_op jit(solution)/shard_map/psum | solution.py:103
  (234 shorter events, 148.5 us)
Async XLA Ops:
  7.2 125.6 %copy-start = (bf16[1,1,256,256]{3,2,1,0:T(8,128)(2,1)S(1)}, bf16[1,1,256,256]{3,2,1,0:T(8,128)(2,1)}, u32[]{:S(2)}) copy-start(bf16[1,1,256,256]{3,2,1,0:T(8,128)(2,1)} %param.25) | copy-start | bytes 393220
  7.2 236.6 %reduce-scatter.2.cloned.1.call-start = ((), (), s32[]{:S(2)}) async-start(), calls=%async_computation.3 | async-start | bytes 5013504 | tf_op jit(solution)/shard_map/reduce_scatter | solution.py:49
  102.5 10.1 %copy-start.17 = (bf16[64,256]{1,0:T(8,128)(2,1)S(1)}, bf16[64,256]{1,0:T(8,128)(2,1)}, u32[]{:S(2)}) copy-start(bf16[64,256]{1,0:T(8,128)(2,1)} %param.16) | copy-start | bytes 98308
  116.7 11.3 %copy-start.18 = (bf16[64,256]{1,0:T(8,128)(2,1)S(1)}, bf16[64,256]{1,0:T(8,128)(2,1)}, u32[]{:S(2)}) copy-start(bf16[64,256]{1,0:T(8,128)(2,1)} %param.17) | copy-start | bytes 98308
  206.0 23.0 %all-to-all-start.1 = ((bf16[16,128,256]{2,1,0:T(8,128)(2,1)}), bf16[16,128,256]{2,1,0:T(8,128)(2,1)S(1)}, u32[]{:S(2)}, u32[]{:S(2)}) async-start(bf16[16,128,256]{2,1,0:T(8,128)(2,1)} %bitcast.53), calls=%async_computation.2 | async-start | bytes 2097152 | tf_op jit(solution)/shard_map/all_to_all | solution.py:90
  213.6 115.5 %all-gather.2.cloned.1.call-start = ((), (), s32[]{:S(2)}) async-start(), calls=%async_computation.4 | async-start | bytes 2506752 | tf_op jit(solution)/shard_map/all_gather | solution.py:98
  219.3 8.0 %copy-start.32 = (s32[256,1]{0,1:T(1,128)}, s32[256,1]{0,1:T(1,128)S(1)}, u32[]{:S(2)}) copy-start(s32[256,1]{0,1:T(1,128)S(1)} %get-tuple-element.47) | copy-start | bytes 3076
  219.3 8.0 %copy-start.34 = (s32[256,1]{0,1:T(1,128)}, s32[256,1]{0,1:T(1,128)S(1)}, u32[]{:S(2)}) copy-start(s32[256,1]{0,1:T(1,128)S(1)} %get-tuple-element.48) | copy-start | bytes 3076
  219.3 8.0 %copy-start.36 = (s32[256,1]{0,1:T(1,128)}, s32[256,1]{0,1:T(1,128)S(1)}, u32[]{:S(2)}) copy-start(s32[256,1]{0,1:T(1,128)S(1)} %get-tuple-element.45) | copy-start | bytes 3076
  241.2 8.5 %copy-start.33 = (s32[256,1]{0,1:T(1,128)S(1)}, s32[256,1]{0,1:T(1,128)}, u32[]{:S(2)}) copy-start(s32[256,1]{0,1:T(1,128)} %copy-done.32) | copy-start | bytes 3076
  241.2 8.5 %copy-start.35 = (s32[256,1]{0,1:T(1,128)S(1)}, s32[256,1]{0,1:T(1,128)}, u32[]{:S(2)}) copy-start(s32[256,1]{0,1:T(1,128)} %copy-done.34) | copy-start | bytes 3076
  241.2 9.0 %copy-start.19 = (s32[1,1,16,128]{3,2,1,0:T(8,128)S(1)}, s32[1,1,16,128]{3,2,1,0:T(8,128)}, u32[]{:S(2)}) copy-start(s32[1,1,16,128]{3,2,1,0:T(8,128)} %param.21) | copy-start | bytes 24580
  259.3 9.0 %copy-start.29 = (s32[256,1]{0,1:T(1,128)S(1)}, s32[256,1]{0,1:T(1,128)}, u32[]{:S(2)}) copy-start(s32[256,1]{0,1:T(1,128)} %copy-done.28) | copy-start | bytes 3076
  259.3 9.0 %copy-start.31 = (s32[256,1]{0,1:T(1,128)S(1)}, s32[256,1]{0,1:T(1,128)}, u32[]{:S(2)}) copy-start(s32[256,1]{0,1:T(1,128)} %copy-done.30) | copy-start | bytes 3076
  259.3 9.6 %copy-start.25 = (s32[256,1]{0,1:T(1,128)S(1)}, s32[256,1]{0,1:T(1,128)}, u32[]{:S(2)}) copy-start(s32[256,1]{0,1:T(1,128)} %copy-done.24) | copy-start | bytes 3076
  259.3 9.6 %copy-start.27 = (s32[256,1]{0,1:T(1,128)S(1)}, s32[256,1]{0,1:T(1,128)}, u32[]{:S(2)}) copy-start(s32[256,1]{0,1:T(1,128)} %copy-done.26) | copy-start | bytes 3076
  261.5 10.1 %copy-start.13 = (bf16[256,256]{1,0:T(8,128)(2,1)S(1)}, bf16[256,256]{1,0:T(8,128)(2,1)}, u32[]{:S(2)}) copy-start(bf16[256,256]{1,0:T(8,128)(2,1)} %param.18) | copy-start | bytes 393220
  261.5 21.0 %all-to-all-start = ((bf16[16,128,256]{2,1,0:T(8,128)(2,1)}), bf16[16,128,256]{2,1,0:T(8,128)(2,1)}, u32[]{:S(2)}, u32[]{:S(2)}) async-start(bf16[16,128,256]{2,1,0:T(8,128)(2,1)} %broadcast_select_fusion), calls=%async_computation.1 | async-start | bytes 2097152 | tf_op jit(solution)/shard_map/all_to_all | solution.py:60
  267.4 314.7 %all-reduce.5.cloned.1.call-start = ((), (), s32[]{:S(2)}) async-start(), calls=%async_computation.5 | async-start | bytes 1048576 | tf_op jit(solution)/shard_map/psum | solution.py:104
  313.5 12.5 %copy-start.45 = (pred[256]{0:T(512)(128)(4,1)S(1)}, pred[256]{0:T(512)(128)(4,1)}, u32[]{:S(2)}) copy-start(pred[256]{0:T(512)(128)(4,1)} %get-tuple-element.73) | copy-start | bytes 772
  313.5 12.5 %copy-start.46 = (pred[256]{0:T(512)(128)(4,1)S(1)}, pred[256]{0:T(512)(128)(4,1)}, u32[]{:S(2)}) copy-start(pred[256]{0:T(512)(128)(4,1)} %get-tuple-element.74) | copy-start | bytes 772
  313.5 12.5 %copy-start.47 = (pred[256]{0:T(512)(128)(4,1)S(1)}, pred[256]{0:T(512)(128)(4,1)}, u32[]{:S(2)}) copy-start(pred[256]{0:T(512)(128)(4,1)} %get-tuple-element.75) | copy-start | bytes 772
  313.5 12.5 %copy-start.48 = (pred[256]{0:T(512)(128)(4,1)S(1)}, pred[256]{0:T(512)(128)(4,1)}, u32[]{:S(2)}) copy-start(pred[256]{0:T(512)(128)(4,1)} %get-tuple-element.76) | copy-start | bytes 772
  329.0 348.1 %all-reduce.7.cloned.1.call-start = ((), (), s32[]{:S(2)}) async-start(), calls=%async_computation.6 | async-start | bytes 262144 | tf_op jit(solution)/shard_map/psum | solution.py:103
  (33 other events, 151.9 us)
Sparse Core Ops, SparseCore 0:
  131.1 64.4 reduce-scatter.1
  245.7 42.7 all-gather.1
  329.2 252.8 all-reduce.4
  585.7 91.3 all-reduce.6
where the time goes:
time: 700 us; the launch traced here: 690 us
  waiting for transfers between devices  354 us (51%)
  local copies, waits for them, and re-layouts  172 us (25%)
  other arithmetic  122 us (17%)
  between operations  14.9 us (2%)
  starting transfers between devices  13.8 us (2%)
  matrix products  13.2 us (2%)
    psum x1, waiting for transfers between devices, per_device(): lax.psum((local_w2_self, local_w2_neigh), ('feat', 'dom'))  248 us
    gather x10, local copies, waits for them, and re-layouts, per_device(): jnp.take(feature_table, neigh_lists[column], axis=1).astype(jnp.float32)  101 us
    psum x1, waiting for transfers between devices, per_device(): first_self, first_mean = lax.psum((first_self, first_mean), 'dom')  95.1 us
    scatter-add x15, other arithmetic, per_device(): slot_sum = slot_sum.at[where_in[:, column]].add(d_mean)  70.2 us
    gather x17, local copies, waits for them, and re-layouts, rows_of(): return jnp.take(source_table, index_rows, axis=0)  53.6 us
    unnamed x108, local copies, waits for them, and re-layouts  15.1 us
  transfers between devices with their start and end apart: 6, of which 4 were waited for; matrix products, arithmetic and copies ran while one was open for 25% of the time, Pallas kernels for 0%

commit v1 on v0

v1 whole, which is shorter than its diff:
```python
import jax
import jax.numpy as jnp
from jax import lax
from jax.experimental import pallas as pl
from jax.experimental.pallas import tpu as pltpu
from jax.sharding import PartitionSpec as P

BF = jnp.bfloat16
F32 = jnp.float32
I32 = jnp.int32
NF = 16
ND = 16
NZ = 8
COLS = 64
PAIR = 128
NIN = 9216
R1 = 4608
OWN = 288
HALF = R1 // 2
K1 = 10
K2 = 15
SEEDS = 256
SLOTS = 128
HID = 256
UNROLL = 16
VMEM = pl.BlockSpec(memory_space=pltpu.VMEM)
SMEM = pl.BlockSpec(memory_space=pltpu.SMEM)


def call(body, name, outs, ins, scratch=(), limit=48):
    return pl.pallas_call(
        body,
        name=name,
        out_shape=outs,
        in_specs=ins,
        out_specs=jax.tree.map(lambda _: VMEM, outs),
        scratch_shapes=list(scratch),
        compiler_params=pltpu.CompilerParams(vmem_limit_bytes=limit << 20),
    )


def shape(dims, dtype):
    return jax.ShapeDtypeStruct(dims, dtype)


def dot(a, b, ca=1, cb=0):
    return lax.dot_general(a, b, (((ca,), (cb,)), ((), ())), preferred_element_type=F32)


def pick_body(count_ref, neigh_ref, dout_ref, picks_ref, t_ref):
    start = jnp.int32(0)
    lanes = neigh_ref[...]
    d_out = dout_ref[...]
    row = lax.broadcasted_iota(I32, (SLOTS, SEEDS), 0)
    for s in range(ND):
        count = count_ref[s]
        position = jnp.where(row < count, row + start, -1)
        total = jnp.zeros((SLOTS, SEEDS), F32)
        for k in range(K2):
            total = total + jnp.where(position == lanes[k : k + 1, :], 1.0, 0.0)
        picks = total.astype(BF)
        picks_ref[s] = picks
        t_ref[s] = dot(picks, d_out).astype(BF)
        start = start + count


def fill_table(core, own_ref, other_ref, table, nodes, step=512):
    first = core == 0
    for c in range(0, nodes, step):
        own = own_ref[:, c : c + step].astype(F32)
        other = other_ref[:, c : c + step].astype(F32)
        low = jnp.where(first, own, other)
        high = jnp.where(first, other, own)
        table[c : c + step, :] = jnp.concatenate([low, high], axis=0).T


def self_body(core_ref, own_ref, other_ref, self_ref, table):
    core = core_ref[0]
    fill_table(core, own_ref, other_ref, table, R1)
    for z in range(NZ):
        base = pl.multiple_of((2 * z + core) * OWN, 32)
        self_ref[z] = table[pl.ds(base, OWN), :].astype(BF)


def mean_body(core_ref, own_ref, other_ref, index_ref, mean_ref, table, sums):
    fill_table(core_ref[0], own_ref, other_ref, table, NIN)

    def block(b, carry):
        base = pl.multiple_of(b * UNROLL, UNROLL)
        for j in range(UNROLL):
            rows = [table[pl.ds(index_ref[k * HALF + base + j], 1), :] for k in range(K1)]
            while len(rows) > 1:
                even = len(rows) // 2 * 2
                rows = [rows[i] + rows[i + 1] for i in range(0, even, 2)] + rows[even:]
            sums[pl.ds(base + j, 1), :] = rows[0]
        return carry

    lax.fori_loop(0, HALF // UNROLL, block, 0)
    for z in range(NZ):
        mean_ref[z] = (sums[z * OWN : (z + 1) * OWN, :] * (1.0 / K1)).astype(BF)


def split(x):
    high = x.astype(BF)
    return high, (x - high.astype(F32)).astype(BF)


def owner_body(t_ref, send_ref, seed_ref, dout_ref, w2s_ref, w2n_ref, x_ref, d_ref, dh_ref):
    d_out = dout_ref[...]
    row = lax.broadcasted_iota(I32, (OWN, SEEDS), 0)
    x = jnp.zeros((OWN, HID), F32)
    for q in range(0, ND, 2):
        lanes = jnp.concatenate([send_ref[q : q + 1, :], send_ref[q + 1 : q + 2, :]], axis=1)
        hot = jnp.where(row == lanes, 1.0, 0.0).astype(BF)
        x = x + dot(hot, t_ref[q * SLOTS : (q + 2) * SLOTS, :])
    x = x * (1.0 / K2)
    hot = jnp.where(row == seed_ref[...], 1.0, 0.0).astype(BF)
    d = dot(hot, d_out).astype(BF)
    high, low = split(x)
    w2n = w2n_ref[...]
    x_ref[...] = x
    d_ref[...] = d
    dh_ref[...] = dot(high, w2n, 1, 1) + dot(low, w2n, 1, 1) + dot(d, w2s_ref[...], 1, 1)


def main_body(
    self_ref, mean_ref, w_ref, x_ref, d_ref, dh_ref, send_ref, seed_ref, w2s_ref,
    g1_ref, g2_ref, out_ref, part_ref, w1,
):
    for f in range(NF):
        for q in range(ND):
            r, h = q // 2, q % 2
            base = f * COLS + (r % 4) * 16
            w1[r // 4, base : base + 16, h * 128 : (h + 1) * 128] = w_ref[q, f]
    pre = jnp.zeros((OWN, HID), F32)
    for z in range(NZ):
        pre = pre + dot(self_ref[z], w1[0, z * PAIR : (z + 1) * PAIR, :])
        pre = pre + dot(mean_ref[z], w1[1, z * PAIR : (z + 1) * PAIR, :])
    slope = jnp.exp(jnp.minimum(pre, 0.0))
    hidden = jnp.where(pre > 0, pre, slope - 1.0).astype(BF)
    d_pre = (dh_ref[...] * slope).astype(BF)
    for z in range(NZ):
        gs = dot(self_ref[z], d_pre, 0, 0).astype(BF)
        gn = dot(mean_ref[z], d_pre, 0, 0).astype(BF)
        g1_ref[2 * z, 0:COLS, :] = gs[0:COLS]
        g1_ref[2 * z + 1, 0:COLS, :] = gs[COLS:PAIR]
        g1_ref[2 * z, COLS:PAIR, :] = gn[0:COLS]
        g1_ref[2 * z + 1, COLS:PAIR, :] = gn[COLS:PAIR]
    high, low = split(x_ref[...])
    g2_ref[0:HID, :] = dot(hidden, d_ref[...], 0, 0)
    g2_ref[HID : 2 * HID, :] = dot(hidden, high, 0, 0) + dot(hidden, low, 0, 0)
    row = lax.broadcasted_iota(I32, (OWN, SEEDS), 0)
    for q in range(0, ND, 2):
        lanes = jnp.concatenate([send_ref[q : q + 1, :], send_ref[q + 1 : q + 2, :]], axis=1)
        hot = jnp.where(row == lanes, 1.0, 0.0).astype(BF)
        out_ref[q * SLOTS : (q + 2) * SLOTS, :] = dot(hot, hidden, 0, 0).astype(BF)
    hot = jnp.where(row == seed_ref[...], 1.0, 0.0).astype(BF)
    part_ref[...] = dot(dot(hot, hidden, 0, 0).astype(BF), w2s_ref[...])


def layer_body(in_ref, picks_ref, part_ref, w2n_ref, layer_ref):
    mean_two = (dot(picks_ref[...], in_ref[...], 0, 0) * (1.0 / K2)).astype(BF)
    layer_ref[...] = (part_ref[...] + dot(mean_two, w2n_ref[...])).astype(BF)


def swap(x, axis, groups=None):
    return lax.all_to_all(
        x, axis, split_axis=0, concat_axis=0, tiled=True, axis_index_groups=groups
    )


def to_all(x, axis, n):
    return swap(jnp.broadcast_to(x[None], (n,) + x.shape), axis)


def per_device(
    features, w1_self, w1_neigh, w2_self, w2_neigh, neigh_one, send_rows, recv_count,
    neigh_two, seed_rows, d_out,
):
    f = lax.axis_index("feat")
    q = lax.axis_index("dom")
    core = f % 2
    core_in = core.reshape(1)
    chips = [[2 * z + c for z in range(NZ)] for c in range(2)]
    own = features[0]
    other = lax.ppermute(own, "feat", [(i, i ^ 1) for i in range(NF)])

    w1 = jnp.concatenate([w1_self, w1_neigh], axis=0)
    piece = lax.dynamic_slice(w1, ((q // 2) * 16, (q % 2) * 128), (16, 128))
    piece = to_all(piece, "feat", NF)
    w1_all = to_all(piece, "dom", ND)

    send = send_rows[0, 0]
    seeds = seed_rows[0]
    grad_out = d_out[0, 0]
    picks, t_out = call(
        pick_body,
        "picks",
        (shape((ND, SLOTS, SEEDS), BF), shape((ND, SLOTS, HID), BF)),
        [SMEM, VMEM, VMEM],
    )(recv_count[:, 0, 0], neigh_two[0, 0].T, grad_out)
    t_in = swap(t_out, "dom")

    self_out = call(
        self_body,
        "self_rows",
        shape((NZ, OWN, PAIR), BF),
        [SMEM, VMEM, VMEM],
        [pltpu.VMEM((R1, PAIR), F32)],
    )(core_in, own, other)
    self_in = swap(self_out, "feat", chips)

    lists = neigh_one[0].reshape(K1, NZ, 2, OWN)
    lists = lax.dynamic_index_in_dim(lists, core, 2, keepdims=False).reshape(-1)
    mean_out = call(
        mean_body,
        "mean_rows",
        shape((NZ, OWN, PAIR), BF),
        [SMEM, VMEM, VMEM, SMEM],
        [pltpu.VMEM((NIN, PAIR), F32), pltpu.VMEM((HALF, PAIR), F32)],
    )(core_in, own, other, lists)
    mean_in = swap(mean_out, "feat", chips)

    x, d, d_hidden = call(
        owner_body,
        "owner_grads",
        (shape((OWN, HID), F32), shape((OWN, HID), BF), shape((OWN, HID), F32)),
        [VMEM] * 6,
    )(t_in.reshape(ND * SLOTS, HID), send, seeds, grad_out, w2_self, w2_neigh)

    g1, g2, outgoing, part = call(
        main_body,
        "project",
        (
            shape((NF, PAIR, HID), BF),
            shape((2 * HID, HID), F32),
            shape((ND * SLOTS, HID), BF),
            shape((SEEDS, HID), F32),
        ),
        [VMEM] * 9,
        [pltpu.VMEM((2, NF * COLS, HID), BF)],
    )(self_in, mean_in, w1_all, x, d, d_hidden, send, seeds, w2_self)

    g1 = jnp.sum(swap(g1, "feat").astype(F32), axis=0)
    g2 = jnp.sum(swap(g2.reshape(ND, 2 * HID // ND, HID), "dom"), axis=0)
    incoming = swap(outgoing.reshape(ND, SLOTS, HID), "dom").reshape(ND * SLOTS, HID)
    layer_out = call(layer_body, "layer_two", shape((SEEDS, HID), BF), [VMEM] * 4)(
        incoming, picks.reshape(ND * SLOTS, SEEDS), part, w2_neigh
    )

    g1 = jnp.sum(swap(g1.reshape(ND, PAIR // ND, HID), "dom"), axis=0)
    g2 = jnp.sum(to_all(g2, "feat", NF), axis=0)
    both = to_all(jnp.concatenate([g1, g2], axis=0), "dom", ND)
    g1 = both[:, : PAIR // ND].reshape(PAIR, HID)
    g2 = both[:, PAIR // ND :].reshape(2 * HID, HID)
    return (layer_out[None, None], g1[:COLS], g1[COLS:], g2[:HID], g2[HID:])


def solution(mesh):
    return jax.shard_map(
        per_device,
        mesh=mesh,
        in_specs=(
            P("dom", "feat", None),
            P("feat", None),
            P("feat", None),
            P(),
            P(),
            P("dom", None, None),
            P("dom", "feat", None, None),
            P(None, "feat", "dom"),
            P("dom", "feat", None, None),
            P("dom", "feat", None),
            P("dom", "feat", None, None),
        ),
        out_specs=(P("dom", "feat", None, None), P("feat", None), P("feat", None), P(), P()),
        check_vma=False,
    )
```

time: 700 us -> 250 us (0.36); the launches traced: 690 us -> 248 us
  waiting for transfers between devices: 354 us -> 114 us
  local copies, waits for them, and re-layouts: 172 us -> 14.9 us
  other arithmetic: 122 us -> 3.01 us
  starting transfers between devices: 13.8 us -> 52.4 us
  Pallas kernels: 0 us -> 35.5 us
  blocking collectives: 0 us -> 27.4 us
  between operations: 14.9 us -> 0.88 us
  matrix products: 13.2 us -> 0 us
    psum x2 -> x0, waiting for transfers between devices: 343 us -> none  [the longest x1 248 us: per_device(): lax.psum((local_w2_self, local_w2_neigh), ('feat', 'dom'))]
    gather x27 -> x0, local copies, waits for them, and re-layouts: 155 us -> none  [the longest x10 101 us: per_device(): jnp.take(feature_table, neigh_lists[column], axis=1).astype(jnp.float32)]
    all_to_all x2 -> x9, waiting for transfers between devices: 11.7 us -> 114 us  [swap(): lax.all_to_all(x, axis, split_axis=0, concat_axis=0, tiled=True, axis_ind...]
    scatter-add x17 -> x0, other arithmetic: 83.7 us -> none  [the longest x15 70.2 us: per_device(): slot_sum = slot_sum.at[where_in[:, column]].add(d_mean)]
    all_to_all x2 -> x9, starting transfers between devices: 13.4 us -> 52 us  [swap(): lax.all_to_all(x, axis, split_axis=0, concat_axis=0, tiled=True, axis_ind...]
    pallas_call x0 -> x6, Pallas kernels: none -> 35.5 us  [the longest x1 21.9 us: per_device(): call(mean_body, 'mean_rows', shape((NZ, OWN, PAIR), BF), [SMEM, VMEM, VME...]
    all_to_all x0 -> x2, blocking collectives: none -> 27.4 us  [swap(): lax.all_to_all(x, axis, split_axis=0, concat_axis=0, tiled=True, axis_ind...]
    convert_element_type x4 -> x0, other arithmetic: 16.9 us -> none  [the longest x1 10.3 us: per_device(): mean_one = (running / fan_one).astype(jnp.bfloat16)]
  transfers between devices with their start and end apart: 6 -> 10, of which waited for: 4 -> 7; matrix products, arithmetic and copies ran while one was open for 25% -> 4% of each run, Pallas kernels for 0% -> 12%
where the time goes in v1:
time: 250 us; the launch traced here: 248 us
  waiting for transfers between devices  114 us (46%)
  starting transfers between devices  52.4 us (21%)
  Pallas kernels  35.5 us (14%)
  blocking collectives  27.4 us (11%)
  local copies, waits for them, and re-layouts  14.9 us (6%)
  other arithmetic  3.01 us (1%)
    all_to_all x9, waiting for transfers between devices, swap(): lax.all_to_all(x, axis, split_axis=0, concat_axis=0, tiled=True, axis_ind...  114 us
    all_to_all x9, starting transfers between devices, swap(): lax.all_to_all(x, axis, split_axis=0, concat_axis=0, tiled=True, axis_ind...  52 us
    all_to_all x2, blocking collectives, swap(): lax.all_to_all(x, axis, split_axis=0, concat_axis=0, tiled=True, axis_ind...  27.4 us
    pallas_call x1, Pallas kernels, per_device(): call(mean_body, 'mean_rows', shape((NZ, OWN, PAIR), BF), [SMEM, VMEM, VME...  21.9 us
    pallas_call x1, Pallas kernels, per_device(): call(main_body, 'project', (shape((NF, PAIR, HID), BF), shape((2 * HID, H...  6.05 us
  transfers between devices with their start and end apart: 10, of which 7 were waited for; matrix products, arithmetic and copies ran while one was open for 4% of the time, Pallas kernels for 12%

profile of v1, /device:TPU:1, one launch (start us, length us, event | category | flops | bytes accessed | tf_op | source)
XLA Modules:
  0.0 248.3 jit_solution(2977162870834457747)
XLA Ops:
  2.0 10.1 %all-to-all-start.2 = ((bf16[16,16,128]{2,1,0:T(8,128)(2,1)}), bf16[16,16,128]{2,1,0:T(8,128)(2,1)S(1)}, u32[]{:S(2)}, u32[]{:S(2)}) async-start(bf16[16,16,128]{2,1,0:T(8,128)(2,1)} %broadcast_in_dim.10), calls=%async_computation.2 | async-start | bytes 131072 | tf_op jit(solution)/shard_map/all_to_all | solution.py:167
  14.4 4.9 %picks.1 = (bf16[16,128,256]{2,1,0:T(8,128)(2,1)S(1)}, bf16[16,128,256]{2,1,0:T(8,128)(2,1)}) custom-call(s32[16]{0:T(128)S(1)} %bitcast.38, s32[15,256]{1,0:T(8,128)S(1)} %bitcast.33, bf16[256,256]{1,0:T(8,128)(2,1)S(1)} %bitcast.30), custom_call_target="tpu_custom_call" | custom-call | tf_op jit(solution)/shard_map/picks/pallas_call | solution.py:196
  20.3 6.8 %all-to-all-start.4 = ((bf16[16,128,256]{2,1,0:T(8,128)(2,1)}), bf16[16,128,256]{2,1,0:T(8,128)(2,1)S(1)}, u32[]{:S(2)}, u32[]{:S(2)}) async-start(bf16[16,128,256]{2,1,0:T(8,128)(2,1)} %get-tuple-element.14), calls=%async_computation.4 | async-start | bytes 2097152 | tf_op jit(solution)/shard_map/all_to_all | solution.py:167
  27.5 16.1 %all-to-all-done.4 = bf16[16,128,256]{2,1,0:T(8,128)(2,1)S(1)} async-done(((bf16[16,128,256]{2,1,0:T(8,128)(2,1)}), bf16[16,128,256]{2,1,0:T(8,128)(2,1)S(1)}, u32[]{:S(2)}, u32[]{:S(2)}) %all-to-all-start.4) | async-done | bytes 1048608 | tf_op jit(solution)/shard_map/all_to_all | solution.py:167
  44.8 4.3 %all-to-all-start.3 = ((bf16[16,16,16,128]{3,2,1,0:T(8,128)(2,1)}), bf16[16,16,16,128]{3,2,1,0:T(8,128)(2,1)}, u32[]{:S(2)}, u32[]{:S(2)}) async-start(bf16[16,16,16,128]{3,2,1,0:T(8,128)(2,1)} %broadcast_in_dim.11), calls=%async_computation.3 | async-start | bytes 2097152 | tf_op jit(solution)/shard_map/all_to_all | solution.py:167
  50.5 13.3 %all-to-all-done.3.w_ref = bf16[16,16,16,128]{3,2,1,0:T(8,128)(2,1)} async-done(((bf16[16,16,16,128]{3,2,1,0:T(8,128)(2,1)}), bf16[16,16,16,128]{3,2,1,0:T(8,128)(2,1)}, u32[]{:S(2)}, u32[]{:S(2)}) %all-to-all-start.3) | async-done | bytes 1048608 | tf_op jit(solution)/shard_map/all_to_all | solution.py:167
  63.8 5.5 %all-to-all-start = ((bf16[8,288,128]{2,1,0:T(8,128)(2,1)}), bf16[8,288,128]{2,1,0:T(8,128)(2,1)}, u32[]{:S(2)}, u32[]{:S(2)}) async-start(bf16[8,288,128]{2,1,0:T(8,128)(2,1)} %copy-done.2), calls=%async_computation | async-start | bytes 1179648 | tf_op jit(solution)/shard_map/all_to_all | solution.py:167
  69.3 2.1 reduce
  71.4 1.9 reshape_squeeze.3
  73.3 1.9 dynamic-slice_reduce_fusion
  76.3 21.9 %mean_rows.1 = bf16[8,288,128]{2,1,0:T(8,128)(2,1)S(1)} custom-call(s32[1]{0:T(128)} %bitcast.core_ref, bf16[64,9216]{1,0:T(8,128)(2,1)S(1)} %bitcast.26, bf16[64,9216]{1,0:T(8,128)(2,1)S(1)} %collective-permute-done.other_ref, s32[23040]{0:T(1024)S(1)} %reshape.46.index_ref), custom_call_target="tpu_custom_call" | custom-call | tf_op jit(solution)/shard_map/mean_rows/pallas_call | solution.py:215
  99.1 6.8 %all-to-all-start.1 = ((bf16[8,288,128]{2,1,0:T(8,128)(2,1)}), bf16[8,288,128]{2,1,0:T(8,128)(2,1)S(1)}, u32[]{:S(2)}, u32[]{:S(2)}) async-start(bf16[8,288,128]{2,1,0:T(8,128)(2,1)} %copy-done.1), calls=%async_computation.1 | async-start | bytes 1179648 | tf_op jit(solution)/shard_map/all_to_all | solution.py:167
  106.8 12.7 %all-to-all-done.1.mean_ref = bf16[8,288,128]{2,1,0:T(8,128)(2,1)S(1)} async-done(((bf16[8,288,128]{2,1,0:T(8,128)(2,1)}), bf16[8,288,128]{2,1,0:T(8,128)(2,1)S(1)}, u32[]{:S(2)}, u32[]{:S(2)}) %all-to-all-start.1) | async-done | bytes 589856 | tf_op jit(solution)/shard_map/all_to_all | solution.py:167
  119.5 6.1 %project.1 = (bf16[16,128,256]{2,1,0:T(8,128)(2,1)}, f32[512,256]{1,0:T(8,128)S(1)}, bf16[2048,256]{1,0:T(8,128)(2,1)}, f32[256,256]{1,0:T(8,128)S(1)}) custom-call(bf16[8,288,128]{2,1,0:T(8,128)(2,1)} %all-to-all-done.self_ref, bf16[8,288,128]{2,1,0:T(8,128)(2,1)S(1)} %all-to-all-done.1.mean_ref, bf16[16,16,16,128]{3,2,1,0:T(8,128)(2,1)} %all-to-all-done.3.w_ref, ...), custom_call_target="tpu_custom_call" | custom-call | tf_op jit(solution)/shard_map/project/pallas_call | solution.py:231
  125.6 17.4 %all_to_all.55 = f32[16,32,256]{2,1,0:T(8,128)S(1)} all-to-all(f32[16,32,256]{2,1,0:T(8,128)S(1)} %bitcast.32), channel_id=1, replica_groups=mesh['feat'=16,'dom'=16] {'dom'}, dimensions={0} | all-to-all | bytes 1048576 | tf_op jit(solution)/shard_map/all_to_all | solution.py:167
  143.0 7.7 %all-to-all-start.6 = ((bf16[16,128,256]{2,1,0:T(8,128)(2,1)}), bf16[16,128,256]{2,1,0:T(8,128)(2,1)S(1)}, u32[]{:S(2)}, u32[]{:S(2)}) async-start(bf16[16,128,256]{2,1,0:T(8,128)(2,1)} %get-tuple-element.21), calls=%async_computation.6 | async-start | bytes 2097152 | tf_op jit(solution)/shard_map/all_to_all | solution.py:167
  150.7 27.9 %all-to-all-done.6 = bf16[16,128,256]{2,1,0:T(8,128)(2,1)S(1)} async-done(((bf16[16,128,256]{2,1,0:T(8,128)(2,1)}), bf16[16,128,256]{2,1,0:T(8,128)(2,1)S(1)}, u32[]{:S(2)}, u32[]{:S(2)}) %all-to-all-start.6) | async-done | bytes 1048608 | tf_op jit(solution)/shard_map/all_to_all | solution.py:167
  179.5 3.5 %all-to-all-start.9 = ((f32[16,32,256]{2,1,0:T(8,128)}), f32[16,32,256]{2,1,0:T(8,128)S(1)}, u32[]{:S(2)}, u32[]{:S(2)}) async-start(f32[16,32,256]{2,1,0:T(8,128)} %broadcast_in_dim.13), calls=%async_computation.9 | async-start | bytes 1048576 | tf_op jit(solution)/shard_map/all_to_all | solution.py:167
  183.2 17.2 %all-to-all-done.9 = f32[16,32,256]{2,1,0:T(8,128)S(1)} async-done(((f32[16,32,256]{2,1,0:T(8,128)}), f32[16,32,256]{2,1,0:T(8,128)S(1)}, u32[]{:S(2)}, u32[]{:S(2)}) %all-to-all-start.9) | async-done | bytes 524320 | tf_op jit(solution)/shard_map/all_to_all | solution.py:167
  200.3 10.0 %all_to_all.56 = f32[16,8,256]{2,1,0:T(8,128)S(1)} all-to-all(f32[16,8,256]{2,1,0:T(8,128)S(1)} %bitcast.39), channel_id=1, replica_groups=mesh['feat'=16,'dom'=16] {'dom'}, dimensions={0} | all-to-all | bytes 262144 | tf_op jit(solution)/shard_map/all_to_all | solution.py:167
  210.3 3.7 %all-to-all-start.5 = ((bf16[16,128,256]{2,1,0:T(8,128)(2,1)}), bf16[16,128,256]{2,1,0:T(8,128)(2,1)S(1)}, u32[]{:S(2)}, u32[]{:S(2)}) async-start(bf16[16,128,256]{2,1,0:T(8,128)(2,1)} %bitcast.8), calls=%async_computation.5 | async-start | bytes 2097152 | tf_op jit(solution)/shard_map/all_to_all | solution.py:167
  214.0 17.0 %all-to-all-done.5 = bf16[16,128,256]{2,1,0:T(8,128)(2,1)S(1)} async-done(((bf16[16,128,256]{2,1,0:T(8,128)(2,1)}), bf16[16,128,256]{2,1,0:T(8,128)(2,1)S(1)}, u32[]{:S(2)}, u32[]{:S(2)}) %all-to-all-start.5) | async-done | bytes 1048608 | tf_op jit(solution)/shard_map/all_to_all | solution.py:167
  232.0 3.6 %all-to-all-start.10 = ((f32[16,40,256]{2,1,0:T(8,128)}), f32[16,40,256]{2,1,0:T(8,128)S(1)}, u32[]{:S(2)}, u32[]{:S(2)}) async-start(f32[16,40,256]{2,1,0:T(8,128)} %broadcast_in_dim.14), calls=%async_computation.10 | async-start | bytes 1310720 | tf_op jit(solution)/shard_map/all_to_all | solution.py:167
  236.9 9.9 %all-to-all-done.10 = f32[16,40,256]{2,1,0:T(8,128)S(1)} async-done(((f32[16,40,256]{2,1,0:T(8,128)}), f32[16,40,256]{2,1,0:T(8,128)S(1)}, u32[]{:S(2)}, u32[]{:S(2)}) %all-to-all-start.10) | async-done | bytes 655392 | tf_op jit(solution)/shard_map/all_to_all | solution.py:167
  (45 shorter events, 15.1 us)
Async XLA Ops:
  2.0 25.1 %copy-start = (bf16[1,64,9216]{2,1,0:T(8,128)(2,1)S(1)}, bf16[1,64,9216]{2,1,0:T(8,128)(2,1)}, u32[]{:S(2)}) copy-start(bf16[1,64,9216]{2,1,0:T(8,128)(2,1)} %param.11) | copy-start | bytes 3538948
  2.0 18.3 %all-to-all-start.2 = ((bf16[16,16,128]{2,1,0:T(8,128)(2,1)}), bf16[16,16,128]{2,1,0:T(8,128)(2,1)S(1)}, u32[]{:S(2)}, u32[]{:S(2)}) async-start(bf16[16,16,128]{2,1,0:T(8,128)(2,1)} %broadcast_in_dim.10), calls=%async_computation.2 | async-start | bytes 131072 | tf_op jit(solution)/shard_map/all_to_all | solution.py:167
  12.8 0.9 copy-start.7
  13.7 0.7 copy-start.11
  19.3 1.0 copy-start.3
  20.3 23.3 %all-to-all-start.4 = ((bf16[16,128,256]{2,1,0:T(8,128)(2,1)}), bf16[16,128,256]{2,1,0:T(8,128)(2,1)S(1)}, u32[]{:S(2)}, u32[]{:S(2)}) async-start(bf16[16,128,256]{2,1,0:T(8,128)(2,1)} %get-tuple-element.14), calls=%async_computation.4 | async-start | bytes 2097152 | tf_op jit(solution)/shard_map/all_to_all | solution.py:167
  27.1 22.1 %collective-permute-start = (bf16[64,9216]{1,0:T(8,128)(2,1)S(1)}, bf16[64,9216]{1,0:T(8,128)(2,1)S(1)}, u32[]{:S(2)}, u32[]{:S(2)}) collective-permute-start(bf16[64,9216]{1,0:T(8,128)(2,1)S(1)} %bitcast.24), channel_id=1, source_target_pairs={{0,16},{16,0},{32,48},{48,32},{64,80},{80,64},{96,112},{112,96},{1... | collective-permute-start | bytes 3538952 | tf_op jit(solution)/shard_map/ppermute | solution.py:186
  44.8 19.0 %all-to-all-start.3 = ((bf16[16,16,16,128]{3,2,1,0:T(8,128)(2,1)}), bf16[16,16,16,128]{3,2,1,0:T(8,128)(2,1)}, u32[]{:S(2)}, u32[]{:S(2)}) async-start(bf16[16,16,16,128]{3,2,1,0:T(8,128)(2,1)} %broadcast_in_dim.11), calls=%async_computation.3 | async-start | bytes 2097152 | tf_op jit(solution)/shard_map/all_to_all | solution.py:167
  49.7 0.8 copy-start.2
  63.8 35.2 %all-to-all-start = ((bf16[8,288,128]{2,1,0:T(8,128)(2,1)}), bf16[8,288,128]{2,1,0:T(8,128)(2,1)}, u32[]{:S(2)}, u32[]{:S(2)}) async-start(bf16[8,288,128]{2,1,0:T(8,128)(2,1)} %copy-done.2), calls=%async_computation | async-start | bytes 1179648 | tf_op jit(solution)/shard_map/all_to_all | solution.py:167
  98.2 0.8 copy-start.1
  99.0 6.8 %copy-start.5 = (bf16[256,256]{1,0:T(8,128)(2,1)S(1)}, bf16[256,256]{1,0:T(8,128)(2,1)}, u32[]{:S(2)}) copy-start(bf16[256,256]{1,0:T(8,128)(2,1)} %w2s_ref.3) | copy-start | bytes 393220
  99.0 6.8 %copy-start.6 = (bf16[256,256]{1,0:T(8,128)(2,1)S(1)}, bf16[256,256]{1,0:T(8,128)(2,1)}, u32[]{:S(2)}) copy-start(bf16[256,256]{1,0:T(8,128)(2,1)} %w2n_ref.3) | copy-start | bytes 393220
  99.0 6.8 %copy-start.8 = (bf16[1,1,256,256]{3,2,1,0:T(8,128)(2,1)S(1)}, bf16[1,1,256,256]{3,2,1,0:T(8,128)(2,1)}, u32[]{:S(2)}) copy-start(bf16[1,1,256,256]{3,2,1,0:T(8,128)(2,1)} %param.21) | copy-start | bytes 393220
  99.0 6.8 %copy-start.9 = (s32[1,1,16,128]{3,2,1,0:T(8,128)S(1)}, s32[1,1,16,128]{3,2,1,0:T(8,128)}, u32[]{:S(2)}) copy-start(s32[1,1,16,128]{3,2,1,0:T(8,128)} %param.17) | copy-start | bytes 24580
  99.0 6.9 %copy-start.10 = (s32[1,1,256]{2,1,0:T(1,128)S(1)}, s32[1,1,256]{2,1,0:T(1,128)}, u32[]{:S(2)}) copy-start(s32[1,1,256]{2,1,0:T(1,128)} %param.20) | copy-start | bytes 3076
  99.1 20.5 %all-to-all-start.1 = ((bf16[8,288,128]{2,1,0:T(8,128)(2,1)}), bf16[8,288,128]{2,1,0:T(8,128)(2,1)S(1)}, u32[]{:S(2)}, u32[]{:S(2)}) async-start(bf16[8,288,128]{2,1,0:T(8,128)(2,1)} %copy-done.1), calls=%async_computation.1 | async-start | bytes 1179648 | tf_op jit(solution)/shard_map/all_to_all | solution.py:167
  143.0 35.6 %all-to-all-start.6 = ((bf16[16,128,256]{2,1,0:T(8,128)(2,1)}), bf16[16,128,256]{2,1,0:T(8,128)(2,1)S(1)}, u32[]{:S(2)}, u32[]{:S(2)}) async-start(bf16[16,128,256]{2,1,0:T(8,128)(2,1)} %get-tuple-element.21), calls=%async_computation.6 | async-start | bytes 2097152 | tf_op jit(solution)/shard_map/all_to_all | solution.py:167
  179.5 20.8 %all-to-all-start.9 = ((f32[16,32,256]{2,1,0:T(8,128)}), f32[16,32,256]{2,1,0:T(8,128)S(1)}, u32[]{:S(2)}, u32[]{:S(2)}) async-start(f32[16,32,256]{2,1,0:T(8,128)} %broadcast_in_dim.13), calls=%async_computation.9 | async-start | bytes 1048576 | tf_op jit(solution)/shard_map/all_to_all | solution.py:167
  210.3 20.8 %all-to-all-start.5 = ((bf16[16,128,256]{2,1,0:T(8,128)(2,1)}), bf16[16,128,256]{2,1,0:T(8,128)(2,1)S(1)}, u32[]{:S(2)}, u32[]{:S(2)}) async-start(bf16[16,128,256]{2,1,0:T(8,128)(2,1)} %bitcast.8), calls=%async_computation.5 | async-start | bytes 2097152 | tf_op jit(solution)/shard_map/all_to_all | solution.py:167
  214.0 21.6 %copy-start.4 = (bf16[16,128,256]{2,1,0:T(8,128)(2,1)S(1)}, bf16[16,128,256]{2,1,0:T(8,128)(2,1)}, u32[]{:S(2)}) copy-start(bf16[16,128,256]{2,1,0:T(8,128)(2,1)} %copy-done.3) | copy-start | bytes 3145732
  232.0 14.8 %all-to-all-start.10 = ((f32[16,40,256]{2,1,0:T(8,128)}), f32[16,40,256]{2,1,0:T(8,128)S(1)}, u32[]{:S(2)}, u32[]{:S(2)}) async-start(f32[16,40,256]{2,1,0:T(8,128)} %broadcast_in_dim.14), calls=%async_computation.10 | async-start | bytes 1310720 | tf_op jit(solution)/shard_map/all_to_all | solution.py:167

commit v2 on v1

v2 whole, which is shorter than its diff:
```python
import jax
import jax.numpy as jnp
from jax import lax
from jax.experimental import pallas as pl
from jax.experimental.pallas import tpu as pltpu
from jax.sharding import PartitionSpec as P

BF = jnp.bfloat16
F32 = jnp.float32
I32 = jnp.int32
NF = 16
ND = 16
NZ = 8
COLS = 64
PAIR = 128
NIN = 9216
R1 = 4608
OWN = 288
HALF = R1 // 2
K1 = 10
K2 = 15
SEEDS = 256
SLOTS = 128
HID = 256
UNROLL = 16
G2 = 256
G1 = 320
VMEM = pl.BlockSpec(memory_space=pltpu.VMEM)
SMEM = pl.BlockSpec(memory_space=pltpu.SMEM)


def call(body, name, outs, ins, scratch=(), limit=16, us=1):
    return pl.pallas_call(
        body,
        name=name,
        out_shape=outs,
        in_specs=ins,
        out_specs=jax.tree.map(lambda _: VMEM, outs),
        scratch_shapes=list(scratch),
        compiler_params=pltpu.CompilerParams(vmem_limit_bytes=limit << 20),
        cost_estimate=pl.CostEstimate(flops=us * 10**9, transcendentals=0, bytes_accessed=us * 10**6),
    )


def shape(dims, dtype):
    return jax.ShapeDtypeStruct(dims, dtype)


def dot(a, b, ca=1, cb=0):
    return lax.dot_general(a, b, (((ca,), (cb,)), ((), ())), preferred_element_type=F32)


def pick_body(count_ref, neigh_ref, dout_ref, picks_ref, t_ref):
    start = jnp.int32(0)
    lanes = neigh_ref[...]
    d_out = dout_ref[...]
    row = lax.broadcasted_iota(I32, (SLOTS, SEEDS), 0)
    for s in range(ND):
        count = count_ref[s]
        position = jnp.where(row < count, row + start, -1)
        total = jnp.zeros((SLOTS, SEEDS), F32)
        for k in range(K2):
            total = total + jnp.where(position == lanes[k : k + 1, :], 1.0, 0.0)
        picks = total.astype(BF)
        picks_ref[s] = picks
        t_ref[s] = dot(picks, d_out).astype(BF)
        start = start + count


def rows_body(core_ref, own_ref, other_ref, index_ref, out_ref, table, sums):
    core = core_ref[0]
    step = 512
    for c in range(0, NIN, step):
        both = jnp.concatenate([own_ref[:, c : c + step], other_ref[:, c : c + step]], axis=0)
        table[c : c + step, :] = both.astype(F32).T
    for z in range(NZ):
        first = pl.multiple_of((2 * z + core) * OWN, 32)
        out_ref[z, :, 0:PAIR] = table[pl.ds(first, OWN), :].astype(BF)

    def block(b, carry):
        z = b // (OWN // UNROLL)
        base = b * UNROLL + (z + core) * OWN
        for j in range(UNROLL):
            rows = [table[pl.ds(index_ref[k * R1 + base + j], 1), :] for k in range(K1)]
            while len(rows) > 1:
                even = len(rows) // 2 * 2
                rows = [rows[i] + rows[i + 1] for i in range(0, even, 2)] + rows[even:]
            sums[pl.ds(b * UNROLL + j, 1), :] = rows[0]
        return carry

    lax.fori_loop(0, HALF // UNROLL, block, 0)
    for z in range(NZ):
        mean = sums[z * OWN : (z + 1) * OWN, :] * (1.0 / K1)
        out_ref[z, :, PAIR : 2 * PAIR] = mean.astype(BF)


def split(x):
    high = x.astype(BF)
    return high, (x - high.astype(F32)).astype(BF)


def owner_body(t_ref, send_ref, seed_ref, dout_ref, w2s_ref, w2n_ref, x_ref, d_ref, dh_ref):
    d_out = dout_ref[...]
    row = lax.broadcasted_iota(I32, (OWN, SEEDS), 0)
    x = jnp.zeros((OWN, HID), F32)
    for q in range(0, ND, 2):
        lanes = jnp.concatenate([send_ref[q : q + 1, :], send_ref[q + 1 : q + 2, :]], axis=1)
        hot = jnp.where(row == lanes, 1.0, 0.0).astype(BF)
        x = x + dot(hot, t_ref[q * SLOTS : (q + 2) * SLOTS, :])
    x = x * (1.0 / K2)
    hot = jnp.where(row == seed_ref[...], 1.0, 0.0).astype(BF)
    d = dot(hot, d_out).astype(BF)
    high, low = split(x)
    w2n = w2n_ref[...]
    x_ref[...] = x
    d_ref[...] = d
    dh_ref[...] = dot(high, w2n, 1, 1) + dot(low, w2n, 1, 1) + dot(d, w2s_ref[...], 1, 1)


def reverse(j):
    return (j % 2) * 4 + (j // 2 % 2) * 2 + j // 4


def main_body(
    core_ref, rows_ref, wa_ref, wb_ref, x_ref, d_ref, dh_ref, send_ref, seed_ref, w2s_ref,
    out_ref, part_ref,
):
    core = core_ref[0]
    here = core_ref[1]
    chips = [jnp.bitwise_xor(here, reverse(j)) for j in range(NZ)]
    pre = jnp.zeros((OWN, HID), F32)
    for j in range(NZ):
        a, b = wa_ref[j], wb_ref[j]
        w = jnp.concatenate([a[:COLS], b[:COLS], a[COLS:], b[COLS:]], axis=0)
        pre = pre + dot(rows_ref[chips[j]], w)
    slope = jnp.exp(jnp.minimum(pre, 0.0))
    hidden = jnp.where(pre > 0, pre, slope - 1.0).astype(BF)
    d_pre = (dh_ref[...] * slope).astype(BF)
    for j in range(NZ):
        g = dot(rows_ref[chips[j]], d_pre, 0, 0).astype(BF)
        for q in range(ND):
            r, h = q // 2, q % 2
            at = (r // 4) * PAIR + (r % 4) * 16
            lanes = slice(h * 128, (h + 1) * 128)
            for side in range(2):
                f = 2 * chips[j] + (core if side == 0 else 1 - core)
                piece = g[at + side * COLS : at + side * COLS + 16, lanes]
                out_ref[q, pl.ds(pl.multiple_of(G1 + f * 16, 16), 16), :] = piece
    high, low = split(x_ref[...])
    g2s = dot(hidden, d_ref[...], 0, 0).astype(BF)
    g2n = (dot(hidden, high, 0, 0) + dot(hidden, low, 0, 0)).astype(BF)
    for q in range(ND):
        g = g2s if q < 8 else g2n
        for h in range(2):
            piece = g[(q % 8) * 32 : (q % 8) * 32 + 32, h * 128 : (h + 1) * 128]
            out_ref[q, G2 + h * 32 : G2 + h * 32 + 32, :] = piece
    row = lax.broadcasted_iota(I32, (OWN, SEEDS), 0)
    for q in range(0, ND, 2):
        lanes = jnp.concatenate([send_ref[q : q + 1, :], send_ref[q + 1 : q + 2, :]], axis=1)
        hot = jnp.where(row == lanes, 1.0, 0.0).astype(BF)
        listed = dot(hot, hidden, 0, 0).astype(BF)
        for i in range(2):
            for h in range(2):
                piece = listed[i * SLOTS : (i + 1) * SLOTS, h * 128 : (h + 1) * 128]
                out_ref[q + i, h * SLOTS : (h + 1) * SLOTS, :] = piece
    hot = jnp.where(row == seed_ref[...], 1.0, 0.0).astype(BF)
    part_ref[...] = dot(dot(hot, hidden, 0, 0).astype(BF), w2s_ref[...])


def first_sum_body(in_ref, out_ref):
    total = in_ref[0, G2:, :].astype(F32)
    for p in range(1, ND):
        total = total + in_ref[p, G2:, :].astype(F32)
    total = total.astype(BF)
    for f in range(NF):
        out_ref[f, 0:16, :] = total[G1 - G2 + f * 16 : G1 - G2 + f * 16 + 16]
        out_ref[f, 16:80, :] = total[0:64]


def second_sum_body(in_ref, out_ref):
    total = in_ref[0].astype(F32)
    for f in range(1, NF):
        total = total + in_ref[f].astype(F32)
    for q in range(ND):
        out_ref[q] = total


def place_body(in_ref, g1s_ref, g1n_ref, g2s_ref, g2n_ref):
    for q in range(ND):
        r, h = q // 2, q % 2
        g1 = g1s_ref if r < 4 else g1n_ref
        g1[(r % 4) * 16 : (r % 4) * 16 + 16, h * 128 : (h + 1) * 128] = in_ref[q, 0:16, :]
        g2 = g2s_ref if q < 8 else g2n_ref
        for half in range(2):
            piece = in_ref[q, 16 + half * 32 : 48 + half * 32, :]
            g2[(q % 8) * 32 : (q % 8) * 32 + 32, half * 128 : (half + 1) * 128] = piece


def layer_body(in_ref, picks_ref, part_ref, w2n_ref, layer_ref):
    total = part_ref[...]
    picks = picks_ref[...]
    for h in range(2):
        rows = in_ref[:, h * SLOTS : (h + 1) * SLOTS, :].reshape(ND * SLOTS, 128)
        mean = (dot(picks, rows, 0, 0) * (1.0 / K2)).astype(BF)
        total = total + dot(mean, w2n_ref[h * 128 : (h + 1) * 128, :])
    layer_ref[...] = total.astype(BF)


def swap(x, axis, groups=None):
    return lax.all_to_all(
        x, axis, split_axis=0, concat_axis=0, tiled=True, axis_index_groups=groups
    )


def fetch(x, bit):
    return lax.ppermute(x, "feat", [(i, i ^ bit) for i in range(NF)])


def per_device(
    features, w1_self, w1_neigh, w2_self, w2_neigh, neigh_one, send_rows, recv_count,
    neigh_two, seed_rows, d_out,
):
    f = lax.axis_index("feat")
    place = jnp.stack([jnp.bitwise_and(f, 1), jnp.right_shift(f, 1)])
    chips = [[2 * z + c for z in range(NZ)] for c in range(2)]
    own = features[0]
    other = fetch(own, 1)

    w1 = jnp.concatenate([w1_self, w1_neigh], axis=0)[None]
    w1 = jnp.concatenate([w1, fetch(w1, 8)], axis=0)
    w1 = jnp.concatenate([w1, fetch(w1, 4)], axis=0)
    place_early, w1 = lax.optimization_barrier((place, w1))
    w1 = jnp.concatenate([w1, fetch(w1, 2)], axis=0)
    w1_other = fetch(w1, 1)

    send = send_rows[0, 0]
    seeds = seed_rows[0]
    grad_out = d_out[0, 0]
    picks, t_out = call(
        pick_body,
        "picks",
        (shape((ND, SLOTS, SEEDS), BF), shape((ND, SLOTS, HID), BF)),
        [SMEM, VMEM, VMEM],
        us=5,
    )(recv_count[:, 0, 0], neigh_two[0, 0].T, grad_out)
    t_in = swap(t_out, "dom")

    rows_out = call(
        rows_body,
        "node_rows",
        shape((NZ, OWN, 2 * PAIR), BF),
        [SMEM, VMEM, VMEM, SMEM],
        [pltpu.VMEM((NIN, PAIR), F32), pltpu.VMEM((HALF, PAIR), F32)],
        limit=24,
        us=22,
    )(place_early, own, other, neigh_one.reshape(-1))
    rows_in = swap(rows_out, "feat", chips)

    x, d, d_hidden = call(
        owner_body,
        "owner_grads",
        (shape((OWN, HID), F32), shape((OWN, HID), BF), shape((OWN, HID), F32)),
        [VMEM] * 6,
    )(t_in.reshape(ND * SLOTS, HID), send, seeds, grad_out, w2_self, w2_neigh)

    to_dom, part = call(
        main_body,
        "project",
        (shape((ND, G1 + 256, 128), BF), shape((SEEDS, HID), F32)),
        [SMEM] + [VMEM] * 9,
        us=6,
    )(place, rows_in, w1, w1_other, x, d, d_hidden, send, seeds, w2_self)
    from_dom = swap(to_dom, "dom")

    to_feat = call(first_sum_body, "sum_dom", shape((NF, 80, 128), BF), [VMEM])(from_dom)
    from_feat = swap(to_feat, "feat")
    layer_out = call(layer_body, "layer_two", shape((SEEDS, HID), BF), [VMEM] * 4)(
        from_dom, picks.reshape(ND * SLOTS, SEEDS), part, w2_neigh
    )
    done = call(second_sum_body, "sum_feat", shape((ND, 80, 128), F32), [VMEM])(from_feat)
    done = swap(done, "dom")
    first = shape((COLS, HID), F32)
    second = shape((HID, HID), F32)
    grads = call(place_body, "place", (first, first, second, second), [VMEM])(done)
    return (layer_out[None, None], *grads)


def solution(mesh):
    return jax.shard_map(
        per_device,
        mesh=mesh,
        in_specs=(
            P("dom", "feat", None),
            P("feat", None),
            P("feat", None),
            P(),
            P(),
            P("dom", None, None),
            P("dom", "feat", None, None),
            P(None, "feat", "dom"),
            P("dom", "feat", None, None),
            P("dom", "feat", None),
            P("dom", "feat", None, None),
        ),
        out_specs=(P("dom", "feat", None, None), P("feat", None), P("feat", None), P(), P()),
        check_vma=False,
    )
```

time: 250 us -> 190 us (0.76)
  waiting for transfers between devices: 114 us -> 41.5 us
  blocking collectives: 27.4 us -> 57 us
  starting transfers between devices: 52.4 us -> 32.9 us
  Pallas kernels: 35.5 us -> 39 us
    all_to_all x9 -> x3, waiting for transfers between devices: 114 us -> 10.6 us  [swap(): lax.all_to_all(x, axis, split_axis=0, concat_axis=0, tiled=True, axis_ind...]
    all_to_all x9 -> x3, starting transfers between devices: 52 us -> 17.6 us  [swap(): lax.all_to_all(x, axis, split_axis=0, concat_axis=0, tiled=True, axis_ind...]
    ppermute x1 -> x5, waiting for transfers between devices: 0.01 us -> 30.9 us  [fetch(): return lax.ppermute(x, 'feat', [(i, i ^ bit) for i in range(NF)])]
    all_to_all x2, blocking collectives: 27.4 us -> 57 us  [swap(): lax.all_to_all(x, axis, split_axis=0, concat_axis=0, tiled=True, axis_ind...]
    ppermute x1 -> x5, starting transfers between devices: 0.45 us -> 15.3 us  [fetch(): return lax.ppermute(x, 'feat', [(i, i ^ bit) for i in range(NF)])]
    unnamed x25 -> x50, local copies, waits for them, and re-layouts: 4.89 us -> 14.7 us
    broadcast_in_dim x4 -> x0, local copies, waits for them, and re-layouts: 3.62 us -> none  [to_all(): return swap(jnp.broadcast_to(x[None], (n,) + x.shape), axis)]
    pallas_call x3 -> x5, Pallas kernels: 28.5 us -> 31.6 us  [the longest x1 26.3 us: per_device(): call(rows_body, 'node_rows', shape((NZ, OWN, 2 * PAIR), BF), [SMEM, VMEM,...]
  transfers between devices with their start and end apart: 10 -> 8, of which waited for: 7 -> 3; matrix products, arithmetic and copies ran while one was open for 4% -> 3% of each run, Pallas kernels for 12% -> 18%
where the time goes in v2:
time: 190 us; the launch traced here: 189 us
  blocking collectives  57 us (30%)
  waiting for transfers between devices  41.5 us (22%)
  Pallas kernels  39 us (21%)
  starting transfers between devices  32.9 us (17%)
  local copies, waits for them, and re-layouts  14.7 us (8%)
  other arithmetic  3.17 us (2%)
    all_to_all x2, blocking collectives, swap(): lax.all_to_all(x, axis, split_axis=0, concat_axis=0, tiled=True, axis_ind...  57 us
    ppermute x5, waiting for transfers between devices, fetch(): return lax.ppermute(x, 'feat', [(i, i ^ bit) for i in range(NF)])  30.9 us
    pallas_call x1, Pallas kernels, per_device(): call(rows_body, 'node_rows', shape((NZ, OWN, 2 * PAIR), BF), [SMEM, VMEM,...  26.3 us
    all_to_all x3, starting transfers between devices, swap(): lax.all_to_all(x, axis, split_axis=0, concat_axis=0, tiled=True, axis_ind...  17.6 us
    ppermute x5, starting transfers between devices, fetch(): return lax.ppermute(x, 'feat', [(i, i ^ bit) for i in range(NF)])  15.3 us
    unnamed x50, local copies, waits for them, and re-layouts  14.7 us
    all_to_all x3, waiting for transfers between devices, swap(): lax.all_to_all(x, axis, split_axis=0, concat_axis=0, tiled=True, axis_ind...  10.6 us
    pallas_call x1, Pallas kernels, per_device(): call(pick_body, 'picks', (shape((ND, SLOTS, SEEDS), BF), shape((ND, SLOTS...  4.85 us
  transfers between devices with their start and end apart: 8, of which 3 were waited for; matrix products, arithmetic and copies ran while one was open for 3% of the time, Pallas kernels for 18%

profile of v2, /device:TPU:1, one launch (start us, length us, event | category | flops | bytes accessed | tf_op | source)
XLA Modules:
  0.0 189.1 jit_solution(9227992987142988985)
XLA Ops:
  0.6 3.3 %collective-permute-start.2 = (bf16[64,9216]{1,0:T(8,128)(2,1)}, bf16[64,9216]{1,0:T(8,128)(2,1)}, u32[]{:S(2)}, u32[]{:S(2)}) collective-permute-start(bf16[64,9216]{1,0:T(8,128)(2,1)} %bitcast.21), channel_id=1, source_target_pairs={{0,16},{16,0},{32,48},{48,32},{64,80},{80,64},{96,112},{112,96},{1... | collective-permute-start | bytes 3538952 | tf_op jit(solution)/shard_map/ppermute | solution.py:216
  4.7 5.2 %collective-permute-start = (bf16[1,128,256]{2,1,0:T(8,128)(2,1)S(1)}, bf16[1,128,256]{2,1,0:T(8,128)(2,1)S(1)}, u32[]{:S(2)}, u32[]{:S(2)}) collective-permute-start(bf16[1,128,256]{2,1,0:T(8,128)(2,1)S(1)} %maximum_bitcast_fusion), channel_id=1, source_target_pairs={{0,128},{16,144},{32,160},{48,176},{64,192},{80,208},{96,224},{112... | collective-permute-start | bytes 196616 | tf_op jit(solution)/shard_map/ppermute | solution.py:216
  10.6 1.7 collective-permute-done
  13.0 2.7 %collective-permute-start.1 = (bf16[2,128,256]{2,1,0:T(8,128)(2,1)}, bf16[2,128,256]{2,1,0:T(8,128)(2,1)}, u32[]{:S(2)}, u32[]{:S(2)}) collective-permute-start(bf16[2,128,256]{2,1,0:T(8,128)(2,1)} %pad_maximum_fusion.1), channel_id=1, source_target_pairs={{0,64},{16,80},{32,96},{48,112},{64,0},{80,16},{96,32},{112,48},{1... | collective-permute-start | bytes 393224 | tf_op jit(solution)/shard_map/ppermute | solution.py:216
  17.3 4.9 %picks.1 = (bf16[16,128,256]{2,1,0:T(8,128)(2,1)S(1)}, bf16[16,128,256]{2,1,0:T(8,128)(2,1)}) custom-call(s32[16]{0:T(128)S(1)} %bitcast.30, s32[15,256]{1,0:T(8,128)S(1)} %bitcast.20, bf16[256,256]{1,0:T(8,128)(2,1)S(1)} %bitcast.24), custom_call_target="tpu_custom_call" | custom-call | flops 5000000000 | bytes 5000000 | tf_op jit(solution)/shard_map/picks/pallas_call | solution.py:239
  22.1 6.9 %all-to-all-start.1 = ((bf16[16,128,256]{2,1,0:T(8,128)(2,1)}), bf16[16,128,256]{2,1,0:T(8,128)(2,1)S(1)}, u32[]{:S(2)}, u32[]{:S(2)}) async-start(bf16[16,128,256]{2,1,0:T(8,128)(2,1)} %get-tuple-element.20), calls=%async_computation.1 | async-start | bytes 2097152 | tf_op jit(solution)/shard_map/all_to_all | solution.py:210
  29.1 1.6 pad_maximum_fusion
  30.7 26.3 %node_rows.1 = bf16[8,288,256]{2,1,0:T(8,128)(2,1)} custom-call(s32[2]{0:T(128)S(1)} %pad_add_fusion.core_ref, bf16[64,9216]{1,0:T(8,128)(2,1)S(1)} %bitcast.22, bf16[64,9216]{1,0:T(8,128)(2,1)} %collective-permute-done.2.other_ref, s32[46080]{0:T(1024)S(1)} %bitcast.23), custom_call_target="tpu_custom_call" | custom-call | flops 22000001024 | bytes 22000000 | tf_op jit(solution)/shard_map/node_rows/pallas_call | solution.py:248
  57.0 6.5 %all-to-all-start = ((bf16[8,288,256]{2,1,0:T(8,128)(2,1)}), bf16[8,288,256]{2,1,0:T(8,128)(2,1)S(1)}, u32[]{:S(2)}, u32[]{:S(2)}) async-start(bf16[8,288,256]{2,1,0:T(8,128)(2,1)} %node_rows.1), calls=%async_computation | async-start | bytes 2359296 | tf_op jit(solution)/shard_map/all_to_all | solution.py:210
  63.5 1.5 collective-permute-start.3
  64.9 1.0 constant_dynamic-update-slice_fusion.1
  66.0 29.2 %collective-permute-done.3 = bf16[4,128,256]{2,1,0:T(8,128)(2,1)S(1)} collective-permute-done((bf16[4,128,256]{2,1,0:T(8,128)(2,1)}, bf16[4,128,256]{2,1,0:T(8,128)(2,1)S(1)}, u32[]{:S(2)}, u32[]{:S(2)}) %collective-permute-start.3) | collective-permute-done | bytes 262176 | tf_op jit(solution)/shard_map/ppermute | solution.py:216
  95.2 2.6 %collective-permute-start.4 = (bf16[8,128,256]{2,1,0:T(8,128)(2,1)S(1)}, bf16[8,128,256]{2,1,0:T(8,128)(2,1)S(1)}, u32[]{:S(2)}, u32[]{:S(2)}) collective-permute-start(bf16[8,128,256]{2,1,0:T(8,128)(2,1)S(1)} %constant_dynamic-update-slice_fusion.wa_ref), channel_id=1, source_target_pairs={{0,16},{16,0},{32,48},{48,32},{64,80},{80,64},{96,112},{112,96},{1... | collective-permute-start | bytes 1572872 | tf_op jit(solution)/shard_map/ppermute | solution.py:216
  102.6 1.0 copy-done.5
  103.6 1.0 copy-done.8
  105.5 1.0 copy-done.18
  106.5 1.0 copy-done.20
  108.4 3.2 %project.1 = (bf16[16,576,128]{2,1,0:T(8,128)(2,1)S(1)}, f32[256,256]{1,0:T(8,128)S(1)}) custom-call(s32[2]{0:T(128)S(1)} %pad_add_fusion.core_ref, bf16[8,288,256]{2,1,0:T(8,128)(2,1)S(1)} %all-to-all-done.rows_ref, bf16[8,128,256]{2,1,0:T(8,128)(2,1)S(1)} %copy-done.5, bf16[8,128,256]{2,1,0:T(8,128)(2,1)S(1)} %copy-done.8, f32[288,256]{1,0:T(8,128)S(1)} %copy-done.18, ...), custom_call_target="tpu_custom_call" | custom-call | flops 6000000000 | bytes 6000000 | tf_op jit(solution)/shard_map/project/pallas_call | solution.py:266
  111.5 36.8 %all_to_all.25.in_ref = bf16[16,576,128]{2,1,0:T(8,128)(2,1)S(1)} all-to-all(bf16[16,576,128]{2,1,0:T(8,128)(2,1)S(1)} %get-tuple-element.24), channel_id=1, replica_groups=mesh['feat'=16,'dom'=16] {'dom'}, dimensions={0} | all-to-all | bytes 4718592 | tf_op jit(solution)/shard_map/all_to_all | solution.py:210
  148.5 20.2 %all_to_all.26.in_ref = bf16[16,80,128]{2,1,0:T(8,128)(2,1)S(1)} all-to-all(bf16[16,80,128]{2,1,0:T(8,128)(2,1)S(1)} %sum_dom.1), channel_id=1, replica_groups=mesh['feat'=16,'dom'=16] {'feat'}, dimensions={0} | all-to-all | bytes 655360 | tf_op jit(solution)/shard_map/all_to_all | solution.py:210
  169.7 4.3 %all-to-all-start.4 = ((f32[16,80,128]{2,1,0:T(8,128)}), f32[16,80,128]{2,1,0:T(8,128)}, u32[]{:S(2)}, u32[]{:S(2)}) async-start(f32[16,80,128]{2,1,0:T(8,128)} %copy-done), calls=%async_computation.4 | async-start | bytes 1310720 | tf_op jit(solution)/shard_map/all_to_all | solution.py:210
  174.9 1.7 layer_two.1
  176.6 10.6 %all-to-all-done.4.in_ref = f32[16,80,128]{2,1,0:T(8,128)} async-done(((f32[16,80,128]{2,1,0:T(8,128)}), f32[16,80,128]{2,1,0:T(8,128)}, u32[]{:S(2)}, u32[]{:S(2)}) %all-to-all-start.4) | async-done | bytes 655392 | tf_op jit(solution)/shard_map/all_to_all | solution.py:210
  187.2 1.9 %place.1 = (f32[64,256]{1,0:T(8,128)}, f32[64,256]{1,0:T(8,128)}, f32[256,256]{1,0:T(8,128)}, f32[256,256]{1,0:T(8,128)}) custom-call(f32[16,80,128]{2,1,0:T(8,128)} %all-to-all-done.4.in_ref), custom_call_target="tpu_custom_call" | custom-call | flops 1000000000 | bytes 1000000 | tf_op jit(solution)/shard_map/place/pallas_call | solution.py:284
  (57 shorter events, 12.4 us)
Async XLA Ops:
  0.6 30.1 %collective-permute-start.2 = (bf16[64,9216]{1,0:T(8,128)(2,1)}, bf16[64,9216]{1,0:T(8,128)(2,1)}, u32[]{:S(2)}, u32[]{:S(2)}) collective-permute-start(bf16[64,9216]{1,0:T(8,128)(2,1)} %bitcast.21), channel_id=1, source_target_pairs={{0,16},{16,0},{32,48},{48,32},{64,80},{80,64},{96,112},{112,96},{1... | collective-permute-start | bytes 3538952 | tf_op jit(solution)/shard_map/ppermute | solution.py:216
  4.7 7.6 %collective-permute-start = (bf16[1,128,256]{2,1,0:T(8,128)(2,1)S(1)}, bf16[1,128,256]{2,1,0:T(8,128)(2,1)S(1)}, u32[]{:S(2)}, u32[]{:S(2)}) collective-permute-start(bf16[1,128,256]{2,1,0:T(8,128)(2,1)S(1)} %maximum_bitcast_fusion), channel_id=1, source_target_pairs={{0,128},{16,144},{32,160},{48,176},{64,192},{80,208},{96,224},{112... | collective-permute-start | bytes 196616 | tf_op jit(solution)/shard_map/ppermute | solution.py:216
  12.4 3.3 %copy-start.23 = (bf16[1,128,256]{2,1,0:T(8,128)(2,1)}, bf16[1,128,256]{2,1,0:T(8,128)(2,1)S(1)}, u32[]{:S(2)}) copy-start(bf16[1,128,256]{2,1,0:T(8,128)(2,1)S(1)} %collective-permute-done) | copy-start | bytes 196612
  13.0 16.1 %collective-permute-start.1 = (bf16[2,128,256]{2,1,0:T(8,128)(2,1)}, bf16[2,128,256]{2,1,0:T(8,128)(2,1)}, u32[]{:S(2)}, u32[]{:S(2)}) collective-permute-start(bf16[2,128,256]{2,1,0:T(8,128)(2,1)} %pad_maximum_fusion.1), channel_id=1, source_target_pairs={{0,64},{16,80},{32,96},{48,112},{64,0},{80,16},{96,32},{112,48},{1... | collective-permute-start | bytes 393224 | tf_op jit(solution)/shard_map/ppermute | solution.py:216
  22.1 8.6 %copy-start.6 = (bf16[1,64,9216]{2,1,0:T(8,128)(2,1)S(1)}, bf16[1,64,9216]{2,1,0:T(8,128)(2,1)}, u32[]{:S(2)}) copy-start(bf16[1,64,9216]{2,1,0:T(8,128)(2,1)} %param.11) | copy-start | bytes 3538948
  22.1 8.6 %copy-start.9 = (s32[1,10,4608]{2,0,1:T(1,128)S(1)}, s32[1,10,4608]{2,0,1:T(1,128)}, u32[]{:S(2)}) copy-start(s32[1,10,4608]{2,0,1:T(1,128)} %param.16) | copy-start | bytes 552964
  22.1 34.9 %all-to-all-start.1 = ((bf16[16,128,256]{2,1,0:T(8,128)(2,1)}), bf16[16,128,256]{2,1,0:T(8,128)(2,1)S(1)}, u32[]{:S(2)}, u32[]{:S(2)}) async-start(bf16[16,128,256]{2,1,0:T(8,128)(2,1)} %get-tuple-element.20), calls=%async_computation.1 | async-start | bytes 2097152 | tf_op jit(solution)/shard_map/all_to_all | solution.py:210
  57.0 40.8 %copy-start.3 = (bf16[256,256]{1,0:T(8,128)(2,1)S(1)}, bf16[256,256]{1,0:T(8,128)(2,1)}, u32[]{:S(2)}) copy-start(bf16[256,256]{1,0:T(8,128)(2,1)} %w2n_ref.3) | copy-start | bytes 393220
  57.0 40.8 %copy-start.11 = (bf16[1,1,256,256]{3,2,1,0:T(8,128)(2,1)S(1)}, bf16[1,1,256,256]{3,2,1,0:T(8,128)(2,1)}, u32[]{:S(2)}) copy-start(bf16[1,1,256,256]{3,2,1,0:T(8,128)(2,1)} %param.21) | copy-start | bytes 393220
  57.0 40.8 %copy-start.14 = (s32[1,1,16,128]{3,2,1,0:T(8,128)S(1)}, s32[1,1,16,128]{3,2,1,0:T(8,128)}, u32[]{:S(2)}) copy-start(s32[1,1,16,128]{3,2,1,0:T(8,128)} %param.17) | copy-start | bytes 24580
  57.0 40.8 %copy-start.15 = (s32[1,1,256]{2,1,0:T(1,128)S(1)}, s32[1,1,256]{2,1,0:T(1,128)}, u32[]{:S(2)}) copy-start(s32[1,1,256]{2,1,0:T(1,128)} %param.20) | copy-start | bytes 3076
  57.0 45.5 %all-to-all-start = ((bf16[8,288,256]{2,1,0:T(8,128)(2,1)}), bf16[8,288,256]{2,1,0:T(8,128)(2,1)S(1)}, u32[]{:S(2)}, u32[]{:S(2)}) async-start(bf16[8,288,256]{2,1,0:T(8,128)(2,1)} %node_rows.1), calls=%async_computation | async-start | bytes 2359296 | tf_op jit(solution)/shard_map/all_to_all | solution.py:210
  63.5 31.6 %collective-permute-start.3 = (bf16[4,128,256]{2,1,0:T(8,128)(2,1)}, bf16[4,128,256]{2,1,0:T(8,128)(2,1)S(1)}, u32[]{:S(2)}, u32[]{:S(2)}) collective-permute-start(bf16[4,128,256]{2,1,0:T(8,128)(2,1)} %pad_maximum_fusion), channel_id=1, source_target_pairs={{0,32},{16,48},{32,0},{48,16},{64,96},{80,112},{96,64},{112,80},{1... | collective-permute-start | bytes 786440 | tf_op jit(solution)/shard_map/ppermute | solution.py:216
  95.2 4.5 %copy-start.4 = (bf16[8,128,256]{2,1,0:T(8,128)(2,1)}, bf16[8,128,256]{2,1,0:T(8,128)(2,1)S(1)}, u32[]{:S(2)}) copy-start(bf16[8,128,256]{2,1,0:T(8,128)(2,1)S(1)} %constant_dynamic-update-slice_fusion.wa_ref) | copy-start | bytes 1572868
  95.2 6.6 %collective-permute-start.4 = (bf16[8,128,256]{2,1,0:T(8,128)(2,1)S(1)}, bf16[8,128,256]{2,1,0:T(8,128)(2,1)S(1)}, u32[]{:S(2)}, u32[]{:S(2)}) collective-permute-start(bf16[8,128,256]{2,1,0:T(8,128)(2,1)S(1)} %constant_dynamic-update-slice_fusion.wa_ref), channel_id=1, source_target_pairs={{0,16},{16,0},{32,48},{48,32},{64,80},{80,64},{96,112},{112,96},{1... | collective-permute-start | bytes 1572872 | tf_op jit(solution)/shard_map/ppermute | solution.py:216
  97.8 0.9 copy-start.12
  102.5 1.0 copy-start.5
  103.6 1.0 copy-start.8
  105.5 1.0 copy-start.18
  106.5 1.0 copy-start.20
  107.5 0.9 copy-start.22
  111.5 36.8 %copy-start.1 = (f32[256,256]{1,0:T(8,128)}, f32[256,256]{1,0:T(8,128)S(1)}, u32[]{:S(2)}) copy-start(f32[256,256]{1,0:T(8,128)S(1)} %get-tuple-element.26.part_ref) | copy-start | bytes 786436
  169.7 17.5 %all-to-all-start.4 = ((f32[16,80,128]{2,1,0:T(8,128)}), f32[16,80,128]{2,1,0:T(8,128)}, u32[]{:S(2)}, u32[]{:S(2)}) async-start(f32[16,80,128]{2,1,0:T(8,128)} %copy-done), calls=%async_computation.4 | async-start | bytes 1310720 | tf_op jit(solution)/shard_map/all_to_all | solution.py:210
  173.9 1.0 copy-start.2
  (8 other events, 6.2 us)

commit v3 on v2

--- a/solution.py
+++ b/solution.py
@@ -63,7 +63,9 @@
             total = total + jnp.where(position == lanes[k : k + 1, :], 1.0, 0.0)
         picks = total.astype(BF)
         picks_ref[s] = picks
-        t_ref[s] = dot(picks, d_out).astype(BF)
+        t = dot(picks, d_out).astype(BF)
+        t_ref[s, 0:SLOTS, :] = t[:, 0:128]
+        t_ref[s, SLOTS : 2 * SLOTS, :] = t[:, 128:256]
         start = start + count
 
 
@@ -99,55 +101,63 @@
     return high, (x - high.astype(F32)).astype(BF)
 
 
-def owner_body(t_ref, send_ref, seed_ref, dout_ref, w2s_ref, w2n_ref, x_ref, d_ref, dh_ref):
+def owner_grads(core, in_ref, send_ref, seed_ref, dout_ref, w2s_ref, w2n_ref, w_ref):
     d_out = dout_ref[...]
     row = lax.broadcasted_iota(I32, (OWN, SEEDS), 0)
     x = jnp.zeros((OWN, HID), F32)
     for q in range(0, ND, 2):
         lanes = jnp.concatenate([send_ref[q : q + 1, :], send_ref[q + 1 : q + 2, :]], axis=1)
         hot = jnp.where(row == lanes, 1.0, 0.0).astype(BF)
-        x = x + dot(hot, t_ref[q * SLOTS : (q + 2) * SLOTS, :])
+        t = jnp.concatenate(
+            [
+                jnp.concatenate([in_ref[i, 0:SLOTS, :], in_ref[i, SLOTS : 2 * SLOTS, :]], axis=1)
+                for i in (q, q + 1)
+            ],
+            axis=0,
+        )
+        x = x + dot(hot, t)
     x = x * (1.0 / K2)
     hot = jnp.where(row == seed_ref[...], 1.0, 0.0).astype(BF)
     d = dot(hot, d_out).astype(BF)
     high, low = split(x)
     w2n = w2n_ref[...]
-    x_ref[...] = x
-    d_ref[...] = d
-    dh_ref[...] = dot(high, w2n, 1, 1) + dot(low, w2n, 1, 1) + dot(d, w2s_ref[...], 1, 1)
-
-
-def reverse(j):
-    return (j % 2) * 4 + (j // 2 % 2) * 2 + j // 4
+    d_hidden = dot(high, w2n, 1, 1) + dot(low, w2n, 1, 1) + dot(d, w2s_ref[...], 1, 1)
+    for z in range(NZ):
+        for side in range(2):
+            f = 2 * z + (core if side == 0 else 1 - core)
+            start = pl.multiple_of(2 * SLOTS + f * 16, 16)
+            for q in range(ND):
+                r, h = q // 2, q % 2
+                at = (r // 4) * PAIR + side * COLS + (r % 4) * 16
+                w_ref[z, at : at + 16, h * 128 : (h + 1) * 128] = in_ref[q, pl.ds(start, 16), :]
+    return high, low, d, d_hidden
 
 
 def main_body(
-    core_ref, rows_ref, wa_ref, wb_ref, x_ref, d_ref, dh_ref, send_ref, seed_ref, w2s_ref,
-    out_ref, part_ref,
+    core_ref, rows_ref, in_ref, send_ref, seed_ref, dout_ref, w2s_ref, w2n_ref,
+    out_ref, part_ref, w_ref,
 ):
     core = core_ref[0]
-    here = core_ref[1]
-    chips = [jnp.bitwise_xor(here, reverse(j)) for j in range(NZ)]
+    high, low, d, d_hidden = owner_grads(
+        core, in_ref, send_ref, seed_ref, dout_ref, w2s_ref, w2n_ref, w_ref
+    )
     pre = jnp.zeros((OWN, HID), F32)
-    for j in range(NZ):
-        a, b = wa_ref[j], wb_ref[j]
-        w = jnp.concatenate([a[:COLS], b[:COLS], a[COLS:], b[COLS:]], axis=0)
-        pre = pre + dot(rows_ref[chips[j]], w)
+    for z in range(NZ):
+        pre = pre + dot(rows_ref[z], w_ref[z])
     slope = jnp.exp(jnp.minimum(pre, 0.0))
     hidden = jnp.where(pre > 0, pre, slope - 1.0).astype(BF)
-    d_pre = (dh_ref[...] * slope).astype(BF)
-    for j in range(NZ):
-        g = dot(rows_ref[chips[j]], d_pre, 0, 0).astype(BF)
+    d_pre = (d_hidden * slope).astype(BF)
+    for z in range(NZ):
+        g = dot(rows_ref[z], d_pre, 0, 0).astype(BF)
         for q in range(ND):
             r, h = q // 2, q % 2
             at = (r // 4) * PAIR + (r % 4) * 16
             lanes = slice(h * 128, (h + 1) * 128)
             for side in range(2):
-                f = 2 * chips[j] + (core if side == 0 else 1 - core)
+                f = 2 * z + (core if side == 0 else 1 - core)
                 piece = g[at + side * COLS : at + side * COLS + 16, lanes]
                 out_ref[q, pl.ds(pl.multiple_of(G1 + f * 16, 16), 16), :] = piece
-    high, low = split(x_ref[...])
-    g2s = dot(hidden, d_ref[...], 0, 0).astype(BF)
+    g2s = dot(hidden, d, 0, 0).astype(BF)
     g2n = (dot(hidden, high, 0, 0) + dot(hidden, low, 0, 0)).astype(BF)
     for q in range(ND):
         g = g2s if q < 8 else g2n
@@ -221,17 +231,16 @@
     neigh_two, seed_rows, d_out,
 ):
     f = lax.axis_index("feat")
-    place = jnp.stack([jnp.bitwise_and(f, 1), jnp.right_shift(f, 1)])
+    q = lax.axis_index("dom")
+    core = jnp.bitwise_and(f, 1).reshape(1)
     chips = [[2 * z + c for z in range(NZ)] for c in range(2)]
     own = features[0]
     other = fetch(own, 1)
 
-    w1 = jnp.concatenate([w1_self, w1_neigh], axis=0)[None]
-    w1 = jnp.concatenate([w1, fetch(w1, 8)], axis=0)
-    w1 = jnp.concatenate([w1, fetch(w1, 4)], axis=0)
-    place_early, w1 = lax.optimization_barrier((place, w1))
-    w1 = jnp.concatenate([w1, fetch(w1, 2)], axis=0)
-    w1_other = fetch(w1, 1)
+    w1 = jnp.concatenate([w1_self, w1_neigh], axis=0)
+    start = (jnp.right_shift(q, 1) * 16, jnp.bitwise_and(q, 1) * 128)
+    piece = lax.dynamic_slice(w1, start, (16, 128))
+    piece = swap(jnp.broadcast_to(piece, (NF, 16, 128)), "feat").reshape(1, NF * 16, 128)
 
     send = send_rows[0, 0]
     seeds = seed_rows[0]
@@ -239,11 +248,12 @@
     picks, t_out = call(
         pick_body,
         "picks",
-        (shape((ND, SLOTS, SEEDS), BF), shape((ND, SLOTS, HID), BF)),
+        (shape((ND, SLOTS, SEEDS), BF), shape((ND, 2 * SLOTS, 128), BF)),
         [SMEM, VMEM, VMEM],
         us=5,
     )(recv_count[:, 0, 0], neigh_two[0, 0].T, grad_out)
-    t_in = swap(t_out, "dom")
+    piece = jnp.broadcast_to(piece, (ND, NF * 16, 128))
+    t_in = swap(jnp.concatenate([t_out, piece], axis=1), "dom")
 
     rows_out = call(
         rows_body,
@@ -253,23 +263,17 @@
         [pltpu.VMEM((NIN, PAIR), F32), pltpu.VMEM((HALF, PAIR), F32)],
         limit=24,
         us=22,
-    )(place_early, own, other, neigh_one.reshape(-1))
+    )(core, own, other, neigh_one.reshape(-1))
     rows_in = swap(rows_out, "feat", chips)
-
-    x, d, d_hidden = call(
-        owner_body,
-        "owner_grads",
-        (shape((OWN, HID), F32), shape((OWN, HID), BF), shape((OWN, HID), F32)),
-        [VMEM] * 6,
-    )(t_in.reshape(ND * SLOTS, HID), send, seeds, grad_out, w2_self, w2_neigh)
 
     to_dom, part = call(
         main_body,
         "project",
         (shape((ND, G1 + 256, 128), BF), shape((SEEDS, HID), F32)),
-        [SMEM] + [VMEM] * 9,
-        us=6,
-    )(place, rows_in, w1, w1_other, x, d, d_hidden, send, seeds, w2_self)
+        [SMEM] + [VMEM] * 7,
+        [pltpu.VMEM((NZ, 2 * PAIR, HID), BF)],
+        us=4,
+    )(core, rows_in, t_in, send, seeds, grad_out, w2_self, w2_neigh)
     from_dom = swap(to_dom, "dom")
 
     to_feat = call(first_sum_body, "sum_dom", shape((NF, 80, 128), BF), [VMEM])(from_dom)

time: 190 us -> 172 us (0.905)
  blocking collectives: 57 us -> 89.8 us
  waiting for transfers between devices: 41.5 us -> 11.5 us
  starting transfers between devices: 32.9 us -> 21.3 us
  local copies, waits for them, and re-layouts: 14.7 us -> 9.49 us
  Pallas kernels: 39 us -> 36.3 us
    all_to_all x2 -> x3, blocking collectives: 57 us -> 89.8 us  [swap(): lax.all_to_all(x, axis, split_axis=0, concat_axis=0, tiled=True, axis_ind...]
    ppermute x5 -> x1, waiting for transfers between devices: 30.9 us -> 0.01 us  [fetch(): return lax.ppermute(x, 'feat', [(i, i ^ bit) for i in range(NF)])]
    ppermute x5 -> x1, starting transfers between devices: 15.3 us -> 3.33 us  [fetch(): return lax.ppermute(x, 'feat', [(i, i ^ bit) for i in range(NF)])]
    unnamed x50 -> x33, local copies, waits for them, and re-layouts: 14.7 us -> 8.65 us
    pallas_call x2 -> x1, Pallas kernels: 5.73 us -> 3.88 us  [per_device(): call(pick_body, 'picks', (shape((ND, SLOTS, SEEDS), BF), shape((ND, 2 * S...]
  transfers between devices with their start and end apart: 8 -> 4, of which waited for: 3 -> 3; matrix products, arithmetic and copies ran while one was open for 3% -> 2% of each run, Pallas kernels for 18% -> 18%
where the time goes in v3:
time: 172 us; the launch traced here: 171 us
  blocking collectives  89.8 us (52%)
  Pallas kernels  36.3 us (21%)
  starting transfers between devices  21.3 us (12%)
  waiting for transfers between devices  11.5 us (7%)
  local copies, waits for them, and re-layouts  9.49 us (6%)
  other arithmetic  2.17 us (1%)
    all_to_all x3, blocking collectives, swap(): lax.all_to_all(x, axis, split_axis=0, concat_axis=0, tiled=True, axis_ind...  89.8 us
    pallas_call x1, Pallas kernels, per_device(): call(rows_body, 'node_rows', shape((NZ, OWN, 2 * PAIR), BF), [SMEM, VMEM,...  25.2 us
    all_to_all x3, starting transfers between devices, swap(): lax.all_to_all(x, axis, split_axis=0, concat_axis=0, tiled=True, axis_ind...  18 us
    all_to_all x3, waiting for transfers between devices, swap(): lax.all_to_all(x, axis, split_axis=0, concat_axis=0, tiled=True, axis_ind...  11.5 us
    unnamed x33, local copies, waits for them, and re-layouts  8.65 us
    pallas_call x1, Pallas kernels, per_device(): call(pick_body, 'picks', (shape((ND, SLOTS, SEEDS), BF), shape((ND, 2 * S...  3.88 us
  transfers between devices with their start and end apart: 4, of which 3 were waited for; matrix products, arithmetic and copies ran while one was open for 2% of the time, Pallas kernels for 18%

profile of v3, /device:TPU:1, one launch (start us, length us, event | category | flops | bytes accessed | tf_op | source)
XLA Modules:
  0.0 171.4 jit_solution(9192944445718699689)
XLA Ops:
  0.6 3.3 %collective-permute-start = (bf16[64,9216]{1,0:T(8,128)(2,1)}, bf16[64,9216]{1,0:T(8,128)(2,1)S(1)}, u32[]{:S(2)}, u32[]{:S(2)}) collective-permute-start(bf16[64,9216]{1,0:T(8,128)(2,1)} %bitcast.17), channel_id=1, source_target_pairs={{0,16},{16,0},{32,48},{48,32},{64,80},{80,64},{96,112},{112,96},{1... | collective-permute-start | bytes 3538952 | tf_op jit(solution)/shard_map/ppermute | solution.py:226
  4.0 0.7 fusion
  5.3 6.9 %all-to-all-start.1 = ((bf16[16,16,128]{2,1,0:T(8,128)(2,1)}), bf16[16,16,128]{2,1,0:T(8,128)(2,1)S(1)}, u32[]{:S(2)}, u32[]{:S(2)}) async-start(bf16[16,16,128]{2,1,0:T(8,128)(2,1)} %broadcast_in_dim.13), calls=%async_computation.1 | async-start | bytes 131072 | tf_op jit(solution)/shard_map/all_to_all | solution.py:220
  12.2 0.7 copy.18
  12.9 0.9 copy-done.10
  14.4 3.9 %picks.1 = (bf16[16,128,256]{2,1,0:T(8,128)(2,1)S(1)}, bf16[16,256,128]{2,1,0:T(8,128)(2,1)S(1)}) custom-call(s32[16]{0:T(128)S(1)} %bitcast.24, s32[15,256]{1,0:T(8,128)S(1)} %bitcast.16, bf16[256,256]{1,0:T(8,128)(2,1)S(1)} %bitcast.20), custom_call_target="tpu_custom_call" | custom-call | flops 5000000000 | bytes 5000000 | tf_op jit(solution)/shard_map/picks/pallas_call | solution.py:248
  18.3 1.0 copy-done
  19.3 0.7 all-to-all-done.1
  20.2 1.5 pad_maximum_fusion
  21.6 6.9 %all-to-all-start.2 = ((bf16[16,512,128]{2,1,0:T(8,128)(2,1)}), bf16[16,512,128]{2,1,0:T(8,128)(2,1)S(1)}, u32[]{:S(2)}, u32[]{:S(2)}) async-start(bf16[16,512,128]{2,1,0:T(8,128)(2,1)} %pad_maximum_fusion), calls=%async_computation.2 | async-start | bytes 4194304 | tf_op jit(solution)/shard_map/all_to_all | solution.py:220
  28.6 1.0 copy-done.7
  29.6 1.3 copy-done.6
  30.9 1.3 copy-done.8
  32.1 25.2 %node_rows.1 = bf16[8,288,256]{2,1,0:T(8,128)(2,1)S(1)} custom-call(s32[1]{0:T(128)} %bitcast.core_ref, bf16[64,9216]{1,0:T(8,128)(2,1)S(1)} %bitcast.18, bf16[64,9216]{1,0:T(8,128)(2,1)S(1)} %copy-done.8, s32[46080]{0:T(1024)S(1)} %bitcast.19), custom_call_target="tpu_custom_call" | custom-call | flops 22000001024 | bytes 22000000 | tf_op jit(solution)/shard_map/node_rows/pallas_call | solution.py:258
  57.7 34.0 %all_to_all.30.rows_ref = bf16[8,288,256]{2,1,0:T(8,128)(2,1)S(1)} all-to-all(bf16[8,288,256]{2,1,0:T(8,128)(2,1)S(1)} %node_rows.1), channel_id=1, replica_groups={{0,32,64,96,128,160,192,224},{16,48,80,112,144,176,208,240},{1,33,65,97..., dimensions={0} | all-to-all | bytes 2359296 | tf_op jit(solution)/shard_map/all_to_all | solution.py:220
  91.8 3.4 %project.1 = (bf16[16,576,128]{2,1,0:T(8,128)(2,1)S(1)}, f32[256,256]{1,0:T(8,128)S(1)}) custom-call(s32[1]{0:T(128)} %bitcast.core_ref, bf16[8,288,256]{2,1,0:T(8,128)(2,1)S(1)} %all_to_all.30.rows_ref, bf16[16,512,128]{2,1,0:T(8,128)(2,1)S(1)} %all-to-all-done.2.in_ref, s32[16,128]{1,0:T(8,128)S(1)} %bitcast.22, s32[1,256]{1,0:T(1,128)S(1)} %bitcast.23, ...), custom_call_target="tpu_custom_call" | custom-call | flops 4000000000 | bytes 4000000 | tf_op jit(solution)/shard_map/project/pallas_call | solution.py:269
  95.1 36.7 %all_to_all.31.in_ref = bf16[16,576,128]{2,1,0:T(8,128)(2,1)S(1)} all-to-all(bf16[16,576,128]{2,1,0:T(8,128)(2,1)S(1)} %get-tuple-element.14), channel_id=1, replica_groups=mesh['feat'=16,'dom'=16] {'dom'}, dimensions={0} | all-to-all | bytes 4718592 | tf_op jit(solution)/shard_map/all_to_all | solution.py:220
  132.0 19.1 %all_to_all.32.in_ref = bf16[16,80,128]{2,1,0:T(8,128)(2,1)S(1)} all-to-all(bf16[16,80,128]{2,1,0:T(8,128)(2,1)S(1)} %sum_dom.1), channel_id=1, replica_groups=mesh['feat'=16,'dom'=16] {'feat'}, dimensions={0} | all-to-all | bytes 655360 | tf_op jit(solution)/shard_map/all_to_all | solution.py:220
  151.2 0.9 copy-done.2
  152.0 4.3 %all-to-all-start.5 = ((f32[16,80,128]{2,1,0:T(8,128)}), f32[16,80,128]{2,1,0:T(8,128)}, u32[]{:S(2)}, u32[]{:S(2)}) async-start(f32[16,80,128]{2,1,0:T(8,128)} %copy-done.2), calls=%async_computation.5 | async-start | bytes 1310720 | tf_op jit(solution)/shard_map/all_to_all | solution.py:220
  156.3 0.9 copy-done.4
  157.3 1.7 layer_two.1
  158.9 10.6 %all-to-all-done.5.in_ref = f32[16,80,128]{2,1,0:T(8,128)} async-done(((f32[16,80,128]{2,1,0:T(8,128)}), f32[16,80,128]{2,1,0:T(8,128)}, u32[]{:S(2)}, u32[]{:S(2)}) %all-to-all-start.5) | async-done | bytes 655392 | tf_op jit(solution)/shard_map/all_to_all | solution.py:220
  169.5 1.9 %place.1 = (f32[64,256]{1,0:T(8,128)}, f32[64,256]{1,0:T(8,128)}, f32[256,256]{1,0:T(8,128)}, f32[256,256]{1,0:T(8,128)}) custom-call(f32[16,80,128]{2,1,0:T(8,128)} %all-to-all-done.5.in_ref), custom_call_target="tpu_custom_call" | custom-call | flops 1000000000 | bytes 1000000 | tf_op jit(solution)/shard_map/place/pallas_call | solution.py:288
  (31 shorter events, 2.1 us)
Async XLA Ops:
  0.6 27.9 %collective-permute-start = (bf16[64,9216]{1,0:T(8,128)(2,1)}, bf16[64,9216]{1,0:T(8,128)(2,1)S(1)}, u32[]{:S(2)}, u32[]{:S(2)}) collective-permute-start(bf16[64,9216]{1,0:T(8,128)(2,1)} %bitcast.17), channel_id=1, source_target_pairs={{0,16},{16,0},{32,48},{48,32},{64,80},{80,64},{96,112},{112,96},{1... | collective-permute-start | bytes 3538952 | tf_op jit(solution)/shard_map/ppermute | solution.py:226
  5.3 14.7 %all-to-all-start.1 = ((bf16[16,16,128]{2,1,0:T(8,128)(2,1)}), bf16[16,16,128]{2,1,0:T(8,128)(2,1)S(1)}, u32[]{:S(2)}, u32[]{:S(2)}) async-start(bf16[16,16,128]{2,1,0:T(8,128)(2,1)} %broadcast_in_dim.13), calls=%async_computation.1 | async-start | bytes 131072 | tf_op jit(solution)/shard_map/all_to_all | solution.py:220
  12.9 0.9 copy-start.10
  13.8 0.7 copy-start.15
  18.3 1.0 copy-start
  21.6 7.9 %copy-start.9 = (s32[1,10,4608]{2,0,1:T(1,128)S(1)}, s32[1,10,4608]{2,0,1:T(1,128)}, u32[]{:S(2)}) copy-start(s32[1,10,4608]{2,0,1:T(1,128)} %param.16) | copy-start | bytes 552964
  21.6 36.0 %all-to-all-start.2 = ((bf16[16,512,128]{2,1,0:T(8,128)(2,1)}), bf16[16,512,128]{2,1,0:T(8,128)(2,1)S(1)}, u32[]{:S(2)}, u32[]{:S(2)}) async-start(bf16[16,512,128]{2,1,0:T(8,128)(2,1)} %pad_maximum_fusion), calls=%async_computation.2 | async-start | bytes 4194304 | tf_op jit(solution)/shard_map/all_to_all | solution.py:220
  28.5 1.0 copy-start.7
  29.6 1.3 copy-start.6
  30.8 1.3 copy-start.8
  57.3 34.4 %copy-start.5 = (bf16[256,256]{1,0:T(8,128)(2,1)S(1)}, bf16[256,256]{1,0:T(8,128)(2,1)}, u32[]{:S(2)}) copy-start(bf16[256,256]{1,0:T(8,128)(2,1)} %w2n_ref.3) | copy-start | bytes 393220
  57.4 34.4 %copy-start.11 = (bf16[1,1,256,256]{3,2,1,0:T(8,128)(2,1)S(1)}, bf16[1,1,256,256]{3,2,1,0:T(8,128)(2,1)}, u32[]{:S(2)}) copy-start(bf16[1,1,256,256]{3,2,1,0:T(8,128)(2,1)} %param.21) | copy-start | bytes 393220
  57.4 34.4 %copy-start.13 = (s32[1,1,16,128]{3,2,1,0:T(8,128)S(1)}, s32[1,1,16,128]{3,2,1,0:T(8,128)}, u32[]{:S(2)}) copy-start(s32[1,1,16,128]{3,2,1,0:T(8,128)} %param.17) | copy-start | bytes 24580
  57.4 34.4 %copy-start.14 = (s32[1,1,256]{2,1,0:T(1,128)S(1)}, s32[1,1,256]{2,1,0:T(1,128)}, u32[]{:S(2)}) copy-start(s32[1,1,256]{2,1,0:T(1,128)} %param.20) | copy-start | bytes 3076
  57.7 34.1 %copy-start.12 = (bf16[256,256]{1,0:T(8,128)(2,1)S(1)}, bf16[256,256]{1,0:T(8,128)(2,1)}, u32[]{:S(2)}) copy-start(bf16[256,256]{1,0:T(8,128)(2,1)} %w2s_ref.1) | copy-start | bytes 393220
  95.1 36.7 %copy-start.3 = (f32[256,256]{1,0:T(8,128)}, f32[256,256]{1,0:T(8,128)S(1)}, u32[]{:S(2)}) copy-start(f32[256,256]{1,0:T(8,128)S(1)} %get-tuple-element.16.part_ref) | copy-start | bytes 786436
  151.1 5.2 %copy-start.1 = (bf16[16,128,256]{2,1,0:T(8,128)(2,1)S(1)}, bf16[16,128,256]{2,1,0:T(8,128)(2,1)}, u32[]{:S(2)}) copy-start(bf16[16,128,256]{2,1,0:T(8,128)(2,1)} %copy-done) | copy-start | bytes 3145732
  151.2 0.9 copy-start.2
  152.0 17.5 %all-to-all-start.5 = ((f32[16,80,128]{2,1,0:T(8,128)}), f32[16,80,128]{2,1,0:T(8,128)}, u32[]{:S(2)}, u32[]{:S(2)}) async-start(f32[16,80,128]{2,1,0:T(8,128)} %copy-done.2), calls=%async_computation.5 | async-start | bytes 1310720 | tf_op jit(solution)/shard_map/all_to_all | solution.py:220
  156.3 1.0 copy-start.4

commit v4 on v3

--- a/solution.py
+++ b/solution.py
@@ -50,23 +50,25 @@
     return lax.dot_general(a, b, (((ca,), (cb,)), ((), ())), preferred_element_type=F32)
 
 
-def pick_body(count_ref, neigh_ref, dout_ref, picks_ref, t_ref):
+def picks_of(source, start, count_ref, lanes):
+    count = count_ref[source]
+    row = lax.broadcasted_iota(I32, (SLOTS, SEEDS), 0)
+    position = jnp.where(row < count, row + start, -1)
+    total = jnp.zeros((SLOTS, SEEDS), F32)
+    for k in range(K2):
+        total = total + jnp.where(position == lanes[k : k + 1, :], 1.0, 0.0)
+    return total.astype(BF), start + count
+
+
+def pick_body(count_ref, neigh_ref, dout_ref, t_ref):
     start = jnp.int32(0)
     lanes = neigh_ref[...]
     d_out = dout_ref[...]
-    row = lax.broadcasted_iota(I32, (SLOTS, SEEDS), 0)
     for s in range(ND):
-        count = count_ref[s]
-        position = jnp.where(row < count, row + start, -1)
-        total = jnp.zeros((SLOTS, SEEDS), F32)
-        for k in range(K2):
-            total = total + jnp.where(position == lanes[k : k + 1, :], 1.0, 0.0)
-        picks = total.astype(BF)
-        picks_ref[s] = picks
+        picks, start = picks_of(s, start, count_ref, lanes)
         t = dot(picks, d_out).astype(BF)
         t_ref[s, 0:SLOTS, :] = t[:, 0:128]
         t_ref[s, SLOTS : 2 * SLOTS, :] = t[:, 128:256]
-        start = start + count
 
 
 def rows_body(core_ref, own_ref, other_ref, index_ref, out_ref, table, sums):
@@ -101,7 +103,7 @@
     return high, (x - high.astype(F32)).astype(BF)
 
 
-def owner_grads(core, in_ref, send_ref, seed_ref, dout_ref, w2s_ref, w2n_ref, w_ref):
+def owner_grads(in_ref, other_ref, send_ref, seed_ref, dout_ref, w2s_ref, w2n_ref, w_ref):
     d_out = dout_ref[...]
     row = lax.broadcasted_iota(I32, (OWN, SEEDS), 0)
     x = jnp.zeros((OWN, HID), F32)
@@ -123,23 +125,23 @@
     w2n = w2n_ref[...]
     d_hidden = dot(high, w2n, 1, 1) + dot(low, w2n, 1, 1) + dot(d, w2s_ref[...], 1, 1)
     for z in range(NZ):
-        for side in range(2):
-            f = 2 * z + (core if side == 0 else 1 - core)
-            start = pl.multiple_of(2 * SLOTS + f * 16, 16)
-            for q in range(ND):
-                r, h = q // 2, q % 2
-                at = (r // 4) * PAIR + side * COLS + (r % 4) * 16
-                w_ref[z, at : at + 16, h * 128 : (h + 1) * 128] = in_ref[q, pl.ds(start, 16), :]
+        for q in range(ND):
+            r, h = q // 2, q % 2
+            at = (r // 4) * PAIR + (r % 4) * 16
+            lanes = slice(h * 128, (h + 1) * 128)
+            own = in_ref[q, 2 * SLOTS + z * 16 : 2 * SLOTS + z * 16 + 16, :]
+            w_ref[z, at : at + 16, lanes] = own
+            w_ref[z, at + COLS : at + COLS + 16, lanes] = other_ref[q, z * 16 : z * 16 + 16, :]
     return high, low, d, d_hidden
 
 
 def main_body(
-    core_ref, rows_ref, in_ref, send_ref, seed_ref, dout_ref, w2s_ref, w2n_ref,
+    core_ref, rows_ref, in_ref, other_ref, send_ref, seed_ref, dout_ref, w2s_ref, w2n_ref,
     out_ref, part_ref, w_ref,
 ):
     core = core_ref[0]
     high, low, d, d_hidden = owner_grads(
-        core, in_ref, send_ref, seed_ref, dout_ref, w2s_ref, w2n_ref, w_ref
+        in_ref, other_ref, send_ref, seed_ref, dout_ref, w2s_ref, w2n_ref, w_ref
     )
     pre = jnp.zeros((OWN, HID), F32)
     for z in range(NZ):
@@ -191,6 +193,7 @@
     total = in_ref[0].astype(F32)
     for f in range(1, NF):
         total = total + in_ref[f].astype(F32)
+    total = total.astype(BF)
     for q in range(ND):
         out_ref[q] = total
 
@@ -199,21 +202,23 @@
     for q in range(ND):
         r, h = q // 2, q % 2
         g1 = g1s_ref if r < 4 else g1n_ref
-        g1[(r % 4) * 16 : (r % 4) * 16 + 16, h * 128 : (h + 1) * 128] = in_ref[q, 0:16, :]
+        g1[(r % 4) * 16 : (r % 4) * 16 + 16, h * 128 : (h + 1) * 128] = in_ref[q, 0:16, :].astype(F32)
         g2 = g2s_ref if q < 8 else g2n_ref
         for half in range(2):
-            piece = in_ref[q, 16 + half * 32 : 48 + half * 32, :]
+            piece = in_ref[q, 16 + half * 32 : 48 + half * 32, :].astype(F32)
             g2[(q % 8) * 32 : (q % 8) * 32 + 32, half * 128 : (half + 1) * 128] = piece
 
 
-def layer_body(in_ref, picks_ref, part_ref, w2n_ref, layer_ref):
-    total = part_ref[...]
-    picks = picks_ref[...]
-    for h in range(2):
-        rows = in_ref[:, h * SLOTS : (h + 1) * SLOTS, :].reshape(ND * SLOTS, 128)
-        mean = (dot(picks, rows, 0, 0) * (1.0 / K2)).astype(BF)
-        total = total + dot(mean, w2n_ref[h * 128 : (h + 1) * 128, :])
-    layer_ref[...] = total.astype(BF)
+def layer_body(count_ref, neigh_ref, in_ref, part_ref, w2n_ref, layer_ref):
+    start = jnp.int32(0)
+    names = neigh_ref[...]
+    total = jnp.zeros((SEEDS, HID), F32)
+    for s in range(ND):
+        picks, start = picks_of(s, start, count_ref, names)
+        rows = [in_ref[s, 0:SLOTS, :], in_ref[s, SLOTS : 2 * SLOTS, :]]
+        total = total + dot(picks, jnp.concatenate(rows, axis=1), 0, 0)
+    mean_two = (total * (1.0 / K2)).astype(BF)
+    layer_ref[...] = (part_ref[...] + dot(mean_two, w2n_ref[...])).astype(BF)
 
 
 def swap(x, axis, groups=None):
@@ -240,20 +245,19 @@
     w1 = jnp.concatenate([w1_self, w1_neigh], axis=0)
     start = (jnp.right_shift(q, 1) * 16, jnp.bitwise_and(q, 1) * 128)
     piece = lax.dynamic_slice(w1, start, (16, 128))
-    piece = swap(jnp.broadcast_to(piece, (NF, 16, 128)), "feat").reshape(1, NF * 16, 128)
+    piece = swap(jnp.broadcast_to(piece, (NZ, 16, 128)), "feat", chips).reshape(1, NZ * 16, 128)
 
     send = send_rows[0, 0]
     seeds = seed_rows[0]
     grad_out = d_out[0, 0]
-    picks, t_out = call(
-        pick_body,
-        "picks",
-        (shape((ND, SLOTS, SEEDS), BF), shape((ND, 2 * SLOTS, 128), BF)),
-        [SMEM, VMEM, VMEM],
-        us=5,
-    )(recv_count[:, 0, 0], neigh_two[0, 0].T, grad_out)
-    piece = jnp.broadcast_to(piece, (ND, NF * 16, 128))
+    counts = recv_count[:, 0, 0]
+    names = neigh_two[0, 0].T
+    t_out = call(
+        pick_body, "picks", shape((ND, 2 * SLOTS, 128), BF), [SMEM, VMEM, VMEM], limit=60, us=5
+    )(counts, names, grad_out)
+    piece = jnp.broadcast_to(piece, (ND, NZ * 16, 128))
     t_in = swap(jnp.concatenate([t_out, piece], axis=1), "dom")
+    w1_other = fetch(t_in[:, 2 * SLOTS :], 1)
 
     rows_out = call(
         rows_body,
@@ -261,7 +265,7 @@
         shape((NZ, OWN, 2 * PAIR), BF),
         [SMEM, VMEM, VMEM, SMEM],
         [pltpu.VMEM((NIN, PAIR), F32), pltpu.VMEM((HALF, PAIR), F32)],
-        limit=24,
+        limit=60,
         us=22,
     )(core, own, other, neigh_one.reshape(-1))
     rows_in = swap(rows_out, "feat", chips)
@@ -270,18 +274,23 @@
         main_body,
         "project",
         (shape((ND, G1 + 256, 128), BF), shape((SEEDS, HID), F32)),
-        [SMEM] + [VMEM] * 7,
+        [SMEM] + [VMEM] * 8,
         [pltpu.VMEM((NZ, 2 * PAIR, HID), BF)],
         us=4,
-    )(core, rows_in, t_in, send, seeds, grad_out, w2_self, w2_neigh)
+    )(core, rows_in, t_in, w1_other, send, seeds, grad_out, w2_self, w2_neigh)
     from_dom = swap(to_dom, "dom")
 
     to_feat = call(first_sum_body, "sum_dom", shape((NF, 80, 128), BF), [VMEM])(from_dom)
     from_feat = swap(to_feat, "feat")
-    layer_out = call(layer_body, "layer_two", shape((SEEDS, HID), BF), [VMEM] * 4)(
-        from_dom, picks.reshape(ND * SLOTS, SEEDS), part, w2_neigh
-    )
-    done = call(second_sum_body, "sum_feat", shape((ND, 80, 128), F32), [VMEM])(from_feat)
+    layer_out = call(
+        layer_body,
+        "layer_two",
+        shape((SEEDS, HID), BF),
+        [SMEM] + [VMEM] * 4,
+        limit=60,
+        us=5,
+    )(counts, names, from_dom, part, w2_neigh)
+    done = call(second_sum_body, "sum_feat", shape((ND, 80, 128), BF), [VMEM], limit=60)(from_feat)
     done = swap(done, "dom")
     first = shape((COLS, HID), F32)
     second = shape((HID, HID), F32)

time: 172 us -> 171 us (level)
  blocking collectives: 89.8 us -> 54.5 us
  waiting for transfers between devices: 11.5 us -> 34 us
  Pallas kernels: 36.3 us -> 43.8 us
  starting transfers between devices: 21.3 us -> 28 us
  local copies, waits for them, and re-layouts: 9.49 us -> 5.96 us
    all_to_all x3 -> x2, blocking collectives: 89.8 us -> 54.5 us  [swap(): lax.all_to_all(x, axis, split_axis=0, concat_axis=0, tiled=True, axis_ind...]
    all_to_all x3 -> x4, waiting for transfers between devices: 11.5 us -> 32.5 us  [swap(): lax.all_to_all(x, axis, split_axis=0, concat_axis=0, tiled=True, axis_ind...]
    pallas_call x3, Pallas kernels: 5.63 us -> 12.9 us  [the longest x1 5.89 us: per_device(): call(layer_body, 'layer_two', shape((SEEDS, HID), BF), [SMEM] + [VMEM] *...]
    all_to_all x3 -> x4, starting transfers between devices: 18 us -> 23.4 us  [swap(): lax.all_to_all(x, axis, split_axis=0, concat_axis=0, tiled=True, axis_ind...]
    unnamed x33 -> x17, local copies, waits for them, and re-layouts: 8.65 us -> 5.2 us
    ppermute x1 -> x2, starting transfers between devices: 3.33 us -> 4.57 us  [fetch(): return lax.ppermute(x, 'feat', [(i, i ^ bit) for i in range(NF)])]
  transfers between devices with their start and end apart: 4 -> 6, of which waited for: 3 -> 4; matrix products, arithmetic and copies ran while one was open for 2% -> 3% of each run, Pallas kernels for 18% -> 22%
where the time goes in v4:
time: 171 us; the launch traced here: 170 us
  blocking collectives  54.5 us (32%)
  Pallas kernels  43.8 us (26%)
  waiting for transfers between devices  34 us (20%)
  starting transfers between devices  28 us (16%)
  local copies, waits for them, and re-layouts  5.96 us (3%)
  other arithmetic  3.24 us (2%)
    all_to_all x2, blocking collectives, swap(): lax.all_to_all(x, axis, split_axis=0, concat_axis=0, tiled=True, axis_ind...  54.5 us
    all_to_all x4, waiting for transfers between devices, swap(): lax.all_to_all(x, axis, split_axis=0, concat_axis=0, tiled=True, axis_ind...  32.5 us
    pallas_call x1, Pallas kernels, per_device(): call(rows_body, 'node_rows', shape((NZ, OWN, 2 * PAIR), BF), [SMEM, VMEM,...  26.5 us
    all_to_all x4, starting transfers between devices, swap(): lax.all_to_all(x, axis, split_axis=0, concat_axis=0, tiled=True, axis_ind...  23.4 us
    pallas_call x1, Pallas kernels, per_device(): call(layer_body, 'layer_two', shape((SEEDS, HID), BF), [SMEM] + [VMEM] *...  5.89 us
    pallas_call x1, Pallas kernels, per_device(): call(pick_body, 'picks', shape((ND, 2 * SLOTS, 128), BF), [SMEM, VMEM, VM...  5.22 us
    unnamed x17, local copies, waits for them, and re-layouts  5.2 us
    ppermute x2, starting transfers between devices, fetch(): return lax.ppermute(x, 'feat', [(i, i ^ bit) for i in range(NF)])  4.57 us
  transfers between devices with their start and end apart: 6, of which 4 were waited for; matrix products, arithmetic and copies ran while one was open for 3% of the time, Pallas kernels for 22%

profile of v4, /device:TPU:1, one launch (start us, length us, event | category | flops | bytes accessed | tf_op | source)
XLA Modules:
  0.0 170.3 jit_solution(5446031256427536416)
XLA Ops:
  0.6 3.3 %collective-permute-start = (bf16[64,9216]{1,0:T(8,128)(2,1)}, bf16[64,9216]{1,0:T(8,128)(2,1)S(1)}, u32[]{:S(2)}, u32[]{:S(2)}) collective-permute-start(bf16[64,9216]{1,0:T(8,128)(2,1)} %bitcast.21), channel_id=1, source_target_pairs={{0,16},{16,0},{32,48},{48,32},{64,80},{80,64},{96,112},{112,96},{1... | collective-permute-start | bytes 3538952 | tf_op jit(solution)/shard_map/ppermute | solution.py:231
  4.0 0.7 fusion
  5.3 6.5 %all-to-all-start.1 = ((bf16[8,16,128]{2,1,0:T(8,128)(2,1)}), bf16[8,16,128]{2,1,0:T(8,128)(2,1)S(1)}, u32[]{:S(2)}, u32[]{:S(2)}) async-start(bf16[8,16,128]{2,1,0:T(8,128)(2,1)} %broadcast_in_dim.13), calls=%async_computation.1 | async-start | bytes 65536 | tf_op jit(solution)/shard_map/all_to_all | solution.py:225
  11.7 1.3 copy.18
  13.0 5.2 %picks.1 = bf16[16,256,128]{2,1,0:T(8,128)(2,1)} custom-call(s32[16]{0:T(128)} %bitcast.24, s32[15,256]{1,0:T(8,128)} %bitcast.19, bf16[256,256]{1,0:T(8,128)(2,1)} %bitcast.14), custom_call_target="tpu_custom_call" | custom-call | flops 5000000000 | bytes 5000000 | tf_op jit(solution)/shard_map/picks/pallas_call | solution.py:255
  18.7 2.5 %pad_maximum_fusion = bf16[16,384,128]{2,1,0:T(8,128)(2,1)} fusion(bf16[16,128,128]{2,1,0:T(8,128)(2,1)S(1)} %broadcast_in_dim.15, bf16[16,256,128]{2,1,0:T(8,128)(2,1)} %picks.1), kind=kLoop, calls=%fused_computation | loop fusion | flops 3145728 | bytes 3145728 | tf_op jit(solution)/shard_map/concatenate | solution.py:259
  21.3 6.8 %all-to-all-start.2 = ((bf16[16,384,128]{2,1,0:T(8,128)(2,1)}), bf16[16,384,128]{2,1,0:T(8,128)(2,1)S(1)}, u32[]{:S(2)}, u32[]{:S(2)}) async-start(bf16[16,384,128]{2,1,0:T(8,128)(2,1)} %pad_maximum_fusion), calls=%async_computation.2 | async-start | bytes 3145728 | tf_op jit(solution)/shard_map/all_to_all | solution.py:225
  28.0 1.0 copy-done.7
  29.1 26.5 %node_rows.1 = bf16[8,288,256]{2,1,0:T(8,128)(2,1)} custom-call(s32[1]{0:T(128)} %bitcast.2.core_ref, bf16[64,9216]{1,0:T(8,128)(2,1)} %bitcast.22, bf16[64,9216]{1,0:T(8,128)(2,1)} %copy-done.7, s32[46080]{0:T(1024)} %bitcast.23), custom_call_target="tpu_custom_call" | custom-call | flops 22000001024 | bytes 22000000 | tf_op jit(solution)/shard_map/node_rows/pallas_call | solution.py:262
  55.6 6.5 %all-to-all-start = ((bf16[8,288,256]{2,1,0:T(8,128)(2,1)}), bf16[8,288,256]{2,1,0:T(8,128)(2,1)S(1)}, u32[]{:S(2)}, u32[]{:S(2)}) async-start(bf16[8,288,256]{2,1,0:T(8,128)(2,1)} %node_rows.1), calls=%async_computation | async-start | bytes 2359296 | tf_op jit(solution)/shard_map/all_to_all | solution.py:225
  62.1 1.2 collective-permute-start.1
  63.3 1.5 collective-permute-done.1.other_ref
  64.9 29.2 %all-to-all-done.rows_ref = bf16[8,288,256]{2,1,0:T(8,128)(2,1)S(1)} async-done(((bf16[8,288,256]{2,1,0:T(8,128)(2,1)}), bf16[8,288,256]{2,1,0:T(8,128)(2,1)S(1)}, u32[]{:S(2)}, u32[]{:S(2)}) %all-to-all-start) | async-done | bytes 1179680 | tf_op jit(solution)/shard_map/all_to_all | solution.py:225
  94.1 0.9 copy-done.3
  95.0 3.4 %project.1 = (bf16[16,576,128]{2,1,0:T(8,128)(2,1)S(1)}, f32[256,256]{1,0:T(8,128)S(1)}) custom-call(s32[1]{0:T(128)} %bitcast.2.core_ref, bf16[8,288,256]{2,1,0:T(8,128)(2,1)S(1)} %all-to-all-done.rows_ref, bf16[16,384,128]{2,1,0:T(8,128)(2,1)S(1)} %all-to-all-done.2.in_ref, bf16[16,128,128]{2,1,0:T(8,128)(2,1)S(1)} %collective-permute-done.1.other_ref, ...), custom_call_target="tpu_custom_call" | custom-call | flops 4000000000 | bytes 4000000 | tf_op jit(solution)/shard_map/project/pallas_call | solution.py:273
  98.4 0.7 copy-done.6
  99.1 36.3 %all_to_all.30.in_ref = bf16[16,576,128]{2,1,0:T(8,128)(2,1)S(1)} all-to-all(bf16[16,576,128]{2,1,0:T(8,128)(2,1)S(1)} %get-tuple-element.11), channel_id=1, replica_groups=mesh['feat'=16,'dom'=16] {'dom'}, dimensions={0} | all-to-all | bytes 4718592 | tf_op jit(solution)/shard_map/all_to_all | solution.py:225
  135.5 1.2 copy-done
  136.8 18.3 %all_to_all.31.in_ref = bf16[16,80,128]{2,1,0:T(8,128)(2,1)} all-to-all(bf16[16,80,128]{2,1,0:T(8,128)(2,1)S(1)} %sum_dom.1), channel_id=1, replica_groups=mesh['feat'=16,'dom'=16] {'feat'}, dimensions={0} | all-to-all | bytes 655360 | tf_op jit(solution)/shard_map/all_to_all | solution.py:225
  155.1 1.7 %sum_feat.1 = bf16[16,80,128]{2,1,0:T(8,128)(2,1)} custom-call(bf16[16,80,128]{2,1,0:T(8,128)(2,1)} %all_to_all.31.in_ref), custom_call_target="tpu_custom_call" | custom-call | flops 1000000000 | bytes 1000000 | tf_op jit(solution)/shard_map/sum_feat/pallas_call | solution.py:293
  156.8 3.7 %all-to-all-start.5 = ((bf16[16,80,128]{2,1,0:T(8,128)(2,1)}), bf16[16,80,128]{2,1,0:T(8,128)(2,1)S(1)}, u32[]{:S(2)}, u32[]{:S(2)}) async-start(bf16[16,80,128]{2,1,0:T(8,128)(2,1)} %sum_feat.1), calls=%async_computation.5 | async-start | bytes 655360 | tf_op jit(solution)/shard_map/all_to_all | solution.py:225
  160.5 5.9 %layer_two.1 = bf16[256,256]{1,0:T(8,128)(2,1)} custom-call(s32[16]{0:T(128)} %bitcast.25, s32[15,256]{1,0:T(8,128)} %bitcast.20, bf16[16,576,128]{2,1,0:T(8,128)(2,1)} %copy-done, f32[256,256]{1,0:T(8,128)} %copy-done.6, bf16[256,256]{1,0:T(8,128)(2,1)} %w2n_ref.3), custom_call_target="tpu_custom_call" | custom-call | flops 5000000000 | bytes 5000000 | tf_op jit(solution)/shard_map/layer_two/pallas_call | solution.py:285
  166.4 3.0 %all-to-all-done.5.in_ref = bf16[16,80,128]{2,1,0:T(8,128)(2,1)S(1)} async-done(((bf16[16,80,128]{2,1,0:T(8,128)(2,1)}), bf16[16,80,128]{2,1,0:T(8,128)(2,1)S(1)}, u32[]{:S(2)}, u32[]{:S(2)}) %all-to-all-start.5) | async-done | bytes 327712 | tf_op jit(solution)/shard_map/all_to_all | solution.py:225
  169.4 0.9 place.1
  (19 shorter events, 1.3 us)
Async XLA Ops:
  0.6 27.4 %collective-permute-start = (bf16[64,9216]{1,0:T(8,128)(2,1)}, bf16[64,9216]{1,0:T(8,128)(2,1)S(1)}, u32[]{:S(2)}, u32[]{:S(2)}) collective-permute-start(bf16[64,9216]{1,0:T(8,128)(2,1)} %bitcast.21), channel_id=1, source_target_pairs={{0,16},{16,0},{32,48},{48,32},{64,80},{80,64},{96,112},{112,96},{1... | collective-permute-start | bytes 3538952 | tf_op jit(solution)/shard_map/ppermute | solution.py:231
  5.3 13.3 %all-to-all-start.1 = ((bf16[8,16,128]{2,1,0:T(8,128)(2,1)}), bf16[8,16,128]{2,1,0:T(8,128)(2,1)S(1)}, u32[]{:S(2)}, u32[]{:S(2)}) async-start(bf16[8,16,128]{2,1,0:T(8,128)(2,1)} %broadcast_in_dim.13), calls=%async_computation.1 | async-start | bytes 65536 | tf_op jit(solution)/shard_map/all_to_all | solution.py:225
  21.3 34.3 %all-to-all-start.2 = ((bf16[16,384,128]{2,1,0:T(8,128)(2,1)}), bf16[16,384,128]{2,1,0:T(8,128)(2,1)S(1)}, u32[]{:S(2)}, u32[]{:S(2)}) async-start(bf16[16,384,128]{2,1,0:T(8,128)(2,1)} %pad_maximum_fusion), calls=%async_computation.2 | async-start | bytes 3145728 | tf_op jit(solution)/shard_map/all_to_all | solution.py:225
  28.0 1.0 copy-start.7
  55.5 38.5 %copy-start.1 = (bf16[1,1,256,256]{3,2,1,0:T(8,128)(2,1)S(1)}, bf16[1,1,256,256]{3,2,1,0:T(8,128)(2,1)}, u32[]{:S(2)}) copy-start(bf16[1,1,256,256]{3,2,1,0:T(8,128)(2,1)} %param.21) | copy-start | bytes 393220
  55.5 38.5 %copy-start.2 = (bf16[256,256]{1,0:T(8,128)(2,1)S(1)}, bf16[256,256]{1,0:T(8,128)(2,1)}, u32[]{:S(2)}) copy-start(bf16[256,256]{1,0:T(8,128)(2,1)} %w2s_ref.1) | copy-start | bytes 393220
  55.6 38.5 %copy-start.4 = (s32[1,1,16,128]{3,2,1,0:T(8,128)S(1)}, s32[1,1,16,128]{3,2,1,0:T(8,128)}, u32[]{:S(2)}) copy-start(s32[1,1,16,128]{3,2,1,0:T(8,128)} %param.17) | copy-start | bytes 24580
  55.6 38.5 %copy-start.5 = (s32[1,1,256]{2,1,0:T(1,128)S(1)}, s32[1,1,256]{2,1,0:T(1,128)}, u32[]{:S(2)}) copy-start(s32[1,1,256]{2,1,0:T(1,128)} %param.20) | copy-start | bytes 3076
  55.6 38.5 %all-to-all-start = ((bf16[8,288,256]{2,1,0:T(8,128)(2,1)}), bf16[8,288,256]{2,1,0:T(8,128)(2,1)S(1)}, u32[]{:S(2)}, u32[]{:S(2)}) async-start(bf16[8,288,256]{2,1,0:T(8,128)(2,1)} %node_rows.1), calls=%async_computation | async-start | bytes 2359296 | tf_op jit(solution)/shard_map/all_to_all | solution.py:225
  62.1 2.8 %collective-permute-start.1 = (bf16[16,128,128]{2,1,0:T(8,128)(2,1)S(1)}, bf16[16,128,128]{2,1,0:T(8,128)(2,1)S(1)}, u32[]{:S(2)}, u32[]{:S(2)}) collective-permute-start(bf16[16,128,128]{2,1,0:T(8,128)(2,1)S(1)} %slice.4), channel_id=1, source_target_pairs={{0,16},{16,0},{32,48},{48,32},{64,80},{80,64},{96,112},{112,96},{1... | collective-permute-start | bytes 1572872 | tf_op jit(solution)/shard_map/ppermute | solution.py:231
  94.1 0.9 copy-start.3
  98.4 0.7 copy-start.6
  135.4 1.4 copy-start
  156.8 12.6 %all-to-all-start.5 = ((bf16[16,80,128]{2,1,0:T(8,128)(2,1)}), bf16[16,80,128]{2,1,0:T(8,128)(2,1)S(1)}, u32[]{:S(2)}, u32[]{:S(2)}) async-start(bf16[16,80,128]{2,1,0:T(8,128)(2,1)} %sum_feat.1), calls=%async_computation.5 | async-start | bytes 655360 | tf_op jit(solution)/shard_map/all_to_all | solution.py:225

commit v5 on v4

--- a/solution.py
+++ b/solution.py
@@ -24,7 +24,7 @@
 HID = 256
 UNROLL = 16
 G2 = 256
-G1 = 320
+RING = (0, -1, 1, -2, 2, -3, 3, -4)
 VMEM = pl.BlockSpec(memory_space=pltpu.VMEM)
 SMEM = pl.BlockSpec(memory_space=pltpu.SMEM)
 
@@ -66,12 +66,12 @@
     d_out = dout_ref[...]
     for s in range(ND):
         picks, start = picks_of(s, start, count_ref, lanes)
-        t = dot(picks, d_out).astype(BF)
-        t_ref[s, 0:SLOTS, :] = t[:, 0:128]
-        t_ref[s, SLOTS : 2 * SLOTS, :] = t[:, 128:256]
-
-
-def rows_body(core_ref, own_ref, other_ref, index_ref, out_ref, table, sums):
+        t_ref[s] = dot(picks, d_out).astype(BF)
+
+
+def rows_body(
+    core_ref, own_ref, other_ref, index_ref, w_ref, wo_ref, out_ref, part_ref, table, sums
+):
     core = core_ref[0]
     step = 512
     for c in range(0, NIN, step):
@@ -93,9 +93,12 @@
         return carry
 
     lax.fori_loop(0, HALF // UNROLL, block, 0)
+    a, b = w_ref[...], wo_ref[...]
+    w = jnp.concatenate([a[:COLS], b[:COLS], a[COLS:], b[COLS:]], axis=0)
     for z in range(NZ):
         mean = sums[z * OWN : (z + 1) * OWN, :] * (1.0 / K1)
         out_ref[z, :, PAIR : 2 * PAIR] = mean.astype(BF)
+        part_ref[z] = dot(out_ref[z], w).astype(BF)
 
 
 def split(x):
@@ -103,62 +106,33 @@
     return high, (x - high.astype(F32)).astype(BF)
 
 
-def owner_grads(in_ref, other_ref, send_ref, seed_ref, dout_ref, w2s_ref, w2n_ref, w_ref):
-    d_out = dout_ref[...]
+def owner_grads(in_ref, send_ref, seed_ref, dout_ref, w2s_ref, w2n_ref):
     row = lax.broadcasted_iota(I32, (OWN, SEEDS), 0)
     x = jnp.zeros((OWN, HID), F32)
     for q in range(0, ND, 2):
         lanes = jnp.concatenate([send_ref[q : q + 1, :], send_ref[q + 1 : q + 2, :]], axis=1)
         hot = jnp.where(row == lanes, 1.0, 0.0).astype(BF)
-        t = jnp.concatenate(
-            [
-                jnp.concatenate([in_ref[i, 0:SLOTS, :], in_ref[i, SLOTS : 2 * SLOTS, :]], axis=1)
-                for i in (q, q + 1)
-            ],
-            axis=0,
-        )
-        x = x + dot(hot, t)
+        x = x + dot(hot, in_ref[q : q + 2].reshape(2 * SLOTS, HID))
     x = x * (1.0 / K2)
     hot = jnp.where(row == seed_ref[...], 1.0, 0.0).astype(BF)
-    d = dot(hot, d_out).astype(BF)
+    d = dot(hot, dout_ref[...]).astype(BF)
     high, low = split(x)
     w2n = w2n_ref[...]
     d_hidden = dot(high, w2n, 1, 1) + dot(low, w2n, 1, 1) + dot(d, w2s_ref[...], 1, 1)
-    for z in range(NZ):
-        for q in range(ND):
-            r, h = q // 2, q % 2
-            at = (r // 4) * PAIR + (r % 4) * 16
-            lanes = slice(h * 128, (h + 1) * 128)
-            own = in_ref[q, 2 * SLOTS + z * 16 : 2 * SLOTS + z * 16 + 16, :]
-            w_ref[z, at : at + 16, lanes] = own
-            w_ref[z, at + COLS : at + COLS + 16, lanes] = other_ref[q, z * 16 : z * 16 + 16, :]
     return high, low, d, d_hidden
 
 
 def main_body(
-    core_ref, rows_ref, in_ref, other_ref, send_ref, seed_ref, dout_ref, w2s_ref, w2n_ref,
-    out_ref, part_ref, w_ref,
+    share_ref, in_ref, send_ref, seed_ref, dout_ref, w2s_ref, w2n_ref,
+    out_ref, part_ref, dpre_ref,
 ):
-    core = core_ref[0]
-    high, low, d, d_hidden = owner_grads(
-        in_ref, other_ref, send_ref, seed_ref, dout_ref, w2s_ref, w2n_ref, w_ref
-    )
-    pre = jnp.zeros((OWN, HID), F32)
-    for z in range(NZ):
-        pre = pre + dot(rows_ref[z], w_ref[z])
+    high, low, d, d_hidden = owner_grads(in_ref, send_ref, seed_ref, dout_ref, w2s_ref, w2n_ref)
+    pre = share_ref[0].astype(F32)
+    for z in range(1, NZ):
+        pre = pre + share_ref[z].astype(F32)
     slope = jnp.exp(jnp.minimum(pre, 0.0))
     hidden = jnp.where(pre > 0, pre, slope - 1.0).astype(BF)
-    d_pre = (d_hidden * slope).astype(BF)
-    for z in range(NZ):
-        g = dot(rows_ref[z], d_pre, 0, 0).astype(BF)
-        for q in range(ND):
-            r, h = q // 2, q % 2
-            at = (r // 4) * PAIR + (r % 4) * 16
-            lanes = slice(h * 128, (h + 1) * 128)
-            for side in range(2):
-                f = 2 * z + (core if side == 0 else 1 - core)
-                piece = g[at + side * COLS : at + side * COLS + 16, lanes]
-                out_ref[q, pl.ds(pl.multiple_of(G1 + f * 16, 16), 16), :] = piece
+    dpre_ref[...] = (d_hidden * slope).astype(BF)
     g2s = dot(hidden, d, 0, 0).astype(BF)
     g2n = (dot(hidden, high, 0, 0) + dot(hidden, low, 0, 0)).astype(BF)
     for q in range(ND):
@@ -179,23 +153,44 @@
     part_ref[...] = dot(dot(hot, hidden, 0, 0).astype(BF), w2s_ref[...])
 
 
+def columns_body(chip_ref, rows_ref, *refs):
+    keep_ref, give_ref = refs[NZ:]
+    chip = chip_ref[0]
+    total = jnp.zeros((2 * PAIR, HID), F32)
+    for i, offset in enumerate(RING):
+        source = jnp.bitwise_and(chip + offset, NZ - 1)
+        total = total + dot(rows_ref[source], refs[i][...], 0, 0)
+    keep_ref[0:COLS, :] = total[0:COLS]
+    keep_ref[COLS:PAIR, :] = total[PAIR : PAIR + COLS]
+    give_ref[0:COLS, :] = total[COLS:PAIR]
+    give_ref[COLS:PAIR, :] = total[PAIR + COLS :]
+
+
+def pair_sum_body(keep_ref, got_ref, out_ref):
+    total = keep_ref[...] + got_ref[...]
+    for q in range(ND):
+        r, h = q // 2, q % 2
+        out_ref[q] = total[r * 16 : r * 16 + 16, h * 128 : (h + 1) * 128]
+
+
 def first_sum_body(in_ref, out_ref):
     total = in_ref[0, G2:, :].astype(F32)
     for p in range(1, ND):
         total = total + in_ref[p, G2:, :].astype(F32)
     total = total.astype(BF)
     for f in range(NF):
-        out_ref[f, 0:16, :] = total[G1 - G2 + f * 16 : G1 - G2 + f * 16 + 16]
-        out_ref[f, 16:80, :] = total[0:64]
-
-
-def second_sum_body(in_ref, out_ref):
-    total = in_ref[0].astype(F32)
+        out_ref[f] = total
+
+
+def second_sum_body(one_ref, two_ref, out_ref):
+    one = one_ref[0]
+    two = two_ref[0].astype(F32)
     for f in range(1, NF):
-        total = total + in_ref[f].astype(F32)
-    total = total.astype(BF)
+        one = one + one_ref[f]
+        two = two + two_ref[f].astype(F32)
+    both = jnp.concatenate([one, two], axis=0).astype(BF)
     for q in range(ND):
-        out_ref[q] = total
+        out_ref[q] = both
 
 
 def place_body(in_ref, g1s_ref, g1n_ref, g2s_ref, g2n_ref):
@@ -227,6 +222,10 @@
     )
 
 
+def turn(x, step):
+    return lax.ppermute(x, "feat", [(i, (i + 2 * step) % NF) for i in range(NF)])
+
+
 def fetch(x, bit):
     return lax.ppermute(x, "feat", [(i, i ^ bit) for i in range(NF)])
 
@@ -236,16 +235,13 @@
     neigh_two, seed_rows, d_out,
 ):
     f = lax.axis_index("feat")
-    q = lax.axis_index("dom")
     core = jnp.bitwise_and(f, 1).reshape(1)
+    chip = jnp.right_shift(f, 1).reshape(1)
     chips = [[2 * z + c for z in range(NZ)] for c in range(2)]
     own = features[0]
     other = fetch(own, 1)
-
     w1 = jnp.concatenate([w1_self, w1_neigh], axis=0)
-    start = (jnp.right_shift(q, 1) * 16, jnp.bitwise_and(q, 1) * 128)
-    piece = lax.dynamic_slice(w1, start, (16, 128))
-    piece = swap(jnp.broadcast_to(piece, (NZ, 16, 128)), "feat", chips).reshape(1, NZ * 16, 128)
+    w1_other = fetch(w1, 1)
 
     send = send_rows[0, 0]
     seeds = seed_rows[0]
@@ -253,35 +249,55 @@
     counts = recv_count[:, 0, 0]
     names = neigh_two[0, 0].T
     t_out = call(
-        pick_body, "picks", shape((ND, 2 * SLOTS, 128), BF), [SMEM, VMEM, VMEM], limit=60, us=5
+        pick_body, "picks", shape((ND, SLOTS, HID), BF), [SMEM, VMEM, VMEM], limit=60, us=5
     )(counts, names, grad_out)
-    piece = jnp.broadcast_to(piece, (ND, NZ * 16, 128))
-    t_in = swap(jnp.concatenate([t_out, piece], axis=1), "dom")
-    w1_other = fetch(t_in[:, 2 * SLOTS :], 1)
-
-    rows_out = call(
+    t_in = swap(t_out, "dom")
+
+    rows = shape((NZ, OWN, 2 * PAIR), BF)
+    rows, share = call(
         rows_body,
         "node_rows",
-        shape((NZ, OWN, 2 * PAIR), BF),
-        [SMEM, VMEM, VMEM, SMEM],
+        (rows, rows),
+        [SMEM, VMEM, VMEM, SMEM, VMEM, VMEM],
         [pltpu.VMEM((NIN, PAIR), F32), pltpu.VMEM((HALF, PAIR), F32)],
         limit=60,
         us=22,
-    )(core, own, other, neigh_one.reshape(-1))
-    rows_in = swap(rows_out, "feat", chips)
-
-    to_dom, part = call(
+    )(core, own, other, neigh_one.reshape(-1), w1, w1_other)
+    share = swap(share, "feat", chips)
+
+    to_dom, part, d_pre = call(
         main_body,
         "project",
-        (shape((ND, G1 + 256, 128), BF), shape((SEEDS, HID), F32)),
-        [SMEM] + [VMEM] * 8,
-        [pltpu.VMEM((NZ, 2 * PAIR, HID), BF)],
+        (
+            shape((ND, G2 + 64, 128), BF),
+            shape((SEEDS, HID), F32),
+            shape((OWN, HID), BF),
+        ),
+        [VMEM] * 7,
         us=4,
-    )(core, rows_in, t_in, w1_other, send, seeds, grad_out, w2_self, w2_neigh)
+    )(share, t_in, send, seeds, grad_out, w2_self, w2_neigh)
+
+    ring = {0: d_pre}
+    for i in range(1, 4):
+        ring[-i] = turn(ring[1 - i], 1)
+        ring[i] = turn(ring[i - 1], -1)
+    ring[-4] = turn(ring[-3], 1)
     from_dom = swap(to_dom, "dom")
 
-    to_feat = call(first_sum_body, "sum_dom", shape((NF, 80, 128), BF), [VMEM])(from_dom)
-    from_feat = swap(to_feat, "feat")
+    keep, give = call(
+        columns_body,
+        "columns",
+        (shape((PAIR, HID), F32), shape((PAIR, HID), F32)),
+        [SMEM] + [VMEM] * (1 + NZ),
+        us=2,
+    )(chip, rows, *[ring[i] for i in RING])
+    one = call(pair_sum_body, "sum_pair", shape((ND, 16, 128), F32), [VMEM] * 2)(
+        keep, fetch(give, 1)
+    )
+
+    two = call(first_sum_body, "sum_dom", shape((NF, 64, 128), BF), [VMEM])(from_dom)
+    two = swap(two, "feat")
+    one = swap(one, "dom")
     layer_out = call(
         layer_body,
         "layer_two",
@@ -290,7 +306,9 @@
         limit=60,
         us=5,
     )(counts, names, from_dom, part, w2_neigh)
-    done = call(second_sum_body, "sum_feat", shape((ND, 80, 128), BF), [VMEM], limit=60)(from_feat)
+    done = call(
+        second_sum_body, "sum_all", shape((ND, 80, 128), BF), [VMEM] * 2, limit=60
+    )(one, two)
     done = swap(done, "dom")
     first = shape((COLS, HID), F32)
     second = shape((HID, HID), F32)

time: 171 us -> 175 us (1.023)
  starting transfers between devices: 28 us -> 41.4 us
  waiting for transfers between devices: 34 us -> 25.7 us
  other arithmetic: 3.24 us -> 0 us
    all_to_all x4, waiting for transfers between devices: 32.5 us -> 10.8 us  [swap(): lax.all_to_all(x, axis, split_axis=0, concat_axis=0, tiled=True, axis_ind...]
    ppermute x0 -> x7, waiting for transfers between devices: none -> 14 us  [turn(): lax.ppermute(x, 'feat', [(i, (i + 2 * step) % NF) for i in range(NF)])]
    ppermute x0 -> x7, starting transfers between devices: none -> 8.69 us  [turn(): lax.ppermute(x, 'feat', [(i, (i + 2 * step) % NF) for i in range(NF)])]
    ppermute x2 -> x3, starting transfers between devices: 4.57 us -> 10.2 us  [fetch(): return lax.ppermute(x, 'feat', [(i, i ^ bit) for i in range(NF)])]
    concatenate x2 -> x0, other arithmetic: 3.24 us -> none  [the longest x1 2.55 us: per_device(): t_in = swap(jnp.concatenate([t_out, piece], axis=1), 'dom')]
    pallas_call x5 -> x7, Pallas kernels: 37 us -> 38.6 us  [the longest x1 27 us: per_device(): call(rows_body, 'node_rows', (rows, rows), [SMEM, VMEM, VMEM, SMEM, VMEM,...]
    unnamed x17 -> x26, local copies, waits for them, and re-layouts: 5.2 us -> 5.13 us
  transfers between devices with their start and end apart: 6 -> 14, of which waited for: 4 -> 7; matrix products, arithmetic and copies ran while one was open for 3% -> 2% of each run, Pallas kernels for 22% -> 23%
where the time goes in v5:
time: 175 us; the launch traced here: 174 us
  blocking collectives  55.4 us (32%)
  Pallas kernels  45 us (26%)
  starting transfers between devices  41.4 us (24%)
  waiting for transfers between devices  25.7 us (15%)
  local copies, waits for them, and re-layouts  5.89 us (3%)
    all_to_all x2, blocking collectives, swap(): lax.all_to_all(x, axis, split_axis=0, concat_axis=0, tiled=True, axis_ind...  55.4 us
    pallas_call x1, Pallas kernels, per_device(): call(rows_body, 'node_rows', (rows, rows), [SMEM, VMEM, VMEM, SMEM, VMEM,...  27 us
    all_to_all x4, starting transfers between devices, swap(): lax.all_to_all(x, axis, split_axis=0, concat_axis=0, tiled=True, axis_ind...  22.6 us
    ppermute x7, waiting for transfers between devices, turn(): lax.ppermute(x, 'feat', [(i, (i + 2 * step) % NF) for i in range(NF)])  14 us
    all_to_all x4, waiting for transfers between devices, swap(): lax.all_to_all(x, axis, split_axis=0, concat_axis=0, tiled=True, axis_ind...  10.8 us
    ppermute x3, starting transfers between devices, fetch(): return lax.ppermute(x, 'feat', [(i, i ^ bit) for i in range(NF)])  10.2 us
    ppermute x7, starting transfers between devices, turn(): lax.ppermute(x, 'feat', [(i, (i + 2 * step) % NF) for i in range(NF)])  8.69 us
    pallas_call x1, Pallas kernels, per_device(): call(layer_body, 'layer_two', shape((SEEDS, HID), BF), [SMEM] + [VMEM] *...  5.58 us
  transfers between devices with their start and end apart: 14, of which 7 were waited for; matrix products, arithmetic and copies ran while one was open for 2% of the time, Pallas kernels for 23%

profile of v5, /device:TPU:1, one launch (start us, length us, event | category | flops | bytes accessed | tf_op | source)
XLA Modules:
  0.0 174.2 jit_solution(3259944026511554420)
XLA Ops:
  0.6 3.3 %collective-permute-start = (bf16[64,9216]{1,0:T(8,128)(2,1)}, bf16[64,9216]{1,0:T(8,128)(2,1)S(1)}, u32[]{:S(2)}, u32[]{:S(2)}) collective-permute-start(bf16[64,9216]{1,0:T(8,128)(2,1)} %bitcast.20), channel_id=1, source_target_pairs={{0,16},{16,0},{32,48},{48,32},{64,80},{80,64},{96,112},{112,96},{1... | collective-permute-start | bytes 3538952 | tf_op jit(solution)/shard_map/ppermute | solution.py:230
  5.5 1.3 copy.18
  6.8 5.2 %picks.1 = bf16[16,128,256]{2,1,0:T(8,128)(2,1)} custom-call(s32[16]{0:T(128)} %bitcast.23, s32[15,256]{1,0:T(8,128)} %bitcast.18, bf16[256,256]{1,0:T(8,128)(2,1)} %bitcast.14), custom_call_target="tpu_custom_call" | custom-call | flops 5000000000 | bytes 5000000 | tf_op jit(solution)/shard_map/picks/pallas_call | solution.py:251
  12.0 5.0 %all-to-all-start.1 = ((bf16[16,128,256]{2,1,0:T(8,128)(2,1)}), bf16[16,128,256]{2,1,0:T(8,128)(2,1)S(1)}, u32[]{:S(2)}, u32[]{:S(2)}) async-start(bf16[16,128,256]{2,1,0:T(8,128)(2,1)} %picks.1), calls=%async_computation.1 | async-start | bytes 2097152 | tf_op jit(solution)/shard_map/all_to_all | solution.py:220
  18.1 27.0 %node_rows.1 = (bf16[8,288,256]{2,1,0:T(8,128)(2,1)}, bf16[8,288,256]{2,1,0:T(8,128)(2,1)}) custom-call(s32[1]{0:T(128)} %bitcast.2.core_ref, bf16[64,9216]{1,0:T(8,128)(2,1)} %bitcast.21, bf16[64,9216]{1,0:T(8,128)(2,1)} %copy-done.10, s32[46080]{0:T(1024)} %bitcast.22, bf16[128,256]{1,0:T(8,128)(2,1)} %copy-done.9, bf16[128,256]{1,0:T(8,128)(2,1)} %copy-done.11), custom_call_target="tpu_custom_call" | custom-call | flops 22000001024 | bytes 22000000 | tf_op jit(solution)/shard_map/node_rows/pallas_call | solution.py:257
  45.2 38.6 %all_to_all.30.share_ref = bf16[8,288,256]{2,1,0:T(8,128)(2,1)S(1)} all-to-all(bf16[8,288,256]{2,1,0:T(8,128)(2,1)} %get-tuple-element.16), channel_id=1, replica_groups={{0,32,64,96,128,160,192,224},{16,48,80,112,144,176,208,240},{1,33,65,97..., dimensions={0} | all-to-all | bytes 2359296 | tf_op jit(solution)/shard_map/all_to_all | solution.py:220
  83.9 3.1 %project.1 = (bf16[16,320,128]{2,1,0:T(8,128)(2,1)}, f32[256,256]{1,0:T(8,128)S(1)}, bf16[288,256]{1,0:T(8,128)(2,1)S(1)}) custom-call(bf16[8,288,256]{2,1,0:T(8,128)(2,1)S(1)} %all_to_all.30.share_ref, bf16[16,128,256]{2,1,0:T(8,128)(2,1)S(1)} %all-to-all-done.1.in_ref, s32[16,128]{1,0:T(8,128)S(1)} %bitcast.16, s32[1,256]{1,0:T(1,128)S(1)} %bitcast.17, ...), custom_call_target="tpu_custom_call" | custom-call | flops 4000000000 | bytes 4000000 | tf_op jit(solution)/shard_map/project/pallas_call | solution.py:268
  87.7 6.6 %all-to-all-start.2 = ((bf16[16,320,128]{2,1,0:T(8,128)(2,1)}), bf16[16,320,128]{2,1,0:T(8,128)(2,1)S(1)}, u32[]{:S(2)}, u32[]{:S(2)}) async-start(bf16[16,320,128]{2,1,0:T(8,128)(2,1)} %get-tuple-element.17), calls=%async_computation.2 | async-start | bytes 2621440 | tf_op jit(solution)/shard_map/all_to_all | solution.py:220
  94.4 2.7 %collective-permute-start.3 = (bf16[288,256]{1,0:T(8,128)(2,1)S(1)}, bf16[288,256]{1,0:T(8,128)(2,1)S(1)}, u32[]{:S(2)}, u32[]{:S(2)}) collective-permute-start(bf16[288,256]{1,0:T(8,128)(2,1)S(1)} %get-tuple-element.20.refs_0_), channel_id=1, source_target_pairs={{0,224},{16,240},{32,0},{48,16},{64,32},{80,48},{96,64},{112,80},{... | collective-permute-start | bytes 442376 | tf_op jit(solution)/shard_map/ppermute | solution.py:226
  97.1 2.5 %collective-permute-done.2.refs_1_ = bf16[288,256]{1,0:T(8,128)(2,1)S(1)} collective-permute-done((bf16[288,256]{1,0:T(8,128)(2,1)S(1)}, bf16[288,256]{1,0:T(8,128)(2,1)S(1)}, u32[]{:S(2)}, u32[]{:S(2)}) %collective-permute-start.2) | collective-permute-done | bytes 147488 | tf_op jit(solution)/shard_map/ppermute | solution.py:226
  99.6 3.0 %collective-permute-start.5 = (bf16[288,256]{1,0:T(8,128)(2,1)S(1)}, bf16[288,256]{1,0:T(8,128)(2,1)S(1)}, u32[]{:S(2)}, u32[]{:S(2)}) collective-permute-start(bf16[288,256]{1,0:T(8,128)(2,1)S(1)} %collective-permute-done.3.refs_2_), channel_id=1, source_target_pairs={{0,224},{16,240},{32,0},{48,16},{64,32},{80,48},{96,64},{112,80},{... | collective-permute-start | bytes 442376 | tf_op jit(solution)/shard_map/ppermute | solution.py:226
  102.6 2.5 %collective-permute-done.4.refs_3_ = bf16[288,256]{1,0:T(8,128)(2,1)S(1)} collective-permute-done((bf16[288,256]{1,0:T(8,128)(2,1)S(1)}, bf16[288,256]{1,0:T(8,128)(2,1)S(1)}, u32[]{:S(2)}, u32[]{:S(2)}) %collective-permute-start.4) | collective-permute-done | bytes 147488 | tf_op jit(solution)/shard_map/ppermute | solution.py:226
  105.1 3.0 %collective-permute-start.7 = (bf16[288,256]{1,0:T(8,128)(2,1)S(1)}, bf16[288,256]{1,0:T(8,128)(2,1)S(1)}, u32[]{:S(2)}, u32[]{:S(2)}) collective-permute-start(bf16[288,256]{1,0:T(8,128)(2,1)S(1)} %collective-permute-done.5.refs_4_), channel_id=1, source_target_pairs={{0,224},{16,240},{32,0},{48,16},{64,32},{80,48},{96,64},{112,80},{... | collective-permute-start | bytes 442376 | tf_op jit(solution)/shard_map/ppermute | solution.py:226
  108.1 2.5 %collective-permute-done.6.refs_5_ = bf16[288,256]{1,0:T(8,128)(2,1)S(1)} collective-permute-done((bf16[288,256]{1,0:T(8,128)(2,1)S(1)}, bf16[288,256]{1,0:T(8,128)(2,1)S(1)}, u32[]{:S(2)}, u32[]{:S(2)}) %collective-permute-start.6) | collective-permute-done | bytes 147488 | tf_op jit(solution)/shard_map/ppermute | solution.py:226
  110.6 6.4 %collective-permute-done.8.refs_7_ = bf16[288,256]{1,0:T(8,128)(2,1)S(1)} collective-permute-done((bf16[288,256]{1,0:T(8,128)(2,1)S(1)}, bf16[288,256]{1,0:T(8,128)(2,1)S(1)}, u32[]{:S(2)}, u32[]{:S(2)}) %collective-permute-start.8) | collective-permute-done | bytes 147488 | tf_op jit(solution)/shard_map/ppermute | solution.py:226
  117.0 1.3 copy-done.6
  119.0 6.8 %collective-permute-start.9 = (f32[128,256]{1,0:T(8,128)S(1)}, f32[128,256]{1,0:T(8,128)S(1)}, u32[]{:S(2)}, u32[]{:S(2)}) collective-permute-start(f32[128,256]{1,0:T(8,128)S(1)} %get-tuple-element.22), channel_id=1, source_target_pairs={{0,16},{16,0},{32,48},{48,32},{64,80},{80,64},{96,112},{112,96},{1... | collective-permute-start | bytes 393224 | tf_op jit(solution)/shard_map/ppermute | solution.py:230
  127.5 7.4 %all-to-all-start.3 = ((f32[16,16,128]{2,1,0:T(8,128)}), f32[16,16,128]{2,1,0:T(8,128)S(1)}, u32[]{:S(2)}, u32[]{:S(2)}) async-start(f32[16,16,128]{2,1,0:T(8,128)} %sum_pair.1), calls=%async_computation.3 | async-start | bytes 262144 | tf_op jit(solution)/shard_map/all_to_all | solution.py:220
  135.0 6.6 %all-to-all-done.3.one_ref = f32[16,16,128]{2,1,0:T(8,128)S(1)} async-done(((f32[16,16,128]{2,1,0:T(8,128)}), f32[16,16,128]{2,1,0:T(8,128)S(1)}, u32[]{:S(2)}, u32[]{:S(2)}) %all-to-all-start.3) | async-done | bytes 131104 | tf_op jit(solution)/shard_map/all_to_all | solution.py:220
  141.6 16.7 %all_to_all.31.two_ref = bf16[16,64,128]{2,1,0:T(8,128)(2,1)} all-to-all(bf16[16,64,128]{2,1,0:T(8,128)(2,1)S(1)} %sum_dom.1), channel_id=1, replica_groups=mesh['feat'=16,'dom'=16] {'feat'}, dimensions={0} | all-to-all | bytes 524288 | tf_op jit(solution)/shard_map/all_to_all | solution.py:220
  158.3 1.8 %sum_all.1 = bf16[16,80,128]{2,1,0:T(8,128)(2,1)} custom-call(f32[16,16,128]{2,1,0:T(8,128)} %copy-done.8, bf16[16,64,128]{2,1,0:T(8,128)(2,1)} %all_to_all.31.two_ref), custom_call_target="tpu_custom_call" | custom-call | flops 1000000000 | bytes 1000000 | tf_op jit(solution)/shard_map/sum_all/pallas_call | solution.py:309
  160.1 3.5 %all-to-all-start.5 = ((bf16[16,80,128]{2,1,0:T(8,128)(2,1)}), bf16[16,80,128]{2,1,0:T(8,128)(2,1)S(1)}, u32[]{:S(2)}, u32[]{:S(2)}) async-start(bf16[16,80,128]{2,1,0:T(8,128)(2,1)} %sum_all.1), calls=%async_computation.5 | async-start | bytes 655360 | tf_op jit(solution)/shard_map/all_to_all | solution.py:220
  163.7 5.6 %layer_two.1 = bf16[256,256]{1,0:T(8,128)(2,1)} custom-call(s32[16]{0:T(128)} %bitcast.24, s32[15,256]{1,0:T(8,128)} %bitcast.19, bf16[16,320,128]{2,1,0:T(8,128)(2,1)} %copy-done, f32[256,256]{1,0:T(8,128)} %copy-done.7, bf16[256,256]{1,0:T(8,128)(2,1)} %w2n_ref.3), custom_call_target="tpu_custom_call" | custom-call | flops 5000000000 | bytes 5000000 | tf_op jit(solution)/shard_map/layer_two/pallas_call | solution.py:301
  169.3 4.1 %all-to-all-done.5.in_ref = bf16[16,80,128]{2,1,0:T(8,128)(2,1)S(1)} async-done(((bf16[16,80,128]{2,1,0:T(8,128)(2,1)}), bf16[16,80,128]{2,1,0:T(8,128)(2,1)S(1)}, u32[]{:S(2)}, u32[]{:S(2)}) %all-to-all-start.5) | async-done | bytes 327712 | tf_op jit(solution)/shard_map/all_to_all | solution.py:220
  (42 shorter events, 6.7 us)
Async XLA Ops:
  0.6 16.5 %collective-permute-start = (bf16[64,9216]{1,0:T(8,128)(2,1)}, bf16[64,9216]{1,0:T(8,128)(2,1)S(1)}, u32[]{:S(2)}, u32[]{:S(2)}) collective-permute-start(bf16[64,9216]{1,0:T(8,128)(2,1)} %bitcast.20), channel_id=1, source_target_pairs={{0,16},{16,0},{32,48},{48,32},{64,80},{80,64},{96,112},{112,96},{1... | collective-permute-start | bytes 3538952 | tf_op jit(solution)/shard_map/ppermute | solution.py:230
  5.5 6.6 %copy-start.9 = (bf16[128,256]{1,0:T(8,128)(2,1)}, bf16[128,256]{1,0:T(8,128)(2,1)S(1)}, u32[]{:S(2)}) copy-start(bf16[128,256]{1,0:T(8,128)(2,1)S(1)} %constant_dynamic-update-slice_fusion.w_ref) | copy-start | bytes 196612
  5.5 11.6 %collective-permute-start.1 = (bf16[128,256]{1,0:T(8,128)(2,1)S(1)}, bf16[128,256]{1,0:T(8,128)(2,1)S(1)}, u32[]{:S(2)}, u32[]{:S(2)}) collective-permute-start(bf16[128,256]{1,0:T(8,128)(2,1)S(1)} %constant_dynamic-update-slice_fusion.w_ref), channel_id=1, source_target_pairs={{0,16},{16,0},{32,48},{48,32},{64,80},{80,64},{96,112},{112,96},{1... | collective-permute-start | bytes 196616 | tf_op jit(solution)/shard_map/ppermute | solution.py:230
  12.0 33.1 %all-to-all-start.1 = ((bf16[16,128,256]{2,1,0:T(8,128)(2,1)}), bf16[16,128,256]{2,1,0:T(8,128)(2,1)S(1)}, u32[]{:S(2)}, u32[]{:S(2)}) async-start(bf16[16,128,256]{2,1,0:T(8,128)(2,1)} %picks.1), calls=%async_computation.1 | async-start | bytes 2097152 | tf_op jit(solution)/shard_map/all_to_all | solution.py:220
  17.1 1.0 copy-start.10
  45.2 38.7 %copy-start.1 = (bf16[1,1,256,256]{3,2,1,0:T(8,128)(2,1)S(1)}, bf16[1,1,256,256]{3,2,1,0:T(8,128)(2,1)}, u32[]{:S(2)}) copy-start(bf16[1,1,256,256]{3,2,1,0:T(8,128)(2,1)} %param.21) | copy-start | bytes 393220
  45.2 38.7 %copy-start.2 = (bf16[256,256]{1,0:T(8,128)(2,1)S(1)}, bf16[256,256]{1,0:T(8,128)(2,1)}, u32[]{:S(2)}) copy-start(bf16[256,256]{1,0:T(8,128)(2,1)} %w2s_ref.1) | copy-start | bytes 393220
  45.2 38.7 %copy-start.3 = (bf16[256,256]{1,0:T(8,128)(2,1)S(1)}, bf16[256,256]{1,0:T(8,128)(2,1)}, u32[]{:S(2)}) copy-start(bf16[256,256]{1,0:T(8,128)(2,1)} %w2n_ref.3) | copy-start | bytes 393220
  45.2 38.7 %copy-start.4 = (s32[1,1,16,128]{3,2,1,0:T(8,128)S(1)}, s32[1,1,16,128]{3,2,1,0:T(8,128)}, u32[]{:S(2)}) copy-start(s32[1,1,16,128]{3,2,1,0:T(8,128)} %param.17) | copy-start | bytes 24580
  45.2 38.7 %copy-start.5 = (s32[1,1,256]{2,1,0:T(1,128)S(1)}, s32[1,1,256]{2,1,0:T(1,128)}, u32[]{:S(2)}) copy-start(s32[1,1,256]{2,1,0:T(1,128)} %param.20) | copy-start | bytes 3076
  87.7 39.8 %all-to-all-start.2 = ((bf16[16,320,128]{2,1,0:T(8,128)(2,1)}), bf16[16,320,128]{2,1,0:T(8,128)(2,1)S(1)}, u32[]{:S(2)}, u32[]{:S(2)}) async-start(bf16[16,320,128]{2,1,0:T(8,128)(2,1)} %get-tuple-element.17), calls=%async_computation.2 | async-start | bytes 2621440 | tf_op jit(solution)/shard_map/all_to_all | solution.py:220
  94.3 5.3 %collective-permute-start.2 = (bf16[288,256]{1,0:T(8,128)(2,1)S(1)}, bf16[288,256]{1,0:T(8,128)(2,1)S(1)}, u32[]{:S(2)}, u32[]{:S(2)}) collective-permute-start(bf16[288,256]{1,0:T(8,128)(2,1)S(1)} %get-tuple-element.20.refs_0_), channel_id=1, source_target_pairs={{0,32},{16,48},{32,64},{48,80},{64,96},{80,112},{96,128},{112,144}... | collective-permute-start | bytes 442376 | tf_op jit(solution)/shard_map/ppermute | solution.py:226
  94.4 5.2 %collective-permute-start.3 = (bf16[288,256]{1,0:T(8,128)(2,1)S(1)}, bf16[288,256]{1,0:T(8,128)(2,1)S(1)}, u32[]{:S(2)}, u32[]{:S(2)}) collective-permute-start(bf16[288,256]{1,0:T(8,128)(2,1)S(1)} %get-tuple-element.20.refs_0_), channel_id=1, source_target_pairs={{0,224},{16,240},{32,0},{48,16},{64,32},{80,48},{96,64},{112,80},{... | collective-permute-start | bytes 442376 | tf_op jit(solution)/shard_map/ppermute | solution.py:226
  99.6 5.5 %collective-permute-start.4 = (bf16[288,256]{1,0:T(8,128)(2,1)S(1)}, bf16[288,256]{1,0:T(8,128)(2,1)S(1)}, u32[]{:S(2)}, u32[]{:S(2)}) collective-permute-start(bf16[288,256]{1,0:T(8,128)(2,1)S(1)} %collective-permute-done.2.refs_1_), channel_id=1, source_target_pairs={{0,32},{16,48},{32,64},{48,80},{64,96},{80,112},{96,128},{112,144}... | collective-permute-start | bytes 442376 | tf_op jit(solution)/shard_map/ppermute | solution.py:226
  99.6 5.5 %collective-permute-start.5 = (bf16[288,256]{1,0:T(8,128)(2,1)S(1)}, bf16[288,256]{1,0:T(8,128)(2,1)S(1)}, u32[]{:S(2)}, u32[]{:S(2)}) collective-permute-start(bf16[288,256]{1,0:T(8,128)(2,1)S(1)} %collective-permute-done.3.refs_2_), channel_id=1, source_target_pairs={{0,224},{16,240},{32,0},{48,16},{64,32},{80,48},{96,64},{112,80},{... | collective-permute-start | bytes 442376 | tf_op jit(solution)/shard_map/ppermute | solution.py:226
  105.1 5.5 %collective-permute-start.6 = (bf16[288,256]{1,0:T(8,128)(2,1)S(1)}, bf16[288,256]{1,0:T(8,128)(2,1)S(1)}, u32[]{:S(2)}, u32[]{:S(2)}) collective-permute-start(bf16[288,256]{1,0:T(8,128)(2,1)S(1)} %collective-permute-done.4.refs_3_), channel_id=1, source_target_pairs={{0,32},{16,48},{32,64},{48,80},{64,96},{80,112},{96,128},{112,144}... | collective-permute-start | bytes 442376 | tf_op jit(solution)/shard_map/ppermute | solution.py:226
  105.1 5.5 %collective-permute-start.7 = (bf16[288,256]{1,0:T(8,128)(2,1)S(1)}, bf16[288,256]{1,0:T(8,128)(2,1)S(1)}, u32[]{:S(2)}, u32[]{:S(2)}) collective-permute-start(bf16[288,256]{1,0:T(8,128)(2,1)S(1)} %collective-permute-done.5.refs_4_), channel_id=1, source_target_pairs={{0,224},{16,240},{32,0},{48,16},{64,32},{80,48},{96,64},{112,80},{... | collective-permute-start | bytes 442376 | tf_op jit(solution)/shard_map/ppermute | solution.py:226
  110.6 6.4 %collective-permute-start.8 = (bf16[288,256]{1,0:T(8,128)(2,1)S(1)}, bf16[288,256]{1,0:T(8,128)(2,1)S(1)}, u32[]{:S(2)}, u32[]{:S(2)}) collective-permute-start(bf16[288,256]{1,0:T(8,128)(2,1)S(1)} %collective-permute-done.6.refs_5_), channel_id=1, source_target_pairs={{0,32},{16,48},{32,64},{48,80},{64,96},{80,112},{96,128},{112,144}... | collective-permute-start | bytes 442376 | tf_op jit(solution)/shard_map/ppermute | solution.py:226
  117.0 1.3 copy-start.6
  119.0 7.8 %collective-permute-start.9 = (f32[128,256]{1,0:T(8,128)S(1)}, f32[128,256]{1,0:T(8,128)S(1)}, u32[]{:S(2)}, u32[]{:S(2)}) collective-permute-start(f32[128,256]{1,0:T(8,128)S(1)} %get-tuple-element.22), channel_id=1, source_target_pairs={{0,16},{16,0},{32,48},{48,32},{64,80},{80,64},{96,112},{112,96},{1... | collective-permute-start | bytes 393224 | tf_op jit(solution)/shard_map/ppermute | solution.py:230
  127.5 7.4 %copy-start = (bf16[16,320,128]{2,1,0:T(8,128)(2,1)}, bf16[16,320,128]{2,1,0:T(8,128)(2,1)S(1)}, u32[]{:S(2)}) copy-start(bf16[16,320,128]{2,1,0:T(8,128)(2,1)S(1)} %all-to-all-done.2.in_ref) | copy-start | bytes 3932164
  127.5 14.1 %all-to-all-start.3 = ((f32[16,16,128]{2,1,0:T(8,128)}), f32[16,16,128]{2,1,0:T(8,128)S(1)}, u32[]{:S(2)}, u32[]{:S(2)}) async-start(f32[16,16,128]{2,1,0:T(8,128)} %sum_pair.1), calls=%async_computation.3 | async-start | bytes 262144 | tf_op jit(solution)/shard_map/all_to_all | solution.py:220
  141.6 16.7 %copy-start.8 = (f32[16,16,128]{2,1,0:T(8,128)}, f32[16,16,128]{2,1,0:T(8,128)S(1)}, u32[]{:S(2)}) copy-start(f32[16,16,128]{2,1,0:T(8,128)S(1)} %all-to-all-done.3.one_ref) | copy-start | bytes 393220
  160.1 13.3 %all-to-all-start.5 = ((bf16[16,80,128]{2,1,0:T(8,128)(2,1)}), bf16[16,80,128]{2,1,0:T(8,128)(2,1)S(1)}, u32[]{:S(2)}, u32[]{:S(2)}) async-start(bf16[16,80,128]{2,1,0:T(8,128)(2,1)} %sum_all.1), calls=%async_computation.5 | async-start | bytes 655360 | tf_op jit(solution)/shard_map/all_to_all | solution.py:220
  (2 other events, 1.3 us)

commit v6 on v5

--- a/solution.py
+++ b/solution.py
@@ -70,7 +70,8 @@
 
 
 def rows_body(
-    core_ref, own_ref, other_ref, index_ref, w_ref, wo_ref, out_ref, part_ref, table, sums
+    core_ref, own_ref, other_ref, index_ref, ws_ref, wn_ref, wso_ref, wno_ref,
+    out_ref, part_ref, table, sums,
 ):
     core = core_ref[0]
     step = 512
@@ -93,8 +94,7 @@
         return carry
 
     lax.fori_loop(0, HALF // UNROLL, block, 0)
-    a, b = w_ref[...], wo_ref[...]
-    w = jnp.concatenate([a[:COLS], b[:COLS], a[COLS:], b[COLS:]], axis=0)
+    w = jnp.concatenate([ws_ref[...], wso_ref[...], wn_ref[...], wno_ref[...]], axis=0)
     for z in range(NZ):
         mean = sums[z * OWN : (z + 1) * OWN, :] * (1.0 / K1)
         out_ref[z, :, PAIR : 2 * PAIR] = mean.astype(BF)
@@ -166,13 +166,6 @@
     give_ref[COLS:PAIR, :] = total[PAIR + COLS :]
 
 
-def pair_sum_body(keep_ref, got_ref, out_ref):
-    total = keep_ref[...] + got_ref[...]
-    for q in range(ND):
-        r, h = q // 2, q % 2
-        out_ref[q] = total[r * 16 : r * 16 + 16, h * 128 : (h + 1) * 128]
-
-
 def first_sum_body(in_ref, out_ref):
     total = in_ref[0, G2:, :].astype(F32)
     for p in range(1, ND):
@@ -182,26 +175,30 @@
         out_ref[f] = total
 
 
-def second_sum_body(one_ref, two_ref, out_ref):
-    one = one_ref[0]
+def second_sum_body(keep_ref, got_ref, two_ref, out_ref):
+    one = (keep_ref[...] + got_ref[...]).astype(BF)
     two = two_ref[0].astype(F32)
     for f in range(1, NF):
-        one = one + one_ref[f]
         two = two + two_ref[f].astype(F32)
-    both = jnp.concatenate([one, two], axis=0).astype(BF)
+    two = two.astype(BF)
     for q in range(ND):
-        out_ref[q] = both
+        out_ref[q, 0:PAIR, :] = one[:, 0:128]
+        out_ref[q, PAIR : 2 * PAIR, :] = one[:, 128:256]
+        out_ref[q, 2 * PAIR :, :] = two
 
 
 def place_body(in_ref, g1s_ref, g1n_ref, g2s_ref, g2n_ref):
-    for q in range(ND):
-        r, h = q // 2, q % 2
-        g1 = g1s_ref if r < 4 else g1n_ref
-        g1[(r % 4) * 16 : (r % 4) * 16 + 16, h * 128 : (h + 1) * 128] = in_ref[q, 0:16, :].astype(F32)
-        g2 = g2s_ref if q < 8 else g2n_ref
-        for half in range(2):
-            piece = in_ref[q, 16 + half * 32 : 48 + half * 32, :].astype(F32)
-            g2[(q % 8) * 32 : (q % 8) * 32 + 32, half * 128 : (half + 1) * 128] = piece
+    one = in_ref[0, 0 : 2 * PAIR, :].astype(F32)
+    for q in range(1, ND):
+        one = one + in_ref[q, 0 : 2 * PAIR, :].astype(F32)
+    for h in range(2):
+        lanes = slice(h * 128, (h + 1) * 128)
+        g1s_ref[:, lanes] = one[h * PAIR : h * PAIR + COLS]
+        g1n_ref[:, lanes] = one[h * PAIR + COLS : (h + 1) * PAIR]
+        for q in range(ND):
+            g2 = g2s_ref if q < 8 else g2n_ref
+            at = 2 * PAIR + h * 32
+            g2[(q % 8) * 32 : (q % 8) * 32 + 32, lanes] = in_ref[q, at : at + 32, :].astype(F32)
 
 
 def layer_body(count_ref, neigh_ref, in_ref, part_ref, w2n_ref, layer_ref):
@@ -240,8 +237,8 @@
     chips = [[2 * z + c for z in range(NZ)] for c in range(2)]
     own = features[0]
     other = fetch(own, 1)
-    w1 = jnp.concatenate([w1_self, w1_neigh], axis=0)
-    w1_other = fetch(w1, 1)
+    ws_other = fetch(w1_self, 1)
+    wn_other = fetch(w1_neigh, 1)
 
     send = send_rows[0, 0]
     seeds = seed_rows[0]
@@ -258,11 +255,11 @@
         rows_body,
         "node_rows",
         (rows, rows),
-        [SMEM, VMEM, VMEM, SMEM, VMEM, VMEM],
+        [SMEM, VMEM, VMEM, SMEM] + [VMEM] * 4,
         [pltpu.VMEM((NIN, PAIR), F32), pltpu.VMEM((HALF, PAIR), F32)],
         limit=60,
         us=22,
-    )(core, own, other, neigh_one.reshape(-1), w1, w1_other)
+    )(core, own, other, neigh_one.reshape(-1), w1_self, w1_neigh, ws_other, wn_other)
     share = swap(share, "feat", chips)
 
     to_dom, part, d_pre = call(
@@ -284,6 +281,9 @@
     ring[-4] = turn(ring[-3], 1)
     from_dom = swap(to_dom, "dom")
 
+    two = call(first_sum_body, "sum_dom", shape((NF, 64, 128), BF), [VMEM])(from_dom)
+    two, ring[-4] = lax.optimization_barrier((two, ring[-4]))
+    two = swap(two, "feat")
     keep, give = call(
         columns_body,
         "columns",
@@ -291,13 +291,7 @@
         [SMEM] + [VMEM] * (1 + NZ),
         us=2,
     )(chip, rows, *[ring[i] for i in RING])
-    one = call(pair_sum_body, "sum_pair", shape((ND, 16, 128), F32), [VMEM] * 2)(
-        keep, fetch(give, 1)
-    )
-
-    two = call(first_sum_body, "sum_dom", shape((NF, 64, 128), BF), [VMEM])(from_dom)
-    two = swap(two, "feat")
-    one = swap(one, "dom")
+    got = fetch(give, 1)
     layer_out = call(
         layer_body,
         "layer_two",
@@ -307,8 +301,8 @@
         us=5,
     )(counts, names, from_dom, part, w2_neigh)
     done = call(
-        second_sum_body, "sum_all", shape((ND, 80, 128), BF), [VMEM] * 2, limit=60
-    )(one, two)
+        second_sum_body, "sum_feat", shape((ND, 2 * PAIR + 64, 128), BF), [VMEM] * 3, limit=60
+    )(keep, got, two)
     done = swap(done, "dom")
     first = shape((COLS, HID), F32)
     second = shape((HID, HID), F32)

time: 175 us -> 172 us (0.983)
  blocking collectives: 55.4 us -> 39.1 us
  waiting for transfers between devices: 25.7 us -> 37.9 us
    all_to_all x2 -> x1, blocking collectives: 55.4 us -> 39.1 us  [swap(): lax.all_to_all(x, axis, split_axis=0, concat_axis=0, tiled=True, axis_ind...]
    ppermute x7, waiting for transfers between devices: 14 us -> 24.1 us  [turn(): lax.ppermute(x, 'feat', [(i, (i + 2 * step) % NF) for i in range(NF)])]
    all_to_all x4, starting transfers between devices: 22.6 us -> 28.6 us  [swap(): lax.all_to_all(x, axis, split_axis=0, concat_axis=0, tiled=True, axis_ind...]
    ppermute x3 -> x4, starting transfers between devices: 10.2 us -> 4.71 us  [fetch(): return lax.ppermute(x, 'feat', [(i, i ^ bit) for i in range(NF)])]
    all_to_all x4, waiting for transfers between devices: 10.8 us -> 12.8 us  [swap(): lax.all_to_all(x, axis, split_axis=0, concat_axis=0, tiled=True, axis_ind...]
    unnamed x26 -> x29, local copies, waits for them, and re-layouts: 5.13 us -> 4.79 us
    pallas_call x3 -> x2, Pallas kernels: 29.5 us -> 29.3 us  [the longest x1 27 us: per_device(): call(rows_body, 'node_rows', (rows, rows), [SMEM, VMEM, VMEM, SMEM] + [VM...]
  transfers between devices with their start and end apart: 14 -> 15, of which waited for: 7 -> 7; matrix products, arithmetic and copies ran while one was open for 2% -> 1% of each run, Pallas kernels for 23% -> 23%
where the time goes in v6:
time: 172 us; the launch traced here: 170 us
  Pallas kernels  45.8 us (27%)
  starting transfers between devices  41.5 us (24%)
  blocking collectives  39.1 us (23%)
  waiting for transfers between devices  37.9 us (22%)
  local copies, waits for them, and re-layouts  4.79 us (3%)
    all_to_all x1, blocking collectives, swap(): lax.all_to_all(x, axis, split_axis=0, concat_axis=0, tiled=True, axis_ind...  39.1 us
    all_to_all x4, starting transfers between devices, swap(): lax.all_to_all(x, axis, split_axis=0, concat_axis=0, tiled=True, axis_ind...  28.6 us
    pallas_call x1, Pallas kernels, per_device(): call(rows_body, 'node_rows', (rows, rows), [SMEM, VMEM, VMEM, SMEM] + [VM...  27 us
    ppermute x7, waiting for transfers between devices, turn(): lax.ppermute(x, 'feat', [(i, (i + 2 * step) % NF) for i in range(NF)])  24.1 us
    all_to_all x4, waiting for transfers between devices, swap(): lax.all_to_all(x, axis, split_axis=0, concat_axis=0, tiled=True, axis_ind...  12.8 us
    ppermute x7, starting transfers between devices, turn(): lax.ppermute(x, 'feat', [(i, (i + 2 * step) % NF) for i in range(NF)])  8.2 us
    pallas_call x1, Pallas kernels, per_device(): call(layer_body, 'layer_two', shape((SEEDS, HID), BF), [SMEM] + [VMEM] *...  5.58 us
    pallas_call x1, Pallas kernels, per_device(): call(pick_body, 'picks', shape((ND, SLOTS, HID), BF), [SMEM, VMEM, VMEM],...  5.22 us
  transfers between devices with their start and end apart: 15, of which 7 were waited for; matrix products, arithmetic and copies ran while one was open for 1% of the time, Pallas kernels for 23%

profile of v6, /device:TPU:1, one launch (start us, length us, event | category | flops | bytes accessed | tf_op | source)
XLA Modules:
  0.0 169.9 jit_solution(6091833962400278211)
XLA Ops:
  0.6 3.3 %collective-permute-start = (bf16[64,9216]{1,0:T(8,128)(2,1)}, bf16[64,9216]{1,0:T(8,128)(2,1)S(1)}, u32[]{:S(2)}, u32[]{:S(2)}) collective-permute-start(bf16[64,9216]{1,0:T(8,128)(2,1)} %bitcast.20), channel_id=1, source_target_pairs={{0,16},{16,0},{32,48},{48,32},{64,80},{80,64},{96,112},{112,96},{1... | collective-permute-start | bytes 3538952 | tf_op jit(solution)/shard_map/ppermute | solution.py:227
  4.5 1.3 copy.18
  5.8 5.2 %picks.1 = bf16[16,128,256]{2,1,0:T(8,128)(2,1)} custom-call(s32[16]{0:T(128)} %bitcast.23, s32[15,256]{1,0:T(8,128)} %bitcast.18, bf16[256,256]{1,0:T(8,128)(2,1)} %bitcast.14), custom_call_target="tpu_custom_call" | custom-call | flops 5000000000 | bytes 5000000 | tf_op jit(solution)/shard_map/picks/pallas_call | solution.py:248
  11.0 5.0 %all-to-all-start.1 = ((bf16[16,128,256]{2,1,0:T(8,128)(2,1)}), bf16[16,128,256]{2,1,0:T(8,128)(2,1)S(1)}, u32[]{:S(2)}, u32[]{:S(2)}) async-start(bf16[16,128,256]{2,1,0:T(8,128)(2,1)} %picks.1), calls=%async_computation.1 | async-start | bytes 2097152 | tf_op jit(solution)/shard_map/all_to_all | solution.py:217
  17.1 27.0 %node_rows.1 = (bf16[8,288,256]{2,1,0:T(8,128)(2,1)}, bf16[8,288,256]{2,1,0:T(8,128)(2,1)}) custom-call(s32[1]{0:T(128)} %bitcast.2.core_ref, bf16[64,9216]{1,0:T(8,128)(2,1)} %bitcast.21, bf16[64,9216]{1,0:T(8,128)(2,1)} %copy-done.10, s32[46080]{0:T(1024)} %bitcast.22, bf16[64,256]{1,0:T(8,128)(2,1)} %ws_ref.1, bf16[64,256]{1,0:T(8,128)(2,1)} %wn_ref.1, ...), custom_call_target="tpu_custom_call" | custom-call | flops 22000001024 | bytes 22000000 | tf_op jit(solution)/shard_map/node_rows/pallas_call | solution.py:254
  44.2 39.1 %all_to_all.25.share_ref = bf16[8,288,256]{2,1,0:T(8,128)(2,1)S(1)} all-to-all(bf16[8,288,256]{2,1,0:T(8,128)(2,1)} %get-tuple-element.18), channel_id=1, replica_groups={{0,32,64,96,128,160,192,224},{16,48,80,112,144,176,208,240},{1,33,65,97..., dimensions={0} | all-to-all | bytes 2359296 | tf_op jit(solution)/shard_map/all_to_all | solution.py:217
  83.3 3.1 %project.1 = (bf16[16,320,128]{2,1,0:T(8,128)(2,1)}, f32[256,256]{1,0:T(8,128)S(1)}, bf16[288,256]{1,0:T(8,128)(2,1)S(1)}) custom-call(bf16[8,288,256]{2,1,0:T(8,128)(2,1)S(1)} %all_to_all.25.share_ref, bf16[16,128,256]{2,1,0:T(8,128)(2,1)S(1)} %all-to-all-done.1.in_ref, s32[16,128]{1,0:T(8,128)S(1)} %bitcast.16, s32[1,256]{1,0:T(1,128)S(1)} %bitcast.17, ...), custom_call_target="tpu_custom_call" | custom-call | flops 4000000000 | bytes 4000000 | tf_op jit(solution)/shard_map/project/pallas_call | solution.py:265
  87.2 6.3 %all-to-all-start.2 = ((bf16[16,320,128]{2,1,0:T(8,128)(2,1)}), bf16[16,320,128]{2,1,0:T(8,128)(2,1)S(1)}, u32[]{:S(2)}, u32[]{:S(2)}) async-start(bf16[16,320,128]{2,1,0:T(8,128)(2,1)} %get-tuple-element.19), calls=%async_computation.2 | async-start | bytes 2621440 | tf_op jit(solution)/shard_map/all_to_all | solution.py:217
  93.6 5.2 %collective-permute-done.3.refs_1_ = bf16[288,256]{1,0:T(8,128)(2,1)S(1)} collective-permute-done((bf16[288,256]{1,0:T(8,128)(2,1)S(1)}, bf16[288,256]{1,0:T(8,128)(2,1)S(1)}, u32[]{:S(2)}, u32[]{:S(2)}) %collective-permute-start.3) | collective-permute-done | bytes 147488 | tf_op jit(solution)/shard_map/ppermute | solution.py:223
  98.8 5.5 %collective-permute-done.5.refs_3_ = bf16[288,256]{1,0:T(8,128)(2,1)S(1)} collective-permute-done((bf16[288,256]{1,0:T(8,128)(2,1)S(1)}, bf16[288,256]{1,0:T(8,128)(2,1)S(1)}, u32[]{:S(2)}, u32[]{:S(2)}) %collective-permute-start.5) | collective-permute-done | bytes 147488 | tf_op jit(solution)/shard_map/ppermute | solution.py:223
  104.3 2.7 %collective-permute-start.4 = (bf16[288,256]{1,0:T(8,128)(2,1)S(1)}, bf16[288,256]{1,0:T(8,128)(2,1)S(1)}, u32[]{:S(2)}, u32[]{:S(2)}) collective-permute-start(bf16[288,256]{1,0:T(8,128)(2,1)S(1)} %get-tuple-element.22.refs_0_), channel_id=1, source_target_pairs={{0,224},{16,240},{32,0},{48,16},{64,32},{80,48},{96,64},{112,80},{... | collective-permute-start | bytes 442376 | tf_op jit(solution)/shard_map/ppermute | solution.py:223
  107.0 2.8 %collective-permute-done.7.refs_5_ = bf16[288,256]{1,0:T(8,128)(2,1)S(1)} collective-permute-done((bf16[288,256]{1,0:T(8,128)(2,1)S(1)}, bf16[288,256]{1,0:T(8,128)(2,1)S(1)}, u32[]{:S(2)}, u32[]{:S(2)}) %collective-permute-start.7) | collective-permute-done | bytes 147488 | tf_op jit(solution)/shard_map/ppermute | solution.py:223
  109.7 2.7 %collective-permute-start.6 = (bf16[288,256]{1,0:T(8,128)(2,1)S(1)}, bf16[288,256]{1,0:T(8,128)(2,1)S(1)}, u32[]{:S(2)}, u32[]{:S(2)}) collective-permute-start(bf16[288,256]{1,0:T(8,128)(2,1)S(1)} %collective-permute-done.4.refs_2_), channel_id=1, source_target_pairs={{0,224},{16,240},{32,0},{48,16},{64,32},{80,48},{96,64},{112,80},{... | collective-permute-start | bytes 442376 | tf_op jit(solution)/shard_map/ppermute | solution.py:223
  113.6 2.3 %collective-permute-done.9.refs_7_ = bf16[288,256]{1,0:T(8,128)(2,1)S(1)} collective-permute-done((bf16[288,256]{1,0:T(8,128)(2,1)S(1)}, bf16[288,256]{1,0:T(8,128)(2,1)S(1)}, u32[]{:S(2)}, u32[]{:S(2)}) %collective-permute-start.9) | collective-permute-done | bytes 147488 | tf_op jit(solution)/shard_map/ppermute | solution.py:223
  115.9 9.7 %all-to-all-start.3 = ((bf16[16,64,128]{2,1,0:T(8,128)(2,1)}), bf16[16,64,128]{2,1,0:T(8,128)(2,1)S(1)}, u32[]{:S(2)}, u32[]{:S(2)}) async-start(bf16[16,64,128]{2,1,0:T(8,128)(2,1)} %sum_dom.1), calls=%async_computation.3 | async-start | bytes 524288 | tf_op jit(solution)/shard_map/all_to_all | solution.py:217
  125.6 2.8 %collective-permute-start.8 = (bf16[288,256]{1,0:T(8,128)(2,1)S(1)}, bf16[288,256]{1,0:T(8,128)(2,1)S(1)}, u32[]{:S(2)}, u32[]{:S(2)}) collective-permute-start(bf16[288,256]{1,0:T(8,128)(2,1)S(1)} %collective-permute-done.6.refs_4_), channel_id=1, source_target_pairs={{0,224},{16,240},{32,0},{48,16},{64,32},{80,48},{96,64},{112,80},{... | collective-permute-start | bytes 442376 | tf_op jit(solution)/shard_map/ppermute | solution.py:223
  128.4 8.4 %collective-permute-done.8.refs_6_ = bf16[288,256]{1,0:T(8,128)(2,1)S(1)} collective-permute-done((bf16[288,256]{1,0:T(8,128)(2,1)S(1)}, bf16[288,256]{1,0:T(8,128)(2,1)S(1)}, u32[]{:S(2)}, u32[]{:S(2)}) %collective-permute-start.8) | collective-permute-done | bytes 147488 | tf_op jit(solution)/shard_map/ppermute | solution.py:223
  138.2 0.9 collective-permute-start.10
  139.0 1.0 collective-permute-done.10.got_ref
  140.8 2.3 %sum_feat.1 = bf16[16,320,128]{2,1,0:T(8,128)(2,1)} custom-call(f32[128,256]{1,0:T(8,128)} %copy-done.7, f32[128,256]{1,0:T(8,128)} %copy-done.11, bf16[16,64,128]{2,1,0:T(8,128)(2,1)} %copy-done.9), custom_call_target="tpu_custom_call" | custom-call | flops 1000000000 | bytes 1000000 | tf_op jit(solution)/shard_map/sum_feat/pallas_call | solution.py:303
  143.1 7.5 %all-to-all-start.4 = ((bf16[16,320,128]{2,1,0:T(8,128)(2,1)}), bf16[16,320,128]{2,1,0:T(8,128)(2,1)S(1)}, u32[]{:S(2)}, u32[]{:S(2)}) async-start(bf16[16,320,128]{2,1,0:T(8,128)(2,1)} %sum_feat.1), calls=%async_computation.4 | async-start | bytes 2621440 | tf_op jit(solution)/shard_map/all_to_all | solution.py:217
  150.6 5.6 %layer_two.1 = bf16[256,256]{1,0:T(8,128)(2,1)} custom-call(s32[16]{0:T(128)} %bitcast.24, s32[15,256]{1,0:T(8,128)} %bitcast.19, bf16[16,320,128]{2,1,0:T(8,128)(2,1)} %copy-done, f32[256,256]{1,0:T(8,128)} %copy-done.8, bf16[256,256]{1,0:T(8,128)(2,1)} %w2n_ref.3), custom_call_target="tpu_custom_call" | custom-call | flops 5000000000 | bytes 5000000 | tf_op jit(solution)/shard_map/layer_two/pallas_call | solution.py:295
  156.2 12.7 %all-to-all-done.4.in_ref = bf16[16,320,128]{2,1,0:T(8,128)(2,1)S(1)} async-done(((bf16[16,320,128]{2,1,0:T(8,128)(2,1)}), bf16[16,320,128]{2,1,0:T(8,128)(2,1)S(1)}, u32[]{:S(2)}, u32[]{:S(2)}) %all-to-all-start.4) | async-done | bytes 1310752 | tf_op jit(solution)/shard_map/all_to_all | solution.py:217
  168.9 1.0 place.1
  (44 shorter events, 5.7 us)
Async XLA Ops:
  0.6 15.5 %collective-permute-start = (bf16[64,9216]{1,0:T(8,128)(2,1)}, bf16[64,9216]{1,0:T(8,128)(2,1)S(1)}, u32[]{:S(2)}, u32[]{:S(2)}) collective-permute-start(bf16[64,9216]{1,0:T(8,128)(2,1)} %bitcast.20), channel_id=1, source_target_pairs={{0,16},{16,0},{32,48},{48,32},{64,80},{80,64},{96,112},{112,96},{1... | collective-permute-start | bytes 3538952 | tf_op jit(solution)/shard_map/ppermute | solution.py:227
  4.0 12.1 %collective-permute-start.1 = (bf16[64,256]{1,0:T(8,128)(2,1)}, bf16[64,256]{1,0:T(8,128)(2,1)S(1)}, u32[]{:S(2)}, u32[]{:S(2)}) collective-permute-start(bf16[64,256]{1,0:T(8,128)(2,1)} %ws_ref.1), channel_id=1, source_target_pairs={{0,16},{16,0},{32,48},{48,32},{64,80},{80,64},{96,112},{112,96},{1... | collective-permute-start | bytes 98312 | tf_op jit(solution)/shard_map/ppermute | solution.py:227
  4.1 12.0 %collective-permute-start.2 = (bf16[64,256]{1,0:T(8,128)(2,1)}, bf16[64,256]{1,0:T(8,128)(2,1)S(1)}, u32[]{:S(2)}, u32[]{:S(2)}) collective-permute-start(bf16[64,256]{1,0:T(8,128)(2,1)} %wn_ref.1), channel_id=1, source_target_pairs={{0,16},{16,0},{32,48},{48,32},{64,80},{80,64},{96,112},{112,96},{1... | collective-permute-start | bytes 98312 | tf_op jit(solution)/shard_map/ppermute | solution.py:227
  11.0 33.1 %all-to-all-start.1 = ((bf16[16,128,256]{2,1,0:T(8,128)(2,1)}), bf16[16,128,256]{2,1,0:T(8,128)(2,1)S(1)}, u32[]{:S(2)}, u32[]{:S(2)}) async-start(bf16[16,128,256]{2,1,0:T(8,128)(2,1)} %picks.1), calls=%async_computation.1 | async-start | bytes 2097152 | tf_op jit(solution)/shard_map/all_to_all | solution.py:217
  16.1 1.0 copy-start.10
  44.1 39.2 %copy-start.1 = (bf16[1,1,256,256]{3,2,1,0:T(8,128)(2,1)S(1)}, bf16[1,1,256,256]{3,2,1,0:T(8,128)(2,1)}, u32[]{:S(2)}) copy-start(bf16[1,1,256,256]{3,2,1,0:T(8,128)(2,1)} %param.21) | copy-start | bytes 393220
  44.1 39.2 %copy-start.2 = (bf16[256,256]{1,0:T(8,128)(2,1)S(1)}, bf16[256,256]{1,0:T(8,128)(2,1)}, u32[]{:S(2)}) copy-start(bf16[256,256]{1,0:T(8,128)(2,1)} %w2s_ref.1) | copy-start | bytes 393220
  44.1 39.2 %copy-start.3 = (bf16[256,256]{1,0:T(8,128)(2,1)S(1)}, bf16[256,256]{1,0:T(8,128)(2,1)}, u32[]{:S(2)}) copy-start(bf16[256,256]{1,0:T(8,128)(2,1)} %w2n_ref.3) | copy-start | bytes 393220
  44.2 39.1 %copy-start.4 = (s32[1,1,16,128]{3,2,1,0:T(8,128)S(1)}, s32[1,1,16,128]{3,2,1,0:T(8,128)}, u32[]{:S(2)}) copy-start(s32[1,1,16,128]{3,2,1,0:T(8,128)} %param.17) | copy-start | bytes 24580
  44.2 39.1 %copy-start.5 = (s32[1,1,256]{2,1,0:T(1,128)S(1)}, s32[1,1,256]{2,1,0:T(1,128)}, u32[]{:S(2)}) copy-start(s32[1,1,256]{2,1,0:T(1,128)} %param.20) | copy-start | bytes 3076
  87.2 25.2 %all-to-all-start.2 = ((bf16[16,320,128]{2,1,0:T(8,128)(2,1)}), bf16[16,320,128]{2,1,0:T(8,128)(2,1)S(1)}, u32[]{:S(2)}, u32[]{:S(2)}) async-start(bf16[16,320,128]{2,1,0:T(8,128)(2,1)} %get-tuple-element.19), calls=%async_computation.2 | async-start | bytes 2621440 | tf_op jit(solution)/shard_map/all_to_all | solution.py:217
  93.5 43.3 %copy-start.6 = (bf16[8,288,256]{2,1,0:T(8,128)(2,1)S(1)}, bf16[8,288,256]{2,1,0:T(8,128)(2,1)}, u32[]{:S(2)}) copy-start(bf16[8,288,256]{2,1,0:T(8,128)(2,1)} %get-tuple-element.21.rows_ref) | copy-start | bytes 3538948
  93.5 5.3 %collective-permute-start.3 = (bf16[288,256]{1,0:T(8,128)(2,1)S(1)}, bf16[288,256]{1,0:T(8,128)(2,1)S(1)}, u32[]{:S(2)}, u32[]{:S(2)}) collective-permute-start(bf16[288,256]{1,0:T(8,128)(2,1)S(1)} %get-tuple-element.22.refs_0_), channel_id=1, source_target_pairs={{0,32},{16,48},{32,64},{48,80},{64,96},{80,112},{96,128},{112,144}... | collective-permute-start | bytes 442376 | tf_op jit(solution)/shard_map/ppermute | solution.py:223
  98.8 5.5 %collective-permute-start.5 = (bf16[288,256]{1,0:T(8,128)(2,1)S(1)}, bf16[288,256]{1,0:T(8,128)(2,1)S(1)}, u32[]{:S(2)}, u32[]{:S(2)}) collective-permute-start(bf16[288,256]{1,0:T(8,128)(2,1)S(1)} %collective-permute-done.3.refs_1_), channel_id=1, source_target_pairs={{0,32},{16,48},{32,64},{48,80},{64,96},{80,112},{96,128},{112,144}... | collective-permute-start | bytes 442376 | tf_op jit(solution)/shard_map/ppermute | solution.py:223
  104.3 5.5 %collective-permute-start.7 = (bf16[288,256]{1,0:T(8,128)(2,1)S(1)}, bf16[288,256]{1,0:T(8,128)(2,1)S(1)}, u32[]{:S(2)}, u32[]{:S(2)}) collective-permute-start(bf16[288,256]{1,0:T(8,128)(2,1)S(1)} %collective-permute-done.5.refs_3_), channel_id=1, source_target_pairs={{0,32},{16,48},{32,64},{48,80},{64,96},{80,112},{96,128},{112,144}... | collective-permute-start | bytes 442376 | tf_op jit(solution)/shard_map/ppermute | solution.py:223
  104.3 5.5 %collective-permute-start.4 = (bf16[288,256]{1,0:T(8,128)(2,1)S(1)}, bf16[288,256]{1,0:T(8,128)(2,1)S(1)}, u32[]{:S(2)}, u32[]{:S(2)}) collective-permute-start(bf16[288,256]{1,0:T(8,128)(2,1)S(1)} %get-tuple-element.22.refs_0_), channel_id=1, source_target_pairs={{0,224},{16,240},{32,0},{48,16},{64,32},{80,48},{96,64},{112,80},{... | collective-permute-start | bytes 442376 | tf_op jit(solution)/shard_map/ppermute | solution.py:223
  109.7 6.1 %collective-permute-start.9 = (bf16[288,256]{1,0:T(8,128)(2,1)S(1)}, bf16[288,256]{1,0:T(8,128)(2,1)S(1)}, u32[]{:S(2)}, u32[]{:S(2)}) collective-permute-start(bf16[288,256]{1,0:T(8,128)(2,1)S(1)} %collective-permute-done.7.refs_5_), channel_id=1, source_target_pairs={{0,32},{16,48},{32,64},{48,80},{64,96},{80,112},{96,128},{112,144}... | collective-permute-start | bytes 442376 | tf_op jit(solution)/shard_map/ppermute | solution.py:223
  109.7 15.9 %collective-permute-start.6 = (bf16[288,256]{1,0:T(8,128)(2,1)S(1)}, bf16[288,256]{1,0:T(8,128)(2,1)S(1)}, u32[]{:S(2)}, u32[]{:S(2)}) collective-permute-start(bf16[288,256]{1,0:T(8,128)(2,1)S(1)} %collective-permute-done.4.refs_2_), channel_id=1, source_target_pairs={{0,224},{16,240},{32,0},{48,16},{64,32},{80,48},{96,64},{112,80},{... | collective-permute-start | bytes 442376 | tf_op jit(solution)/shard_map/ppermute | solution.py:223
  112.4 1.2 copy-start
  115.9 24.2 %all-to-all-start.3 = ((bf16[16,64,128]{2,1,0:T(8,128)(2,1)}), bf16[16,64,128]{2,1,0:T(8,128)(2,1)S(1)}, u32[]{:S(2)}, u32[]{:S(2)}) async-start(bf16[16,64,128]{2,1,0:T(8,128)(2,1)} %sum_dom.1), calls=%async_computation.3 | async-start | bytes 524288 | tf_op jit(solution)/shard_map/all_to_all | solution.py:217
  125.6 11.1 %collective-permute-start.8 = (bf16[288,256]{1,0:T(8,128)(2,1)S(1)}, bf16[288,256]{1,0:T(8,128)(2,1)S(1)}, u32[]{:S(2)}, u32[]{:S(2)}) collective-permute-start(bf16[288,256]{1,0:T(8,128)(2,1)S(1)} %collective-permute-done.6.refs_4_), channel_id=1, source_target_pairs={{0,224},{16,240},{32,0},{48,16},{64,32},{80,48},{96,64},{112,80},{... | collective-permute-start | bytes 442376 | tf_op jit(solution)/shard_map/ppermute | solution.py:223
  138.2 1.9 %collective-permute-start.10 = (f32[128,256]{1,0:T(8,128)S(1)}, f32[128,256]{1,0:T(8,128)S(1)}, u32[]{:S(2)}, u32[]{:S(2)}) collective-permute-start(f32[128,256]{1,0:T(8,128)S(1)} %get-tuple-element.25), channel_id=1, source_target_pairs={{0,16},{16,0},{32,48},{48,32},{64,80},{80,64},{96,112},{112,96},{1... | collective-permute-start | bytes 393224 | tf_op jit(solution)/shard_map/ppermute | solution.py:227
  140.0 0.7 copy-start.9
  143.1 25.8 %all-to-all-start.4 = ((bf16[16,320,128]{2,1,0:T(8,128)(2,1)}), bf16[16,320,128]{2,1,0:T(8,128)(2,1)S(1)}, u32[]{:S(2)}, u32[]{:S(2)}) async-start(bf16[16,320,128]{2,1,0:T(8,128)(2,1)} %sum_feat.1), calls=%async_computation.4 | async-start | bytes 2621440 | tf_op jit(solution)/shard_map/all_to_all | solution.py:217
  (5 other events, 3.2 us)

commit v7 on v6

--- a/solution.py
+++ b/solution.py
@@ -22,7 +22,7 @@
 SEEDS = 256
 SLOTS = 128
 HID = 256
-UNROLL = 16
+UNROLL = 32
 G2 = 256
 RING = (0, -1, 1, -2, 2, -3, 3, -4)
 VMEM = pl.BlockSpec(memory_space=pltpu.VMEM)
@@ -50,22 +50,31 @@
     return lax.dot_general(a, b, (((ca,), (cb,)), ((), ())), preferred_element_type=F32)
 
 
-def picks_of(source, start, count_ref, lanes):
-    count = count_ref[source]
+def picks_by_source(count_ref, neigh_ref, hot):
+    names = neigh_ref[...].T
+    source = jnp.zeros(names.shape, I32)
+    base = jnp.zeros(names.shape, I32)
+    start = jnp.int32(0)
+    for s in range(1, ND):
+        start = start + count_ref[s - 1]
+        later = names >= start
+        source = jnp.where(later, s, source)
+        base = jnp.where(later, start, base)
+    slot = names - base
     row = lax.broadcasted_iota(I32, (SLOTS, SEEDS), 0)
-    position = jnp.where(row < count, row + start, -1)
-    total = jnp.zeros((SLOTS, SEEDS), F32)
     for k in range(K2):
-        total = total + jnp.where(position == lanes[k : k + 1, :], 1.0, 0.0)
-    return total.astype(BF), start + count
-
-
-def pick_body(count_ref, neigh_ref, dout_ref, t_ref):
-    start = jnp.int32(0)
-    lanes = neigh_ref[...]
+        hot[k] = jnp.where(row == slot[k : k + 1, :], 1.0, 0.0).astype(BF)
+    for s in range(ND):
+        here = jnp.where(source == s, 1.0, 0.0).astype(BF)
+        total = jnp.zeros((SLOTS, SEEDS), BF)
+        for k in range(K2):
+            total = total + hot[k] * here[k : k + 1, :]
+        yield s, total
+
+
+def pick_body(count_ref, neigh_ref, dout_ref, t_ref, hot):
     d_out = dout_ref[...]
-    for s in range(ND):
-        picks, start = picks_of(s, start, count_ref, lanes)
+    for s, picks in picks_by_source(count_ref, neigh_ref, hot):
         t_ref[s] = dot(picks, d_out).astype(BF)
 
 
@@ -201,12 +210,9 @@
             g2[(q % 8) * 32 : (q % 8) * 32 + 32, lanes] = in_ref[q, at : at + 32, :].astype(F32)
 
 
-def layer_body(count_ref, neigh_ref, in_ref, part_ref, w2n_ref, layer_ref):
-    start = jnp.int32(0)
-    names = neigh_ref[...]
+def layer_body(count_ref, neigh_ref, in_ref, part_ref, w2n_ref, layer_ref, hot):
     total = jnp.zeros((SEEDS, HID), F32)
-    for s in range(ND):
-        picks, start = picks_of(s, start, count_ref, names)
+    for s, picks in picks_by_source(count_ref, neigh_ref, hot):
         rows = [in_ref[s, 0:SLOTS, :], in_ref[s, SLOTS : 2 * SLOTS, :]]
         total = total + dot(picks, jnp.concatenate(rows, axis=1), 0, 0)
     mean_two = (total * (1.0 / K2)).astype(BF)
@@ -244,9 +250,10 @@
     seeds = seed_rows[0]
     grad_out = d_out[0, 0]
     counts = recv_count[:, 0, 0]
-    names = neigh_two[0, 0].T
+    names = neigh_two[0, 0]
+    hot = [pltpu.VMEM((K2, SLOTS, SEEDS), BF)]
     t_out = call(
-        pick_body, "picks", shape((ND, SLOTS, HID), BF), [SMEM, VMEM, VMEM], limit=60, us=5
+        pick_body, "picks", shape((ND, SLOTS, HID), BF), [SMEM, VMEM, VMEM], hot, limit=60, us=4
     )(counts, names, grad_out)
     t_in = swap(t_out, "dom")
 
@@ -274,15 +281,14 @@
         us=4,
     )(share, t_in, send, seeds, grad_out, w2_self, w2_neigh)
 
+    from_dom = swap(to_dom, "dom")
     ring = {0: d_pre}
     for i in range(1, 4):
-        ring[-i] = turn(ring[1 - i], 1)
-        ring[i] = turn(ring[i - 1], -1)
-    ring[-4] = turn(ring[-3], 1)
-    from_dom = swap(to_dom, "dom")
-
+        ring[-i], ring[i] = lax.optimization_barrier((turn(ring[1 - i], 1), turn(ring[i - 1], -1)))
+    from_dom, last = lax.optimization_barrier((from_dom, ring[-3]))
+    ring[-4] = turn(last, 1)
     two = call(first_sum_body, "sum_dom", shape((NF, 64, 128), BF), [VMEM])(from_dom)
-    two, ring[-4] = lax.optimization_barrier((two, ring[-4]))
+    two, ring[-3] = lax.optimization_barrier((two, ring[-3]))
     two = swap(two, "feat")
     keep, give = call(
         columns_body,
@@ -297,6 +303,7 @@
         "layer_two",
         shape((SEEDS, HID), BF),
         [SMEM] + [VMEM] * 4,
+        hot,
         limit=60,
         us=5,
     )(counts, names, from_dom, part, w2_neigh)

time: 172 us -> 166 us (0.965)
  Pallas kernels: 45.8 us -> 41.5 us
    ppermute x7, waiting for transfers between devices: 24.1 us -> 20.6 us  [turn(): lax.ppermute(x, 'feat', [(i, (i + 2 * step) % NF) for i in range(NF)])]
    all_to_all x4, waiting for transfers between devices: 12.8 us -> 15.1 us  [swap(): lax.all_to_all(x, axis, split_axis=0, concat_axis=0, tiled=True, axis_ind...]
  transfers between devices with their start and end apart: 15 -> 15, of which waited for: 7 -> 9; matrix products, arithmetic and copies ran while one was open for 1% -> 1% of each run, Pallas kernels for 23% -> 21%
where the time goes in v7:
time: 166 us; the launch traced here: 165 us
  starting transfers between devices  41.6 us (25%)
  Pallas kernels  41.5 us (25%)
  blocking collectives  39.1 us (24%)
  waiting for transfers between devices  36.7 us (22%)
  local copies, waits for them, and re-layouts  4.93 us (3%)
    all_to_all x1, blocking collectives, swap(): lax.all_to_all(x, axis, split_axis=0, concat_axis=0, tiled=True, axis_ind...  39.1 us
    all_to_all x4, starting transfers between devices, swap(): lax.all_to_all(x, axis, split_axis=0, concat_axis=0, tiled=True, axis_ind...  28.6 us
    pallas_call x1, Pallas kernels, per_device(): call(rows_body, 'node_rows', (rows, rows), [SMEM, VMEM, VMEM, SMEM] + [VM...  25.7 us
    ppermute x7, waiting for transfers between devices, turn(): lax.ppermute(x, 'feat', [(i, (i + 2 * step) % NF) for i in range(NF)])  20.6 us
    all_to_all x4, waiting for transfers between devices, swap(): lax.all_to_all(x, axis, split_axis=0, concat_axis=0, tiled=True, axis_ind...  15.1 us
    ppermute x7, starting transfers between devices, turn(): lax.ppermute(x, 'feat', [(i, (i + 2 * step) % NF) for i in range(NF)])  8.28 us
    unnamed x29, local copies, waits for them, and re-layouts  4.93 us
    ppermute x4, starting transfers between devices, fetch(): return lax.ppermute(x, 'feat', [(i, i ^ bit) for i in range(NF)])  4.71 us
  transfers between devices with their start and end apart: 15, of which 9 were waited for; matrix products, arithmetic and copies ran while one was open for 1% of the time, Pallas kernels for 21%

profile of v7, /device:TPU:1, one launch (start us, length us, event | category | flops | bytes accessed | tf_op | source)
XLA Modules:
  0.0 164.6 jit_solution(11926761086744430603)
XLA Ops:
  0.6 3.3 %collective-permute-start = (bf16[64,9216]{1,0:T(8,128)(2,1)}, bf16[64,9216]{1,0:T(8,128)(2,1)S(1)}, u32[]{:S(2)}, u32[]{:S(2)}) collective-permute-start(bf16[64,9216]{1,0:T(8,128)(2,1)} %bitcast.16), channel_id=1, source_target_pairs={{0,16},{16,0},{32,48},{48,32},{64,80},{80,64},{96,112},{112,96},{1... | collective-permute-start | bytes 3538952 | tf_op jit(solution)/shard_map/ppermute | solution.py:233
  4.5 1.5 copy.16
  5.9 3.6 %picks.1 = bf16[16,128,256]{2,1,0:T(8,128)(2,1)} custom-call(s32[16]{0:T(128)} %bitcast.19, s32[256,15]{1,0:T(8,128)} %bitcast.14, bf16[256,256]{1,0:T(8,128)(2,1)} %bitcast.10), custom_call_target="tpu_custom_call" | custom-call | flops 4000000000 | bytes 4000000 | tf_op jit(solution)/shard_map/picks/pallas_call | solution.py:255
  9.6 5.0 %all-to-all-start.1 = ((bf16[16,128,256]{2,1,0:T(8,128)(2,1)}), bf16[16,128,256]{2,1,0:T(8,128)(2,1)S(1)}, u32[]{:S(2)}, u32[]{:S(2)}) async-start(bf16[16,128,256]{2,1,0:T(8,128)(2,1)} %picks.1), calls=%async_computation.1 | async-start | bytes 2097152 | tf_op jit(solution)/shard_map/all_to_all | solution.py:223
  15.7 25.7 %node_rows.1 = (bf16[8,288,256]{2,1,0:T(8,128)(2,1)}, bf16[8,288,256]{2,1,0:T(8,128)(2,1)}) custom-call(s32[1]{0:T(128)} %bitcast.2.core_ref, bf16[64,9216]{1,0:T(8,128)(2,1)} %bitcast.17, bf16[64,9216]{1,0:T(8,128)(2,1)} %copy-done.10, s32[46080]{0:T(1024)} %bitcast.18, bf16[64,256]{1,0:T(8,128)(2,1)} %ws_ref.1, bf16[64,256]{1,0:T(8,128)(2,1)} %wn_ref.1, ...), custom_call_target="tpu_custom_call" | custom-call | flops 22000001024 | bytes 22000000 | tf_op jit(solution)/shard_map/node_rows/pallas_call | solution.py:261
  41.5 39.1 %all_to_all.25.share_ref = bf16[8,288,256]{2,1,0:T(8,128)(2,1)S(1)} all-to-all(bf16[8,288,256]{2,1,0:T(8,128)(2,1)} %get-tuple-element.26), channel_id=1, replica_groups={{0,32,64,96,128,160,192,224},{16,48,80,112,144,176,208,240},{1,33,65,97..., dimensions={0} | all-to-all | bytes 2359296 | tf_op jit(solution)/shard_map/all_to_all | solution.py:223
  80.6 3.1 %project.1 = (bf16[16,320,128]{2,1,0:T(8,128)(2,1)}, f32[256,256]{1,0:T(8,128)S(1)}, bf16[288,256]{1,0:T(8,128)(2,1)S(1)}) custom-call(bf16[8,288,256]{2,1,0:T(8,128)(2,1)S(1)} %all_to_all.25.share_ref, bf16[16,128,256]{2,1,0:T(8,128)(2,1)S(1)} %all-to-all-done.1.in_ref, s32[16,128]{1,0:T(8,128)S(1)} %bitcast.12, s32[1,256]{1,0:T(1,128)S(1)} %bitcast.13, ...), custom_call_target="tpu_custom_call" | custom-call | flops 4000000000 | bytes 4000000 | tf_op jit(solution)/shard_map/project/pallas_call | solution.py:272
  84.5 6.3 %all-to-all-start.2 = ((bf16[16,320,128]{2,1,0:T(8,128)(2,1)}), bf16[16,320,128]{2,1,0:T(8,128)(2,1)S(1)}, u32[]{:S(2)}, u32[]{:S(2)}) async-start(bf16[16,320,128]{2,1,0:T(8,128)(2,1)} %get-tuple-element.27), calls=%async_computation.2 | async-start | bytes 2621440 | tf_op jit(solution)/shard_map/all_to_all | solution.py:223
  90.9 1.5 collective-permute-start.3
  92.3 2.5 %collective-permute-done.4.refs_2_ = bf16[288,256]{1,0:T(8,128)(2,1)S(1)} collective-permute-done((bf16[288,256]{1,0:T(8,128)(2,1)S(1)}, bf16[288,256]{1,0:T(8,128)(2,1)S(1)}, u32[]{:S(2)}, u32[]{:S(2)}) %collective-permute-start.4) | collective-permute-done | bytes 147488 | tf_op jit(solution)/shard_map/ppermute | solution.py:229
  94.9 1.3 collective-permute-done.3.refs_1_
  96.3 2.5 %collective-permute-start.6 = (bf16[288,256]{1,0:T(8,128)(2,1)S(1)}, bf16[288,256]{1,0:T(8,128)(2,1)S(1)}, u32[]{:S(2)}, u32[]{:S(2)}) collective-permute-start(bf16[288,256]{1,0:T(8,128)(2,1)S(1)} %collective-permute-done.4.refs_2_), channel_id=1, source_target_pairs={{0,224},{16,240},{32,0},{48,16},{64,32},{80,48},{96,64},{112,80},{... | collective-permute-start | bytes 442376 | tf_op jit(solution)/shard_map/ppermute | solution.py:229
  98.8 2.8 %collective-permute-done.5.refs_3_ = bf16[288,256]{1,0:T(8,128)(2,1)S(1)} collective-permute-done((bf16[288,256]{1,0:T(8,128)(2,1)S(1)}, bf16[288,256]{1,0:T(8,128)(2,1)S(1)}, u32[]{:S(2)}, u32[]{:S(2)}) %collective-permute-start.5) | collective-permute-done | bytes 147488 | tf_op jit(solution)/shard_map/ppermute | solution.py:229
  101.7 2.7 %collective-permute-start.8 = (bf16[288,256]{1,0:T(8,128)(2,1)S(1)}, bf16[288,256]{1,0:T(8,128)(2,1)S(1)}, u32[]{:S(2)}, u32[]{:S(2)}) collective-permute-start(bf16[288,256]{1,0:T(8,128)(2,1)S(1)} %collective-permute-done.6.refs_4_), channel_id=1, source_target_pairs={{0,224},{16,240},{32,0},{48,16},{64,32},{80,48},{96,64},{112,80},{... | collective-permute-start | bytes 442376 | tf_op jit(solution)/shard_map/ppermute | solution.py:229
  104.3 2.7 %collective-permute-done.7.refs_5_ = bf16[288,256]{1,0:T(8,128)(2,1)S(1)} collective-permute-done((bf16[288,256]{1,0:T(8,128)(2,1)S(1)}, bf16[288,256]{1,0:T(8,128)(2,1)S(1)}, u32[]{:S(2)}, u32[]{:S(2)}) %collective-permute-start.7) | collective-permute-done | bytes 147488 | tf_op jit(solution)/shard_map/ppermute | solution.py:229
  109.4 10.2 %all-to-all-start.3 = ((bf16[16,64,128]{2,1,0:T(8,128)(2,1)}), bf16[16,64,128]{2,1,0:T(8,128)(2,1)S(1)}, u32[]{:S(2)}, u32[]{:S(2)}) async-start(bf16[16,64,128]{2,1,0:T(8,128)(2,1)} %sum_dom.1), calls=%async_computation.3 | async-start | bytes 524288 | tf_op jit(solution)/shard_map/all_to_all | solution.py:223
  119.6 1.4 collective-permute-start.9
  121.0 11.0 %collective-permute-done.9.refs_7_ = bf16[288,256]{1,0:T(8,128)(2,1)S(1)} collective-permute-done((bf16[288,256]{1,0:T(8,128)(2,1)S(1)}, bf16[288,256]{1,0:T(8,128)(2,1)S(1)}, u32[]{:S(2)}, u32[]{:S(2)}) %collective-permute-start.9) | collective-permute-done | bytes 147488 | tf_op jit(solution)/shard_map/ppermute | solution.py:229
  134.3 1.0 collective-permute-done.10.got_ref
  136.0 2.3 %sum_feat.1 = bf16[16,320,128]{2,1,0:T(8,128)(2,1)} custom-call(f32[128,256]{1,0:T(8,128)} %copy-done.7, f32[128,256]{1,0:T(8,128)} %copy-done.11, bf16[16,64,128]{2,1,0:T(8,128)(2,1)} %copy-done.9), custom_call_target="tpu_custom_call" | custom-call | flops 1000000000 | bytes 1000000 | tf_op jit(solution)/shard_map/sum_feat/pallas_call | solution.py:310
  138.3 7.0 %all-to-all-start.4 = ((bf16[16,320,128]{2,1,0:T(8,128)(2,1)}), bf16[16,320,128]{2,1,0:T(8,128)(2,1)S(1)}, u32[]{:S(2)}, u32[]{:S(2)}) async-start(bf16[16,320,128]{2,1,0:T(8,128)(2,1)} %sum_feat.1), calls=%async_computation.4 | async-start | bytes 2621440 | tf_op jit(solution)/shard_map/all_to_all | solution.py:223
  145.3 4.2 %layer_two.1 = bf16[256,256]{1,0:T(8,128)(2,1)} custom-call(s32[16]{0:T(128)} %bitcast.20, s32[256,15]{1,0:T(8,128)} %bitcast.15, bf16[16,320,128]{2,1,0:T(8,128)(2,1)} %copy-done, f32[256,256]{1,0:T(8,128)} %copy-done.8, bf16[256,256]{1,0:T(8,128)(2,1)} %w2n_ref.3), custom_call_target="tpu_custom_call" | custom-call | flops 5000000000 | bytes 5000000 | tf_op jit(solution)/shard_map/layer_two/pallas_call | solution.py:301
  149.5 14.2 %all-to-all-done.4.in_ref = bf16[16,320,128]{2,1,0:T(8,128)(2,1)S(1)} async-done(((bf16[16,320,128]{2,1,0:T(8,128)(2,1)}), bf16[16,320,128]{2,1,0:T(8,128)(2,1)S(1)}, u32[]{:S(2)}, u32[]{:S(2)}) %all-to-all-start.4) | async-done | bytes 1310752 | tf_op jit(solution)/shard_map/all_to_all | solution.py:223
  163.7 1.0 place.1
  (44 shorter events, 7.9 us)
Async XLA Ops:
  0.6 14.0 %collective-permute-start = (bf16[64,9216]{1,0:T(8,128)(2,1)}, bf16[64,9216]{1,0:T(8,128)(2,1)S(1)}, u32[]{:S(2)}, u32[]{:S(2)}) collective-permute-start(bf16[64,9216]{1,0:T(8,128)(2,1)} %bitcast.16), channel_id=1, source_target_pairs={{0,16},{16,0},{32,48},{48,32},{64,80},{80,64},{96,112},{112,96},{1... | collective-permute-start | bytes 3538952 | tf_op jit(solution)/shard_map/ppermute | solution.py:233
  4.0 10.7 %collective-permute-start.1 = (bf16[64,256]{1,0:T(8,128)(2,1)}, bf16[64,256]{1,0:T(8,128)(2,1)S(1)}, u32[]{:S(2)}, u32[]{:S(2)}) collective-permute-start(bf16[64,256]{1,0:T(8,128)(2,1)} %ws_ref.1), channel_id=1, source_target_pairs={{0,16},{16,0},{32,48},{48,32},{64,80},{80,64},{96,112},{112,96},{1... | collective-permute-start | bytes 98312 | tf_op jit(solution)/shard_map/ppermute | solution.py:233
  4.1 10.6 %collective-permute-start.2 = (bf16[64,256]{1,0:T(8,128)(2,1)}, bf16[64,256]{1,0:T(8,128)(2,1)S(1)}, u32[]{:S(2)}, u32[]{:S(2)}) collective-permute-start(bf16[64,256]{1,0:T(8,128)(2,1)} %wn_ref.1), channel_id=1, source_target_pairs={{0,16},{16,0},{32,48},{48,32},{64,80},{80,64},{96,112},{112,96},{1... | collective-permute-start | bytes 98312 | tf_op jit(solution)/shard_map/ppermute | solution.py:233
  9.6 31.8 %all-to-all-start.1 = ((bf16[16,128,256]{2,1,0:T(8,128)(2,1)}), bf16[16,128,256]{2,1,0:T(8,128)(2,1)S(1)}, u32[]{:S(2)}, u32[]{:S(2)}) async-start(bf16[16,128,256]{2,1,0:T(8,128)(2,1)} %picks.1), calls=%async_computation.1 | async-start | bytes 2097152 | tf_op jit(solution)/shard_map/all_to_all | solution.py:223
  14.7 1.0 copy-start.10
  41.4 39.2 %copy-start.1 = (bf16[1,1,256,256]{3,2,1,0:T(8,128)(2,1)S(1)}, bf16[1,1,256,256]{3,2,1,0:T(8,128)(2,1)}, u32[]{:S(2)}) copy-start(bf16[1,1,256,256]{3,2,1,0:T(8,128)(2,1)} %param.21) | copy-start | bytes 393220
  41.4 39.2 %copy-start.2 = (bf16[256,256]{1,0:T(8,128)(2,1)S(1)}, bf16[256,256]{1,0:T(8,128)(2,1)}, u32[]{:S(2)}) copy-start(bf16[256,256]{1,0:T(8,128)(2,1)} %w2s_ref.1) | copy-start | bytes 393220
  41.4 39.2 %copy-start.3 = (bf16[256,256]{1,0:T(8,128)(2,1)S(1)}, bf16[256,256]{1,0:T(8,128)(2,1)}, u32[]{:S(2)}) copy-start(bf16[256,256]{1,0:T(8,128)(2,1)} %w2n_ref.3) | copy-start | bytes 393220
  41.4 39.1 %copy-start.4 = (s32[1,1,16,128]{3,2,1,0:T(8,128)S(1)}, s32[1,1,16,128]{3,2,1,0:T(8,128)}, u32[]{:S(2)}) copy-start(s32[1,1,16,128]{3,2,1,0:T(8,128)} %param.17) | copy-start | bytes 24580
  41.5 39.1 %copy-start.5 = (s32[1,1,256]{2,1,0:T(1,128)S(1)}, s32[1,1,256]{2,1,0:T(1,128)}, u32[]{:S(2)}) copy-start(s32[1,1,256]{2,1,0:T(1,128)} %param.20) | copy-start | bytes 3076
  84.5 23.8 %all-to-all-start.2 = ((bf16[16,320,128]{2,1,0:T(8,128)(2,1)}), bf16[16,320,128]{2,1,0:T(8,128)(2,1)S(1)}, u32[]{:S(2)}, u32[]{:S(2)}) async-start(bf16[16,320,128]{2,1,0:T(8,128)(2,1)} %get-tuple-element.27), calls=%async_computation.2 | async-start | bytes 2621440 | tf_op jit(solution)/shard_map/all_to_all | solution.py:223
  90.8 41.2 %copy-start.6 = (bf16[8,288,256]{2,1,0:T(8,128)(2,1)S(1)}, bf16[8,288,256]{2,1,0:T(8,128)(2,1)}, u32[]{:S(2)}) copy-start(bf16[8,288,256]{2,1,0:T(8,128)(2,1)} %get-tuple-element.36.rows_ref) | copy-start | bytes 3538948
  90.8 4.1 %collective-permute-start.4 = (bf16[288,256]{1,0:T(8,128)(2,1)S(1)}, bf16[288,256]{1,0:T(8,128)(2,1)S(1)}, u32[]{:S(2)}, u32[]{:S(2)}) collective-permute-start(bf16[288,256]{1,0:T(8,128)(2,1)S(1)} %get-tuple-element.28.refs_0_), channel_id=1, source_target_pairs={{0,224},{16,240},{32,0},{48,16},{64,32},{80,48},{96,64},{112,80},{... | collective-permute-start | bytes 442376 | tf_op jit(solution)/shard_map/ppermute | solution.py:229
  90.9 5.3 %collective-permute-start.3 = (bf16[288,256]{1,0:T(8,128)(2,1)S(1)}, bf16[288,256]{1,0:T(8,128)(2,1)S(1)}, u32[]{:S(2)}, u32[]{:S(2)}) collective-permute-start(bf16[288,256]{1,0:T(8,128)(2,1)S(1)} %get-tuple-element.28.refs_0_), channel_id=1, source_target_pairs={{0,32},{16,48},{32,64},{48,80},{64,96},{80,112},{96,128},{112,144}... | collective-permute-start | bytes 442376 | tf_op jit(solution)/shard_map/ppermute | solution.py:229
  96.2 5.5 %collective-permute-start.5 = (bf16[288,256]{1,0:T(8,128)(2,1)S(1)}, bf16[288,256]{1,0:T(8,128)(2,1)S(1)}, u32[]{:S(2)}, u32[]{:S(2)}) collective-permute-start(bf16[288,256]{1,0:T(8,128)(2,1)S(1)} %collective-permute-done.3.refs_1_), channel_id=1, source_target_pairs={{0,32},{16,48},{32,64},{48,80},{64,96},{80,112},{96,128},{112,144}... | collective-permute-start | bytes 442376 | tf_op jit(solution)/shard_map/ppermute | solution.py:229
  96.3 5.3 %collective-permute-start.6 = (bf16[288,256]{1,0:T(8,128)(2,1)S(1)}, bf16[288,256]{1,0:T(8,128)(2,1)S(1)}, u32[]{:S(2)}, u32[]{:S(2)}) collective-permute-start(bf16[288,256]{1,0:T(8,128)(2,1)S(1)} %collective-permute-done.4.refs_2_), channel_id=1, source_target_pairs={{0,224},{16,240},{32,0},{48,16},{64,32},{80,48},{96,64},{112,80},{... | collective-permute-start | bytes 442376 | tf_op jit(solution)/shard_map/ppermute | solution.py:229
  101.7 5.4 %collective-permute-start.7 = (bf16[288,256]{1,0:T(8,128)(2,1)S(1)}, bf16[288,256]{1,0:T(8,128)(2,1)S(1)}, u32[]{:S(2)}, u32[]{:S(2)}) collective-permute-start(bf16[288,256]{1,0:T(8,128)(2,1)S(1)} %collective-permute-done.5.refs_3_), channel_id=1, source_target_pairs={{0,32},{16,48},{32,64},{48,80},{64,96},{80,112},{96,128},{112,144}... | collective-permute-start | bytes 442376 | tf_op jit(solution)/shard_map/ppermute | solution.py:229
  101.7 5.7 %collective-permute-start.8 = (bf16[288,256]{1,0:T(8,128)(2,1)S(1)}, bf16[288,256]{1,0:T(8,128)(2,1)S(1)}, u32[]{:S(2)}, u32[]{:S(2)}) collective-permute-start(bf16[288,256]{1,0:T(8,128)(2,1)S(1)} %collective-permute-done.6.refs_4_), channel_id=1, source_target_pairs={{0,224},{16,240},{32,0},{48,16},{64,32},{80,48},{96,64},{112,80},{... | collective-permute-start | bytes 442376 | tf_op jit(solution)/shard_map/ppermute | solution.py:229
  108.2 1.2 copy-start
  109.4 25.8 %all-to-all-start.3 = ((bf16[16,64,128]{2,1,0:T(8,128)(2,1)}), bf16[16,64,128]{2,1,0:T(8,128)(2,1)S(1)}, u32[]{:S(2)}, u32[]{:S(2)}) async-start(bf16[16,64,128]{2,1,0:T(8,128)(2,1)} %sum_dom.1), calls=%async_computation.3 | async-start | bytes 524288 | tf_op jit(solution)/shard_map/all_to_all | solution.py:223
  119.6 12.3 %collective-permute-start.9 = (bf16[288,256]{1,0:T(8,128)(2,1)S(1)}, bf16[288,256]{1,0:T(8,128)(2,1)S(1)}, u32[]{:S(2)}, u32[]{:S(2)}) collective-permute-start(bf16[288,256]{1,0:T(8,128)(2,1)S(1)} %collective-permute-done.7.refs_5_), channel_id=1, source_target_pairs={{0,32},{16,48},{32,64},{48,80},{64,96},{80,112},{96,128},{112,144}... | collective-permute-start | bytes 442376 | tf_op jit(solution)/shard_map/ppermute | solution.py:229
  133.4 1.9 %collective-permute-start.10 = (f32[128,256]{1,0:T(8,128)S(1)}, f32[128,256]{1,0:T(8,128)S(1)}, u32[]{:S(2)}, u32[]{:S(2)}) collective-permute-start(f32[128,256]{1,0:T(8,128)S(1)} %get-tuple-element.41), channel_id=1, source_target_pairs={{0,16},{16,0},{32,48},{48,32},{64,80},{80,64},{96,112},{112,96},{1... | collective-permute-start | bytes 393224 | tf_op jit(solution)/shard_map/ppermute | solution.py:233
  135.3 0.7 copy-start.9
  138.3 25.4 %all-to-all-start.4 = ((bf16[16,320,128]{2,1,0:T(8,128)(2,1)}), bf16[16,320,128]{2,1,0:T(8,128)(2,1)S(1)}, u32[]{:S(2)}, u32[]{:S(2)}) async-start(bf16[16,320,128]{2,1,0:T(8,128)(2,1)} %sum_feat.1), calls=%async_computation.4 | async-start | bytes 2621440 | tf_op jit(solution)/shard_map/all_to_all | solution.py:223
  (5 other events, 3.2 us)

commit v8 on v7

--- a/solution.py
+++ b/solution.py
@@ -51,7 +51,7 @@
 
 
 def picks_by_source(count_ref, neigh_ref, hot):
-    names = neigh_ref[...].T
+    names = neigh_ref[...].reshape(K2, SEEDS)
     source = jnp.zeros(names.shape, I32)
     base = jnp.zeros(names.shape, I32)
     start = jnp.int32(0)
@@ -184,30 +184,21 @@
         out_ref[f] = total
 
 
-def second_sum_body(keep_ref, got_ref, two_ref, out_ref):
-    one = (keep_ref[...] + got_ref[...]).astype(BF)
+def second_sum_body(two_ref, out_ref):
     two = two_ref[0].astype(F32)
     for f in range(1, NF):
         two = two + two_ref[f].astype(F32)
     two = two.astype(BF)
     for q in range(ND):
-        out_ref[q, 0:PAIR, :] = one[:, 0:128]
-        out_ref[q, PAIR : 2 * PAIR, :] = one[:, 128:256]
-        out_ref[q, 2 * PAIR :, :] = two
-
-
-def place_body(in_ref, g1s_ref, g1n_ref, g2s_ref, g2n_ref):
-    one = in_ref[0, 0 : 2 * PAIR, :].astype(F32)
-    for q in range(1, ND):
-        one = one + in_ref[q, 0 : 2 * PAIR, :].astype(F32)
-    for h in range(2):
-        lanes = slice(h * 128, (h + 1) * 128)
-        g1s_ref[:, lanes] = one[h * PAIR : h * PAIR + COLS]
-        g1n_ref[:, lanes] = one[h * PAIR + COLS : (h + 1) * PAIR]
-        for q in range(ND):
-            g2 = g2s_ref if q < 8 else g2n_ref
-            at = 2 * PAIR + h * 32
-            g2[(q % 8) * 32 : (q % 8) * 32 + 32, lanes] = in_ref[q, at : at + 32, :].astype(F32)
+        out_ref[q] = two
+
+
+def place_body(in_ref, g2s_ref, g2n_ref):
+    for q in range(ND):
+        g2 = g2s_ref if q < 8 else g2n_ref
+        for h in range(2):
+            piece = in_ref[q, h * 32 : h * 32 + 32, :].astype(F32)
+            g2[(q % 8) * 32 : (q % 8) * 32 + 32, h * 128 : (h + 1) * 128] = piece
 
 
 def layer_body(count_ref, neigh_ref, in_ref, part_ref, w2n_ref, layer_ref, hot):
@@ -227,6 +218,11 @@
 
 def turn(x, step):
     return lax.ppermute(x, "feat", [(i, (i + 2 * step) % NF) for i in range(NF)])
+
+
+def along(x, step):
+    pairs = [(i, (i + step) % ND if step % 4 == 0 else i // 4 * 4 + (i + step) % 4) for i in range(ND)]
+    return lax.ppermute(x, "dom", pairs)
 
 
 def fetch(x, bit):
@@ -250,7 +246,7 @@
     seeds = seed_rows[0]
     grad_out = d_out[0, 0]
     counts = recv_count[:, 0, 0]
-    names = neigh_two[0, 0]
+    names = neigh_two[0].transpose(2, 0, 1)
     hot = [pltpu.VMEM((K2, SLOTS, SEEDS), BF)]
     t_out = call(
         pick_body, "picks", shape((ND, SLOTS, HID), BF), [SMEM, VMEM, VMEM], hot, limit=60, us=4
@@ -288,7 +284,7 @@
     from_dom, last = lax.optimization_barrier((from_dom, ring[-3]))
     ring[-4] = turn(last, 1)
     two = call(first_sum_body, "sum_dom", shape((NF, 64, 128), BF), [VMEM])(from_dom)
-    two, ring[-3] = lax.optimization_barrier((two, ring[-3]))
+    two, ring[-4] = lax.optimization_barrier((two, ring[-4]))
     two = swap(two, "feat")
     keep, give = call(
         columns_body,
@@ -297,24 +293,22 @@
         [SMEM] + [VMEM] * (1 + NZ),
         us=2,
     )(chip, rows, *[ring[i] for i in RING])
-    got = fetch(give, 1)
+    one = keep + fetch(give, 1)
+    one = one + sum(along(one, 4 * i) for i in range(1, 4))
+    one = one + sum(along(one, i) for i in range(1, 4))
     layer_out = call(
         layer_body,
         "layer_two",
         shape((SEEDS, HID), BF),
         [SMEM] + [VMEM] * 4,
         hot,
-        limit=60,
         us=5,
     )(counts, names, from_dom, part, w2_neigh)
-    done = call(
-        second_sum_body, "sum_feat", shape((ND, 2 * PAIR + 64, 128), BF), [VMEM] * 3, limit=60
-    )(keep, got, two)
+    done = call(second_sum_body, "sum_feat", shape((ND, 64, 128), BF), [VMEM], limit=60)(two)
     done = swap(done, "dom")
-    first = shape((COLS, HID), F32)
     second = shape((HID, HID), F32)
-    grads = call(place_body, "place", (first, first, second, second), [VMEM])(done)
-    return (layer_out[None, None], *grads)
+    two_self, two_neigh = call(place_body, "place", (second, second), [VMEM])(done)
+    return (layer_out[None, None], one[:COLS], one[COLS:], two_self, two_neigh)
 
 
 def solution(mesh):

time: 166 us -> 159 us (0.958)
  waiting for transfers between devices: 36.7 us -> 29.4 us
  starting transfers between devices: 41.6 us -> 46.7 us
  local copies, waits for them, and re-layouts: 4.93 us -> 2.42 us
    ppermute x0 -> x6, starting transfers between devices: none -> 6.87 us  [along(): return lax.ppermute(x, 'dom', pairs)]
    all_to_all x4, starting transfers between devices: 28.6 us -> 22.2 us  [swap(): lax.all_to_all(x, axis, split_axis=0, concat_axis=0, tiled=True, axis_ind...]
    all_to_all x4, waiting for transfers between devices: 15.1 us -> 8.9 us  [swap(): lax.all_to_all(x, axis, split_axis=0, concat_axis=0, tiled=True, axis_ind...]
    ppermute x4, starting transfers between devices: 4.71 us -> 10.7 us  [fetch(): return lax.ppermute(x, 'feat', [(i, i ^ bit) for i in range(NF)])]
    ppermute x7, waiting for transfers between devices: 20.6 us -> 15.5 us  [turn(): lax.ppermute(x, 'feat', [(i, (i + 2 * step) % NF) for i in range(NF)])]
    ppermute x0 -> x6, waiting for transfers between devices: none -> 4.05 us  [along(): return lax.ppermute(x, 'dom', pairs)]
    unnamed x29 -> x24, local copies, waits for them, and re-layouts: 4.93 us -> 1.76 us
  transfers between devices with their start and end apart: 15 -> 21, of which waited for: 9 -> 12; matrix products, arithmetic and copies ran while one was open for 1% -> 0% of each run, Pallas kernels for 21% -> 22%
where the time goes in v8:
time: 159 us
  starting transfers between devices  46.7 us (29%)
  Pallas kernels  40.1 us (25%)
  blocking collectives  39.1 us (25%)
  waiting for transfers between devices  29.4 us (18%)
  local copies, waits for them, and re-layouts  2.42 us (2%)
    all_to_all x1, blocking collectives, swap(): lax.all_to_all(x, axis, split_axis=0, concat_axis=0, tiled=True, axis_ind...  39.1 us
    pallas_call x1, Pallas kernels, per_device(): call(rows_body, 'node_rows', (rows, rows), [SMEM, VMEM, VMEM, SMEM] + [VM...  25.7 us
    all_to_all x4, starting transfers between devices, swap(): lax.all_to_all(x, axis, split_axis=0, concat_axis=0, tiled=True, axis_ind...  22.2 us
    ppermute x7, waiting for transfers between devices, turn(): lax.ppermute(x, 'feat', [(i, (i + 2 * step) % NF) for i in range(NF)])  15.5 us
    ppermute x4, starting transfers between devices, fetch(): return lax.ppermute(x, 'feat', [(i, i ^ bit) for i in range(NF)])  10.7 us
    all_to_all x4, waiting for transfers between devices, swap(): lax.all_to_all(x, axis, split_axis=0, concat_axis=0, tiled=True, axis_ind...  8.9 us
    ppermute x7, starting transfers between devices, turn(): lax.ppermute(x, 'feat', [(i, (i + 2 * step) % NF) for i in range(NF)])  6.92 us
    ppermute x6, starting transfers between devices, along(): return lax.ppermute(x, 'dom', pairs)  6.87 us
  transfers between devices with their start and end apart: 21, of which 12 were waited for; matrix products, arithmetic and copies ran while one was open for 0% of the time, Pallas kernels for 22%

profile of v8, /device:TPU:1, one launch (start us, length us, event | category | flops | bytes accessed | tf_op | source)
XLA Modules:
  0.0 158.7 jit_solution(1827473180461894566)
XLA Ops:
  0.6 3.3 %collective-permute-start = (bf16[64,9216]{1,0:T(8,128)(2,1)}, bf16[64,9216]{1,0:T(8,128)(2,1)S(1)}, u32[]{:S(2)}, u32[]{:S(2)}) collective-permute-start(bf16[64,9216]{1,0:T(8,128)(2,1)} %bitcast.20), channel_id=1, source_target_pairs={{0,16},{16,0},{32,48},{48,32},{64,80},{80,64},{96,112},{112,96},{1... | collective-permute-start | bytes 3538952 | tf_op jit(solution)/shard_map/ppermute | solution.py:229
  4.5 3.8 %picks.1 = bf16[16,128,256]{2,1,0:T(8,128)(2,1)} custom-call(s32[16]{0:T(128)} %bitcast.18, s32[15,1,256]{2,1,0:T(1,128)} %bitcast.14, bf16[256,256]{1,0:T(8,128)(2,1)} %bitcast.12), custom_call_target="tpu_custom_call" | custom-call | flops 4000000000 | bytes 4000000 | tf_op jit(solution)/shard_map/picks/pallas_call | solution.py:251
  8.3 5.0 %all-to-all-start.1 = ((bf16[16,128,256]{2,1,0:T(8,128)(2,1)}), bf16[16,128,256]{2,1,0:T(8,128)(2,1)S(1)}, u32[]{:S(2)}, u32[]{:S(2)}) async-start(bf16[16,128,256]{2,1,0:T(8,128)(2,1)} %picks.1), calls=%async_computation.1 | async-start | bytes 2097152 | tf_op jit(solution)/shard_map/all_to_all | solution.py:214
  14.4 25.7 %node_rows.1 = (bf16[8,288,256]{2,1,0:T(8,128)(2,1)}, bf16[8,288,256]{2,1,0:T(8,128)(2,1)}) custom-call(s32[1]{0:T(128)} %bitcast.3.core_ref, bf16[64,9216]{1,0:T(8,128)(2,1)} %bitcast.21, bf16[64,9216]{1,0:T(8,128)(2,1)} %copy-done.9, s32[46080]{0:T(1024)} %bitcast.22, bf16[64,256]{1,0:T(8,128)(2,1)} %ws_ref.1, bf16[64,256]{1,0:T(8,128)(2,1)} %wn_ref.1, ...), custom_call_target="tpu_custom_call" | custom-call | flops 22000001024 | bytes 22000000 | tf_op jit(solution)/shard_map/node_rows/pallas_call | solution.py:257
  40.2 39.1 %all_to_all.25.share_ref = bf16[8,288,256]{2,1,0:T(8,128)(2,1)S(1)} all-to-all(bf16[8,288,256]{2,1,0:T(8,128)(2,1)} %get-tuple-element.24), channel_id=1, replica_groups={{0,32,64,96,128,160,192,224},{16,48,80,112,144,176,208,240},{1,33,65,97..., dimensions={0} | all-to-all | bytes 2359296 | tf_op jit(solution)/shard_map/all_to_all | solution.py:214
  79.3 3.1 %project.1 = (bf16[16,320,128]{2,1,0:T(8,128)(2,1)}, f32[256,256]{1,0:T(8,128)S(1)}, bf16[288,256]{1,0:T(8,128)(2,1)S(1)}) custom-call(bf16[8,288,256]{2,1,0:T(8,128)(2,1)S(1)} %all_to_all.25.share_ref, bf16[16,128,256]{2,1,0:T(8,128)(2,1)S(1)} %all-to-all-done.1.in_ref, s32[16,128]{1,0:T(8,128)S(1)} %bitcast.16, s32[1,256]{1,0:T(1,128)S(1)} %bitcast.17, ...), custom_call_target="tpu_custom_call" | custom-call | flops 4000000000 | bytes 4000000 | tf_op jit(solution)/shard_map/project/pallas_call | solution.py:268
  82.5 6.3 %all-to-all-start.2 = ((bf16[16,320,128]{2,1,0:T(8,128)(2,1)}), bf16[16,320,128]{2,1,0:T(8,128)(2,1)S(1)}, u32[]{:S(2)}, u32[]{:S(2)}) async-start(bf16[16,320,128]{2,1,0:T(8,128)(2,1)} %get-tuple-element.25), calls=%async_computation.2 | async-start | bytes 2621440 | tf_op jit(solution)/shard_map/all_to_all | solution.py:214
  88.9 1.5 collective-permute-start.3
  90.3 2.5 %collective-permute-done.4.refs_2_ = bf16[288,256]{1,0:T(8,128)(2,1)S(1)} collective-permute-done((bf16[288,256]{1,0:T(8,128)(2,1)S(1)}, bf16[288,256]{1,0:T(8,128)(2,1)S(1)}, u32[]{:S(2)}, u32[]{:S(2)}) %collective-permute-start.4) | collective-permute-done | bytes 147488 | tf_op jit(solution)/shard_map/ppermute | solution.py:220
  92.9 1.3 collective-permute-done.3.refs_1_
  94.3 2.5 %collective-permute-start.6 = (bf16[288,256]{1,0:T(8,128)(2,1)S(1)}, bf16[288,256]{1,0:T(8,128)(2,1)S(1)}, u32[]{:S(2)}, u32[]{:S(2)}) collective-permute-start(bf16[288,256]{1,0:T(8,128)(2,1)S(1)} %collective-permute-done.4.refs_2_), channel_id=1, source_target_pairs={{0,224},{16,240},{32,0},{48,16},{64,32},{80,48},{96,64},{112,80},{... | collective-permute-start | bytes 442376 | tf_op jit(solution)/shard_map/ppermute | solution.py:220
  96.8 2.8 %collective-permute-done.5.refs_3_ = bf16[288,256]{1,0:T(8,128)(2,1)S(1)} collective-permute-done((bf16[288,256]{1,0:T(8,128)(2,1)S(1)}, bf16[288,256]{1,0:T(8,128)(2,1)S(1)}, u32[]{:S(2)}, u32[]{:S(2)}) %collective-permute-start.5) | collective-permute-done | bytes 147488 | tf_op jit(solution)/shard_map/ppermute | solution.py:220
  99.7 2.7 %collective-permute-start.8 = (bf16[288,256]{1,0:T(8,128)(2,1)S(1)}, bf16[288,256]{1,0:T(8,128)(2,1)S(1)}, u32[]{:S(2)}, u32[]{:S(2)}) collective-permute-start(bf16[288,256]{1,0:T(8,128)(2,1)S(1)} %collective-permute-done.6.refs_4_), channel_id=1, source_target_pairs={{0,224},{16,240},{32,0},{48,16},{64,32},{80,48},{96,64},{112,80},{... | collective-permute-start | bytes 442376 | tf_op jit(solution)/shard_map/ppermute | solution.py:220
  102.3 2.7 %collective-permute-done.7.refs_5_ = bf16[288,256]{1,0:T(8,128)(2,1)S(1)} collective-permute-done((bf16[288,256]{1,0:T(8,128)(2,1)S(1)}, bf16[288,256]{1,0:T(8,128)(2,1)S(1)}, u32[]{:S(2)}, u32[]{:S(2)}) %collective-permute-start.7) | collective-permute-done | bytes 147488 | tf_op jit(solution)/shard_map/ppermute | solution.py:220
  107.0 5.8 %collective-permute-done.9.refs_7_ = bf16[288,256]{1,0:T(8,128)(2,1)S(1)} collective-permute-done((bf16[288,256]{1,0:T(8,128)(2,1)S(1)}, bf16[288,256]{1,0:T(8,128)(2,1)S(1)}, u32[]{:S(2)}, u32[]{:S(2)}) %collective-permute-start.9) | collective-permute-done | bytes 147488 | tf_op jit(solution)/shard_map/ppermute | solution.py:220
  113.6 6.8 %collective-permute-start.10 = (f32[128,256]{1,0:T(8,128)S(1)}, f32[128,256]{1,0:T(8,128)S(1)}, u32[]{:S(2)}, u32[]{:S(2)}) collective-permute-start(f32[128,256]{1,0:T(8,128)S(1)} %get-tuple-element.39), channel_id=1, source_target_pairs={{0,16},{16,0},{32,48},{48,32},{64,80},{80,64},{96,112},{112,96},{1... | collective-permute-start | bytes 393224 | tf_op jit(solution)/shard_map/ppermute | solution.py:229
  121.5 2.4 %collective-permute-start.13 = (f32[128,256]{1,0:T(8,128)S(1)}, f32[128,256]{1,0:T(8,128)S(1)}, u32[]{:S(2)}, u32[]{:S(2)}) collective-permute-start(f32[128,256]{1,0:T(8,128)S(1)} %add.21), channel_id=1, source_target_pairs={{0,12},{1,13},{2,14},{3,15},{4,0},{5,1},{6,2},{7,3},{8,4},{9,5},{1... | collective-permute-start | bytes 393224 | tf_op jit(solution)/shard_map/ppermute | solution.py:225
  124.9 4.7 %all-to-all-start.3 = ((bf16[16,64,128]{2,1,0:T(8,128)(2,1)}), bf16[16,64,128]{2,1,0:T(8,128)(2,1)S(1)}, u32[]{:S(2)}, u32[]{:S(2)}) async-start(bf16[16,64,128]{2,1,0:T(8,128)(2,1)} %sum_dom.1), calls=%async_computation.3 | async-start | bytes 524288 | tf_op jit(solution)/shard_map/all_to_all | solution.py:214
  129.8 3.8 %collective-permute-done.11 = f32[128,256]{1,0:T(8,128)S(1)} collective-permute-done((f32[128,256]{1,0:T(8,128)S(1)}, f32[128,256]{1,0:T(8,128)S(1)}, u32[]{:S(2)}, u32[]{:S(2)}) %collective-permute-start.11) | collective-permute-done | bytes 131104 | tf_op jit(solution)/shard_map/ppermute | solution.py:225
  133.7 2.5 %collective-permute-start.16 = (f32[128,256]{1,0:T(8,128)S(1)}, f32[128,256]{1,0:T(8,128)S(1)}, u32[]{:S(2)}, u32[]{:S(2)}) collective-permute-start(f32[128,256]{1,0:T(8,128)S(1)} %add_add_fusion.1), channel_id=1, source_target_pairs={{0,3},{1,0},{2,1},{3,2},{4,7},{5,4},{6,5},{7,6},{8,11},{9,8},{10,9... | collective-permute-start | bytes 393224 | tf_op jit(solution)/shard_map/ppermute | solution.py:225
  137.1 3.4 %layer_two.1 = bf16[256,256]{1,0:T(8,128)(2,1)} custom-call(s32[16]{0:T(128)S(1)} %bitcast.19, s32[15,1,256]{2,1,0:T(1,128)S(1)} %bitcast.15, bf16[16,320,128]{2,1,0:T(8,128)(2,1)S(1)} %all-to-all-done.2.in_ref, f32[256,256]{1,0:T(8,128)S(1)} %get-tuple-element.33.part_ref, bf16[256,256]{1,0:T(8,128)(2,1)S(1)} %copy-done.2), custom_call_target="tpu_custom_call" | custom-call | flops 5000000000 | bytes 5000000 | tf_op jit(solution)/shard_map/layer_two/pallas_call | solution.py:299
  142.0 1.7 %sum_feat.1 = bf16[16,64,128]{2,1,0:T(8,128)(2,1)} custom-call(bf16[16,64,128]{2,1,0:T(8,128)(2,1)} %copy-done.8), custom_call_target="tpu_custom_call" | custom-call | flops 1000000000 | bytes 1000000 | tf_op jit(solution)/shard_map/sum_feat/pallas_call | solution.py:307
  143.7 6.2 %all-to-all-start.4 = ((bf16[16,64,128]{2,1,0:T(8,128)(2,1)}), bf16[16,64,128]{2,1,0:T(8,128)(2,1)S(1)}, u32[]{:S(2)}, u32[]{:S(2)}) async-start(bf16[16,64,128]{2,1,0:T(8,128)(2,1)} %sum_feat.1), calls=%async_computation.4 | async-start | bytes 524288 | tf_op jit(solution)/shard_map/all_to_all | solution.py:214
  150.6 7.2 %all-to-all-done.4.in_ref = bf16[16,64,128]{2,1,0:T(8,128)(2,1)S(1)} async-done(((bf16[16,64,128]{2,1,0:T(8,128)(2,1)}), bf16[16,64,128]{2,1,0:T(8,128)(2,1)S(1)}, u32[]{:S(2)}, u32[]{:S(2)}) %all-to-all-start.4) | async-done | bytes 262176 | tf_op jit(solution)/shard_map/all_to_all | solution.py:214
  (55 shorter events, 10.8 us)
Async XLA Ops:
  0.6 12.8 %collective-permute-start = (bf16[64,9216]{1,0:T(8,128)(2,1)}, bf16[64,9216]{1,0:T(8,128)(2,1)S(1)}, u32[]{:S(2)}, u32[]{:S(2)}) collective-permute-start(bf16[64,9216]{1,0:T(8,128)(2,1)} %bitcast.20), channel_id=1, source_target_pairs={{0,16},{16,0},{32,48},{48,32},{64,80},{80,64},{96,112},{112,96},{1... | collective-permute-start | bytes 3538952 | tf_op jit(solution)/shard_map/ppermute | solution.py:229
  4.0 9.4 %collective-permute-start.1 = (bf16[64,256]{1,0:T(8,128)(2,1)}, bf16[64,256]{1,0:T(8,128)(2,1)S(1)}, u32[]{:S(2)}, u32[]{:S(2)}) collective-permute-start(bf16[64,256]{1,0:T(8,128)(2,1)} %ws_ref.1), channel_id=1, source_target_pairs={{0,16},{16,0},{32,48},{48,32},{64,80},{80,64},{96,112},{112,96},{1... | collective-permute-start | bytes 98312 | tf_op jit(solution)/shard_map/ppermute | solution.py:229
  4.1 9.3 %collective-permute-start.2 = (bf16[64,256]{1,0:T(8,128)(2,1)}, bf16[64,256]{1,0:T(8,128)(2,1)S(1)}, u32[]{:S(2)}, u32[]{:S(2)}) collective-permute-start(bf16[64,256]{1,0:T(8,128)(2,1)} %wn_ref.1), channel_id=1, source_target_pairs={{0,16},{16,0},{32,48},{48,32},{64,80},{80,64},{96,112},{112,96},{1... | collective-permute-start | bytes 98312 | tf_op jit(solution)/shard_map/ppermute | solution.py:229
  8.3 31.8 %all-to-all-start.1 = ((bf16[16,128,256]{2,1,0:T(8,128)(2,1)}), bf16[16,128,256]{2,1,0:T(8,128)(2,1)S(1)}, u32[]{:S(2)}, u32[]{:S(2)}) async-start(bf16[16,128,256]{2,1,0:T(8,128)(2,1)} %picks.1), calls=%async_computation.1 | async-start | bytes 2097152 | tf_op jit(solution)/shard_map/all_to_all | solution.py:214
  40.1 39.2 %copy-start = (bf16[1,1,256,256]{3,2,1,0:T(8,128)(2,1)S(1)}, bf16[1,1,256,256]{3,2,1,0:T(8,128)(2,1)}, u32[]{:S(2)}) copy-start(bf16[1,1,256,256]{3,2,1,0:T(8,128)(2,1)} %param.21) | copy-start | bytes 393220
  40.1 39.2 %copy-start.1 = (bf16[256,256]{1,0:T(8,128)(2,1)S(1)}, bf16[256,256]{1,0:T(8,128)(2,1)}, u32[]{:S(2)}) copy-start(bf16[256,256]{1,0:T(8,128)(2,1)} %w2s_ref.1) | copy-start | bytes 393220
  40.1 39.2 %copy-start.2 = (bf16[256,256]{1,0:T(8,128)(2,1)S(1)}, bf16[256,256]{1,0:T(8,128)(2,1)}, u32[]{:S(2)}) copy-start(bf16[256,256]{1,0:T(8,128)(2,1)} %w2n_ref.3) | copy-start | bytes 393220
  82.5 23.8 %all-to-all-start.2 = ((bf16[16,320,128]{2,1,0:T(8,128)(2,1)}), bf16[16,320,128]{2,1,0:T(8,128)(2,1)S(1)}, u32[]{:S(2)}, u32[]{:S(2)}) async-start(bf16[16,320,128]{2,1,0:T(8,128)(2,1)} %get-tuple-element.25), calls=%async_computation.2 | async-start | bytes 2621440 | tf_op jit(solution)/shard_map/all_to_all | solution.py:214
  88.8 4.1 %collective-permute-start.4 = (bf16[288,256]{1,0:T(8,128)(2,1)S(1)}, bf16[288,256]{1,0:T(8,128)(2,1)S(1)}, u32[]{:S(2)}, u32[]{:S(2)}) collective-permute-start(bf16[288,256]{1,0:T(8,128)(2,1)S(1)} %get-tuple-element.26.refs_0_), channel_id=1, source_target_pairs={{0,224},{16,240},{32,0},{48,16},{64,32},{80,48},{96,64},{112,80},{... | collective-permute-start | bytes 442376 | tf_op jit(solution)/shard_map/ppermute | solution.py:220
  88.9 5.3 %collective-permute-start.3 = (bf16[288,256]{1,0:T(8,128)(2,1)S(1)}, bf16[288,256]{1,0:T(8,128)(2,1)S(1)}, u32[]{:S(2)}, u32[]{:S(2)}) collective-permute-start(bf16[288,256]{1,0:T(8,128)(2,1)S(1)} %get-tuple-element.26.refs_0_), channel_id=1, source_target_pairs={{0,32},{16,48},{32,64},{48,80},{64,96},{80,112},{96,128},{112,144}... | collective-permute-start | bytes 442376 | tf_op jit(solution)/shard_map/ppermute | solution.py:220
  94.2 5.5 %collective-permute-start.5 = (bf16[288,256]{1,0:T(8,128)(2,1)S(1)}, bf16[288,256]{1,0:T(8,128)(2,1)S(1)}, u32[]{:S(2)}, u32[]{:S(2)}) collective-permute-start(bf16[288,256]{1,0:T(8,128)(2,1)S(1)} %collective-permute-done.3.refs_1_), channel_id=1, source_target_pairs={{0,32},{16,48},{32,64},{48,80},{64,96},{80,112},{96,128},{112,144}... | collective-permute-start | bytes 442376 | tf_op jit(solution)/shard_map/ppermute | solution.py:220
  94.3 5.3 %collective-permute-start.6 = (bf16[288,256]{1,0:T(8,128)(2,1)S(1)}, bf16[288,256]{1,0:T(8,128)(2,1)S(1)}, u32[]{:S(2)}, u32[]{:S(2)}) collective-permute-start(bf16[288,256]{1,0:T(8,128)(2,1)S(1)} %collective-permute-done.4.refs_2_), channel_id=1, source_target_pairs={{0,224},{16,240},{32,0},{48,16},{64,32},{80,48},{96,64},{112,80},{... | collective-permute-start | bytes 442376 | tf_op jit(solution)/shard_map/ppermute | solution.py:220
  99.7 5.4 %collective-permute-start.7 = (bf16[288,256]{1,0:T(8,128)(2,1)S(1)}, bf16[288,256]{1,0:T(8,128)(2,1)S(1)}, u32[]{:S(2)}, u32[]{:S(2)}) collective-permute-start(bf16[288,256]{1,0:T(8,128)(2,1)S(1)} %collective-permute-done.5.refs_3_), channel_id=1, source_target_pairs={{0,32},{16,48},{32,64},{48,80},{64,96},{80,112},{96,128},{112,144}... | collective-permute-start | bytes 442376 | tf_op jit(solution)/shard_map/ppermute | solution.py:220
  99.7 5.7 %collective-permute-start.8 = (bf16[288,256]{1,0:T(8,128)(2,1)S(1)}, bf16[288,256]{1,0:T(8,128)(2,1)S(1)}, u32[]{:S(2)}, u32[]{:S(2)}) collective-permute-start(bf16[288,256]{1,0:T(8,128)(2,1)S(1)} %collective-permute-done.6.refs_4_), channel_id=1, source_target_pairs={{0,224},{16,240},{32,0},{48,16},{64,32},{80,48},{96,64},{112,80},{... | collective-permute-start | bytes 442376 | tf_op jit(solution)/shard_map/ppermute | solution.py:220
  106.2 6.6 %collective-permute-start.9 = (bf16[288,256]{1,0:T(8,128)(2,1)S(1)}, bf16[288,256]{1,0:T(8,128)(2,1)S(1)}, u32[]{:S(2)}, u32[]{:S(2)}) collective-permute-start(bf16[288,256]{1,0:T(8,128)(2,1)S(1)} %collective-permute-done.7.refs_5_), channel_id=1, source_target_pairs={{0,32},{16,48},{32,64},{48,80},{64,96},{80,112},{96,128},{112,144}... | collective-permute-start | bytes 442376 | tf_op jit(solution)/shard_map/ppermute | solution.py:220
  113.6 7.8 %collective-permute-start.10 = (f32[128,256]{1,0:T(8,128)S(1)}, f32[128,256]{1,0:T(8,128)S(1)}, u32[]{:S(2)}, u32[]{:S(2)}) collective-permute-start(f32[128,256]{1,0:T(8,128)S(1)} %get-tuple-element.39), channel_id=1, source_target_pairs={{0,16},{16,0},{32,48},{48,32},{64,80},{80,64},{96,112},{112,96},{1... | collective-permute-start | bytes 393224 | tf_op jit(solution)/shard_map/ppermute | solution.py:229
  121.5 8.1 %collective-permute-start.13 = (f32[128,256]{1,0:T(8,128)S(1)}, f32[128,256]{1,0:T(8,128)S(1)}, u32[]{:S(2)}, u32[]{:S(2)}) collective-permute-start(f32[128,256]{1,0:T(8,128)S(1)} %add.21), channel_id=1, source_target_pairs={{0,12},{1,13},{2,14},{3,15},{4,0},{5,1},{6,2},{7,3},{8,4},{9,5},{1... | collective-permute-start | bytes 393224 | tf_op jit(solution)/shard_map/ppermute | solution.py:225
  123.9 5.9 %collective-permute-start.12 = (f32[128,256]{1,0:T(8,128)S(1)}, f32[128,256]{1,0:T(8,128)S(1)}, u32[]{:S(2)}, u32[]{:S(2)}) collective-permute-start(f32[128,256]{1,0:T(8,128)S(1)} %add.21), channel_id=1, source_target_pairs={{0,8},{1,9},{2,10},{3,11},{4,12},{5,13},{6,14},{7,15},{8,0},{9,1},... | collective-permute-start | bytes 393224 | tf_op jit(solution)/shard_map/ppermute | solution.py:225
  124.3 9.3 %collective-permute-start.11 = (f32[128,256]{1,0:T(8,128)S(1)}, f32[128,256]{1,0:T(8,128)S(1)}, u32[]{:S(2)}, u32[]{:S(2)}) collective-permute-start(f32[128,256]{1,0:T(8,128)S(1)} %add.21), channel_id=1, source_target_pairs={{0,4},{1,5},{2,6},{3,7},{4,8},{5,9},{6,10},{7,11},{8,12},{9,13},{1... | collective-permute-start | bytes 393224 | tf_op jit(solution)/shard_map/ppermute | solution.py:225
  124.9 16.4 %all-to-all-start.3 = ((bf16[16,64,128]{2,1,0:T(8,128)(2,1)}), bf16[16,64,128]{2,1,0:T(8,128)(2,1)S(1)}, u32[]{:S(2)}, u32[]{:S(2)}) async-start(bf16[16,64,128]{2,1,0:T(8,128)(2,1)} %sum_dom.1), calls=%async_computation.3 | async-start | bytes 524288 | tf_op jit(solution)/shard_map/all_to_all | solution.py:214
  133.7 16.2 %collective-permute-start.16 = (f32[128,256]{1,0:T(8,128)S(1)}, f32[128,256]{1,0:T(8,128)S(1)}, u32[]{:S(2)}, u32[]{:S(2)}) collective-permute-start(f32[128,256]{1,0:T(8,128)S(1)} %add_add_fusion.1), channel_id=1, source_target_pairs={{0,3},{1,0},{2,1},{3,2},{4,7},{5,4},{6,5},{7,6},{8,11},{9,8},{10,9... | collective-permute-start | bytes 393224 | tf_op jit(solution)/shard_map/ppermute | solution.py:225
  136.2 13.8 %collective-permute-start.15 = (f32[128,256]{1,0:T(8,128)S(1)}, f32[128,256]{1,0:T(8,128)S(1)}, u32[]{:S(2)}, u32[]{:S(2)}) collective-permute-start(f32[128,256]{1,0:T(8,128)S(1)} %add_add_fusion.1), channel_id=1, source_target_pairs={{0,2},{1,3},{2,0},{3,1},{4,6},{5,7},{6,4},{7,5},{8,10},{9,11},{10,... | collective-permute-start | bytes 393224 | tf_op jit(solution)/shard_map/ppermute | solution.py:225
  136.6 13.4 %collective-permute-start.14 = (f32[128,256]{1,0:T(8,128)S(1)}, f32[128,256]{1,0:T(8,128)S(1)}, u32[]{:S(2)}, u32[]{:S(2)}) collective-permute-start(f32[128,256]{1,0:T(8,128)S(1)} %add_add_fusion.1), channel_id=1, source_target_pairs={{0,1},{1,2},{2,3},{3,0},{4,5},{5,6},{6,7},{7,4},{8,9},{9,10},{10,1... | collective-permute-start | bytes 393224 | tf_op jit(solution)/shard_map/ppermute | solution.py:225
  143.7 14.2 %all-to-all-start.4 = ((bf16[16,64,128]{2,1,0:T(8,128)(2,1)}), bf16[16,64,128]{2,1,0:T(8,128)(2,1)S(1)}, u32[]{:S(2)}, u32[]{:S(2)}) async-start(bf16[16,64,128]{2,1,0:T(8,128)(2,1)} %sum_feat.1), calls=%async_computation.4 | async-start | bytes 524288 | tf_op jit(solution)/shard_map/all_to_all | solution.py:214
  (9 other events, 134.9 us)

commit v9 on v8

--- a/solution.py
+++ b/solution.py
@@ -284,7 +284,15 @@
     from_dom, last = lax.optimization_barrier((from_dom, ring[-3]))
     ring[-4] = turn(last, 1)
     two = call(first_sum_body, "sum_dom", shape((NF, 64, 128), BF), [VMEM])(from_dom)
-    two, ring[-4] = lax.optimization_barrier((two, ring[-4]))
+    layer_out = call(
+        layer_body,
+        "layer_two",
+        shape((SEEDS, HID), BF),
+        [SMEM] + [VMEM] * 4,
+        hot,
+        us=5,
+    )(counts, names, from_dom, part, w2_neigh)
+    two, ring[-4], layer_out = lax.optimization_barrier((two, ring[-4], layer_out))
     two = swap(two, "feat")
     keep, give = call(
         columns_body,
@@ -295,16 +303,9 @@
     )(chip, rows, *[ring[i] for i in RING])
     one = keep + fetch(give, 1)
     one = one + sum(along(one, 4 * i) for i in range(1, 4))
+    one, two = lax.optimization_barrier((one, two))
     one = one + sum(along(one, i) for i in range(1, 4))
-    layer_out = call(
-        layer_body,
-        "layer_two",
-        shape((SEEDS, HID), BF),
-        [SMEM] + [VMEM] * 4,
-        hot,
-        us=5,
-    )(counts, names, from_dom, part, w2_neigh)
-    done = call(second_sum_body, "sum_feat", shape((ND, 64, 128), BF), [VMEM], limit=60)(two)
+    done = call(second_sum_body, "sum_feat", shape((ND, 64, 128), BF), [VMEM])(two)
     done = swap(done, "dom")
     second = shape((HID, HID), F32)
     two_self, two_neigh = call(place_body, "place", (second, second), [VMEM])(done)

time: 159 us -> 156 us (0.981)
    ppermute x6, waiting for transfers between devices: 4.05 us -> 10.7 us  [along(): return lax.ppermute(x, 'dom', pairs)]
    ppermute x7, waiting for transfers between devices: 15.5 us -> 12.1 us  [turn(): lax.ppermute(x, 'feat', [(i, (i + 2 * step) % NF) for i in range(NF)])]
    all_to_all x4, waiting for transfers between devices: 8.9 us -> 5.67 us  [swap(): lax.all_to_all(x, axis, split_axis=0, concat_axis=0, tiled=True, axis_ind...]
    all_to_all x4, starting transfers between devices: 22.2 us -> 20.3 us  [swap(): lax.all_to_all(x, axis, split_axis=0, concat_axis=0, tiled=True, axis_ind...]
where the time goes in v9:
time: 156 us; the launch traced here: 155 us
  starting transfers between devices  45.5 us (29%)
  Pallas kernels  39.2 us (25%)
  blocking collectives  39.1 us (25%)
  waiting for transfers between devices  28.4 us (18%)
  local copies, waits for them, and re-layouts  1.72 us (1%)
    all_to_all x1, blocking collectives, swap(): lax.all_to_all(x, axis, split_axis=0, concat_axis=0, tiled=True, axis_ind...  39.1 us
    pallas_call x1, Pallas kernels, per_device(): call(rows_body, 'node_rows', (rows, rows), [SMEM, VMEM, VMEM, SMEM] + [VM...  25.7 us
    all_to_all x4, starting transfers between devices, swap(): lax.all_to_all(x, axis, split_axis=0, concat_axis=0, tiled=True, axis_ind...  20.3 us
    ppermute x7, waiting for transfers between devices, turn(): lax.ppermute(x, 'feat', [(i, (i + 2 * step) % NF) for i in range(NF)])  12.1 us
    ppermute x4, starting transfers between devices, fetch(): return lax.ppermute(x, 'feat', [(i, i ^ bit) for i in range(NF)])  10.7 us
    ppermute x6, waiting for transfers between devices, along(): return lax.ppermute(x, 'dom', pairs)  10.7 us
    ppermute x6, starting transfers between devices, along(): return lax.ppermute(x, 'dom', pairs)  7.63 us
    ppermute x7, starting transfers between devices, turn(): lax.ppermute(x, 'feat', [(i, (i + 2 * step) % NF) for i in range(NF)])  6.92 us
  transfers between devices with their start and end apart: 21, of which 12 were waited for; matrix products, arithmetic and copies ran while one was open for 0% of the time, Pallas kernels for 22%

profile of v9, /device:TPU:1, one launch (start us, length us, event | category | flops | bytes accessed | tf_op | source)
XLA Modules:
  0.0 154.9 jit_solution(16326989025610916243)
XLA Ops:
  0.6 3.3 %collective-permute-start = (bf16[64,9216]{1,0:T(8,128)(2,1)}, bf16[64,9216]{1,0:T(8,128)(2,1)S(1)}, u32[]{:S(2)}, u32[]{:S(2)}) collective-permute-start(bf16[64,9216]{1,0:T(8,128)(2,1)} %bitcast.20), channel_id=1, source_target_pairs={{0,16},{16,0},{32,48},{48,32},{64,80},{80,64},{96,112},{112,96},{1... | collective-permute-start | bytes 3538952 | tf_op jit(solution)/shard_map/ppermute | solution.py:229
  4.5 3.8 %picks.1 = bf16[16,128,256]{2,1,0:T(8,128)(2,1)} custom-call(s32[16]{0:T(128)} %bitcast.18, s32[15,1,256]{2,1,0:T(1,128)} %bitcast.14, bf16[256,256]{1,0:T(8,128)(2,1)} %bitcast.12), custom_call_target="tpu_custom_call" | custom-call | flops 4000000000 | bytes 4000000 | tf_op jit(solution)/shard_map/picks/pallas_call | solution.py:251
  8.3 5.0 %all-to-all-start.1 = ((bf16[16,128,256]{2,1,0:T(8,128)(2,1)}), bf16[16,128,256]{2,1,0:T(8,128)(2,1)S(1)}, u32[]{:S(2)}, u32[]{:S(2)}) async-start(bf16[16,128,256]{2,1,0:T(8,128)(2,1)} %picks.1), calls=%async_computation.1 | async-start | bytes 2097152 | tf_op jit(solution)/shard_map/all_to_all | solution.py:214
  14.4 25.7 %node_rows.1 = (bf16[8,288,256]{2,1,0:T(8,128)(2,1)}, bf16[8,288,256]{2,1,0:T(8,128)(2,1)}) custom-call(s32[1]{0:T(128)} %bitcast.core_ref, bf16[64,9216]{1,0:T(8,128)(2,1)} %bitcast.21, bf16[64,9216]{1,0:T(8,128)(2,1)} %copy-done.8, s32[46080]{0:T(1024)} %bitcast.22, bf16[64,256]{1,0:T(8,128)(2,1)} %ws_ref.1, bf16[64,256]{1,0:T(8,128)(2,1)} %wn_ref.1, ...), custom_call_target="tpu_custom_call" | custom-call | flops 22000001024 | bytes 22000000 | tf_op jit(solution)/shard_map/node_rows/pallas_call | solution.py:257
  40.2 39.1 %all_to_all.25.share_ref = bf16[8,288,256]{2,1,0:T(8,128)(2,1)S(1)} all-to-all(bf16[8,288,256]{2,1,0:T(8,128)(2,1)} %get-tuple-element.27), channel_id=1, replica_groups={{0,32,64,96,128,160,192,224},{16,48,80,112,144,176,208,240},{1,33,65,97..., dimensions={0} | all-to-all | bytes 2359296 | tf_op jit(solution)/shard_map/all_to_all | solution.py:214
  79.3 3.1 %project.1 = (bf16[16,320,128]{2,1,0:T(8,128)(2,1)}, f32[256,256]{1,0:T(8,128)S(1)}, bf16[288,256]{1,0:T(8,128)(2,1)S(1)}) custom-call(bf16[8,288,256]{2,1,0:T(8,128)(2,1)S(1)} %all_to_all.25.share_ref, bf16[16,128,256]{2,1,0:T(8,128)(2,1)S(1)} %all-to-all-done.1.in_ref, s32[16,128]{1,0:T(8,128)S(1)} %bitcast.16, s32[1,256]{1,0:T(1,128)S(1)} %bitcast.17, ...), custom_call_target="tpu_custom_call" | custom-call | flops 4000000000 | bytes 4000000 | tf_op jit(solution)/shard_map/project/pallas_call | solution.py:268
  82.5 6.4 %all-to-all-start.2 = ((bf16[16,320,128]{2,1,0:T(8,128)(2,1)}), bf16[16,320,128]{2,1,0:T(8,128)(2,1)S(1)}, u32[]{:S(2)}, u32[]{:S(2)}) async-start(bf16[16,320,128]{2,1,0:T(8,128)(2,1)} %get-tuple-element.28), calls=%async_computation.2 | async-start | bytes 2621440 | tf_op jit(solution)/shard_map/all_to_all | solution.py:214
  89.0 1.5 collective-permute-start.3
  90.5 2.5 %collective-permute-done.4.refs_2_ = bf16[288,256]{1,0:T(8,128)(2,1)S(1)} collective-permute-done((bf16[288,256]{1,0:T(8,128)(2,1)S(1)}, bf16[288,256]{1,0:T(8,128)(2,1)S(1)}, u32[]{:S(2)}, u32[]{:S(2)}) %collective-permute-start.4) | collective-permute-done | bytes 147488 | tf_op jit(solution)/shard_map/ppermute | solution.py:220
  94.5 2.5 %collective-permute-start.6 = (bf16[288,256]{1,0:T(8,128)(2,1)S(1)}, bf16[288,256]{1,0:T(8,128)(2,1)S(1)}, u32[]{:S(2)}, u32[]{:S(2)}) collective-permute-start(bf16[288,256]{1,0:T(8,128)(2,1)S(1)} %collective-permute-done.4.refs_2_), channel_id=1, source_target_pairs={{0,224},{16,240},{32,0},{48,16},{64,32},{80,48},{96,64},{112,80},{... | collective-permute-start | bytes 442376 | tf_op jit(solution)/shard_map/ppermute | solution.py:220
  97.0 2.8 %collective-permute-done.5.refs_3_ = bf16[288,256]{1,0:T(8,128)(2,1)S(1)} collective-permute-done((bf16[288,256]{1,0:T(8,128)(2,1)S(1)}, bf16[288,256]{1,0:T(8,128)(2,1)S(1)}, u32[]{:S(2)}, u32[]{:S(2)}) %collective-permute-start.5) | collective-permute-done | bytes 147488 | tf_op jit(solution)/shard_map/ppermute | solution.py:220
  99.8 2.7 %collective-permute-start.8 = (bf16[288,256]{1,0:T(8,128)(2,1)S(1)}, bf16[288,256]{1,0:T(8,128)(2,1)S(1)}, u32[]{:S(2)}, u32[]{:S(2)}) collective-permute-start(bf16[288,256]{1,0:T(8,128)(2,1)S(1)} %collective-permute-done.6.refs_4_), channel_id=1, source_target_pairs={{0,224},{16,240},{32,0},{48,16},{64,32},{80,48},{96,64},{112,80},{... | collective-permute-start | bytes 442376 | tf_op jit(solution)/shard_map/ppermute | solution.py:220
  102.5 2.7 %collective-permute-done.7.refs_5_ = bf16[288,256]{1,0:T(8,128)(2,1)S(1)} collective-permute-done((bf16[288,256]{1,0:T(8,128)(2,1)S(1)}, bf16[288,256]{1,0:T(8,128)(2,1)S(1)}, u32[]{:S(2)}, u32[]{:S(2)}) %collective-permute-start.7) | collective-permute-done | bytes 147488 | tf_op jit(solution)/shard_map/ppermute | solution.py:220
  106.4 3.5 %layer_two.1 = bf16[256,256]{1,0:T(8,128)(2,1)} custom-call(s32[16]{0:T(128)S(1)} %bitcast.19, s32[15,1,256]{2,1,0:T(1,128)S(1)} %bitcast.15, bf16[16,320,128]{2,1,0:T(8,128)(2,1)S(1)} %all-to-all-done.2.in_ref, f32[256,256]{1,0:T(8,128)S(1)} %get-tuple-element.37.part_ref, bf16[256,256]{1,0:T(8,128)(2,1)S(1)} %copy-done.2), custom_call_target="tpu_custom_call" | custom-call | flops 5000000000 | bytes 5000000 | tf_op jit(solution)/shard_map/layer_two/pallas_call | solution.py:287
  110.6 2.4 %collective-permute-done.9.refs_7_ = bf16[288,256]{1,0:T(8,128)(2,1)S(1)} collective-permute-done((bf16[288,256]{1,0:T(8,128)(2,1)S(1)}, bf16[288,256]{1,0:T(8,128)(2,1)S(1)}, u32[]{:S(2)}, u32[]{:S(2)}) %collective-permute-start.9) | collective-permute-done | bytes 147488 | tf_op jit(solution)/shard_map/ppermute | solution.py:220
  113.8 6.8 %collective-permute-start.10 = (f32[128,256]{1,0:T(8,128)S(1)}, f32[128,256]{1,0:T(8,128)S(1)}, u32[]{:S(2)}, u32[]{:S(2)}) collective-permute-start(f32[128,256]{1,0:T(8,128)S(1)} %get-tuple-element.43), channel_id=1, source_target_pairs={{0,16},{16,0},{32,48},{48,32},{64,80},{80,64},{96,112},{112,96},{1... | collective-permute-start | bytes 393224 | tf_op jit(solution)/shard_map/ppermute | solution.py:229
  120.7 3.4 %all-to-all-start.3 = ((bf16[16,64,128]{2,1,0:T(8,128)(2,1)}), bf16[16,64,128]{2,1,0:T(8,128)(2,1)S(1)}, u32[]{:S(2)}, u32[]{:S(2)}) async-start(bf16[16,64,128]{2,1,0:T(8,128)(2,1)} %sum_dom.1), calls=%async_computation.3 | async-start | bytes 524288 | tf_op jit(solution)/shard_map/all_to_all | solution.py:214
  124.1 2.6 %collective-permute-start.13 = (f32[128,256]{1,0:T(8,128)S(1)}, f32[128,256]{1,0:T(8,128)S(1)}, u32[]{:S(2)}, u32[]{:S(2)}) collective-permute-start(f32[128,256]{1,0:T(8,128)S(1)} %add.21), channel_id=1, source_target_pairs={{0,12},{1,13},{2,14},{3,15},{4,0},{5,1},{6,2},{7,3},{8,4},{9,5},{1... | collective-permute-start | bytes 393224 | tf_op jit(solution)/shard_map/ppermute | solution.py:225
  128.0 4.2 %collective-permute-done.13 = f32[128,256]{1,0:T(8,128)S(1)} collective-permute-done((f32[128,256]{1,0:T(8,128)S(1)}, f32[128,256]{1,0:T(8,128)S(1)}, u32[]{:S(2)}, u32[]{:S(2)}) %collective-permute-start.13) | collective-permute-done | bytes 131104 | tf_op jit(solution)/shard_map/ppermute | solution.py:225
  133.0 3.5 %collective-permute-done.11 = f32[128,256]{1,0:T(8,128)S(1)} collective-permute-done((f32[128,256]{1,0:T(8,128)S(1)}, f32[128,256]{1,0:T(8,128)S(1)}, u32[]{:S(2)}, u32[]{:S(2)}) %collective-permute-start.11) | collective-permute-done | bytes 131104 | tf_op jit(solution)/shard_map/ppermute | solution.py:225
  136.5 2.5 %collective-permute-start.16 = (f32[128,256]{1,0:T(8,128)S(1)}, f32[128,256]{1,0:T(8,128)S(1)}, u32[]{:S(2)}, u32[]{:S(2)}) collective-permute-start(f32[128,256]{1,0:T(8,128)S(1)} %add_add_fusion.1), channel_id=1, source_target_pairs={{0,3},{1,0},{2,1},{3,2},{4,7},{5,4},{6,5},{7,6},{8,11},{9,8},{10,9... | collective-permute-start | bytes 393224 | tf_op jit(solution)/shard_map/ppermute | solution.py:225
  141.0 5.4 %all-to-all-start.4 = ((bf16[16,64,128]{2,1,0:T(8,128)(2,1)}), bf16[16,64,128]{2,1,0:T(8,128)(2,1)S(1)}, u32[]{:S(2)}, u32[]{:S(2)}) async-start(bf16[16,64,128]{2,1,0:T(8,128)(2,1)} %sum_feat.1), calls=%async_computation.4 | async-start | bytes 524288 | tf_op jit(solution)/shard_map/all_to_all | solution.py:214
  146.4 2.2 %collective-permute-done.14 = f32[128,256]{1,0:T(8,128)S(1)} collective-permute-done((f32[128,256]{1,0:T(8,128)S(1)}, f32[128,256]{1,0:T(8,128)S(1)}, u32[]{:S(2)}, u32[]{:S(2)}) %collective-permute-start.14) | collective-permute-done | bytes 131104 | tf_op jit(solution)/shard_map/ppermute | solution.py:225
  149.3 4.8 %all-to-all-done.4.in_ref = bf16[16,64,128]{2,1,0:T(8,128)(2,1)S(1)} async-done(((bf16[16,64,128]{2,1,0:T(8,128)(2,1)}), bf16[16,64,128]{2,1,0:T(8,128)(2,1)S(1)}, u32[]{:S(2)}, u32[]{:S(2)}) %all-to-all-start.4) | async-done | bytes 262176 | tf_op jit(solution)/shard_map/all_to_all | solution.py:214
  (53 shorter events, 11.5 us)
Async XLA Ops:
  0.6 12.8 %collective-permute-start = (bf16[64,9216]{1,0:T(8,128)(2,1)}, bf16[64,9216]{1,0:T(8,128)(2,1)S(1)}, u32[]{:S(2)}, u32[]{:S(2)}) collective-permute-start(bf16[64,9216]{1,0:T(8,128)(2,1)} %bitcast.20), channel_id=1, source_target_pairs={{0,16},{16,0},{32,48},{48,32},{64,80},{80,64},{96,112},{112,96},{1... | collective-permute-start | bytes 3538952 | tf_op jit(solution)/shard_map/ppermute | solution.py:229
  4.0 9.4 %collective-permute-start.1 = (bf16[64,256]{1,0:T(8,128)(2,1)}, bf16[64,256]{1,0:T(8,128)(2,1)S(1)}, u32[]{:S(2)}, u32[]{:S(2)}) collective-permute-start(bf16[64,256]{1,0:T(8,128)(2,1)} %ws_ref.1), channel_id=1, source_target_pairs={{0,16},{16,0},{32,48},{48,32},{64,80},{80,64},{96,112},{112,96},{1... | collective-permute-start | bytes 98312 | tf_op jit(solution)/shard_map/ppermute | solution.py:229
  4.1 9.3 %collective-permute-start.2 = (bf16[64,256]{1,0:T(8,128)(2,1)}, bf16[64,256]{1,0:T(8,128)(2,1)S(1)}, u32[]{:S(2)}, u32[]{:S(2)}) collective-permute-start(bf16[64,256]{1,0:T(8,128)(2,1)} %wn_ref.1), channel_id=1, source_target_pairs={{0,16},{16,0},{32,48},{48,32},{64,80},{80,64},{96,112},{112,96},{1... | collective-permute-start | bytes 98312 | tf_op jit(solution)/shard_map/ppermute | solution.py:229
  8.3 31.8 %all-to-all-start.1 = ((bf16[16,128,256]{2,1,0:T(8,128)(2,1)}), bf16[16,128,256]{2,1,0:T(8,128)(2,1)S(1)}, u32[]{:S(2)}, u32[]{:S(2)}) async-start(bf16[16,128,256]{2,1,0:T(8,128)(2,1)} %picks.1), calls=%async_computation.1 | async-start | bytes 2097152 | tf_op jit(solution)/shard_map/all_to_all | solution.py:214
  40.1 39.2 %copy-start = (bf16[1,1,256,256]{3,2,1,0:T(8,128)(2,1)S(1)}, bf16[1,1,256,256]{3,2,1,0:T(8,128)(2,1)}, u32[]{:S(2)}) copy-start(bf16[1,1,256,256]{3,2,1,0:T(8,128)(2,1)} %param.21) | copy-start | bytes 393220
  40.1 39.2 %copy-start.1 = (bf16[256,256]{1,0:T(8,128)(2,1)S(1)}, bf16[256,256]{1,0:T(8,128)(2,1)}, u32[]{:S(2)}) copy-start(bf16[256,256]{1,0:T(8,128)(2,1)} %w2s_ref.1) | copy-start | bytes 393220
  40.2 39.2 %copy-start.2 = (bf16[256,256]{1,0:T(8,128)(2,1)S(1)}, bf16[256,256]{1,0:T(8,128)(2,1)}, u32[]{:S(2)}) copy-start(bf16[256,256]{1,0:T(8,128)(2,1)} %w2n_ref.3) | copy-start | bytes 393220
  82.5 23.9 %all-to-all-start.2 = ((bf16[16,320,128]{2,1,0:T(8,128)(2,1)}), bf16[16,320,128]{2,1,0:T(8,128)(2,1)S(1)}, u32[]{:S(2)}, u32[]{:S(2)}) async-start(bf16[16,320,128]{2,1,0:T(8,128)(2,1)} %get-tuple-element.28), calls=%async_computation.2 | async-start | bytes 2621440 | tf_op jit(solution)/shard_map/all_to_all | solution.py:214
  88.9 4.1 %collective-permute-start.4 = (bf16[288,256]{1,0:T(8,128)(2,1)S(1)}, bf16[288,256]{1,0:T(8,128)(2,1)S(1)}, u32[]{:S(2)}, u32[]{:S(2)}) collective-permute-start(bf16[288,256]{1,0:T(8,128)(2,1)S(1)} %get-tuple-element.29.refs_0_), channel_id=1, source_target_pairs={{0,224},{16,240},{32,0},{48,16},{64,32},{80,48},{96,64},{112,80},{... | collective-permute-start | bytes 442376 | tf_op jit(solution)/shard_map/ppermute | solution.py:220
  89.0 5.3 %collective-permute-start.3 = (bf16[288,256]{1,0:T(8,128)(2,1)S(1)}, bf16[288,256]{1,0:T(8,128)(2,1)S(1)}, u32[]{:S(2)}, u32[]{:S(2)}) collective-permute-start(bf16[288,256]{1,0:T(8,128)(2,1)S(1)} %get-tuple-element.29.refs_0_), channel_id=1, source_target_pairs={{0,32},{16,48},{32,64},{48,80},{64,96},{80,112},{96,128},{112,144}... | collective-permute-start | bytes 442376 | tf_op jit(solution)/shard_map/ppermute | solution.py:220
  94.3 5.5 %collective-permute-start.5 = (bf16[288,256]{1,0:T(8,128)(2,1)S(1)}, bf16[288,256]{1,0:T(8,128)(2,1)S(1)}, u32[]{:S(2)}, u32[]{:S(2)}) collective-permute-start(bf16[288,256]{1,0:T(8,128)(2,1)S(1)} %collective-permute-done.3.refs_1_), channel_id=1, source_target_pairs={{0,32},{16,48},{32,64},{48,80},{64,96},{80,112},{96,128},{112,144}... | collective-permute-start | bytes 442376 | tf_op jit(solution)/shard_map/ppermute | solution.py:220
  94.5 5.3 %collective-permute-start.6 = (bf16[288,256]{1,0:T(8,128)(2,1)S(1)}, bf16[288,256]{1,0:T(8,128)(2,1)S(1)}, u32[]{:S(2)}, u32[]{:S(2)}) collective-permute-start(bf16[288,256]{1,0:T(8,128)(2,1)S(1)} %collective-permute-done.4.refs_2_), channel_id=1, source_target_pairs={{0,224},{16,240},{32,0},{48,16},{64,32},{80,48},{96,64},{112,80},{... | collective-permute-start | bytes 442376 | tf_op jit(solution)/shard_map/ppermute | solution.py:220
  99.8 5.4 %collective-permute-start.7 = (bf16[288,256]{1,0:T(8,128)(2,1)S(1)}, bf16[288,256]{1,0:T(8,128)(2,1)S(1)}, u32[]{:S(2)}, u32[]{:S(2)}) collective-permute-start(bf16[288,256]{1,0:T(8,128)(2,1)S(1)} %collective-permute-done.5.refs_3_), channel_id=1, source_target_pairs={{0,32},{16,48},{32,64},{48,80},{64,96},{80,112},{96,128},{112,144}... | collective-permute-start | bytes 442376 | tf_op jit(solution)/shard_map/ppermute | solution.py:220
  99.8 5.7 %collective-permute-start.8 = (bf16[288,256]{1,0:T(8,128)(2,1)S(1)}, bf16[288,256]{1,0:T(8,128)(2,1)S(1)}, u32[]{:S(2)}, u32[]{:S(2)}) collective-permute-start(bf16[288,256]{1,0:T(8,128)(2,1)S(1)} %collective-permute-done.6.refs_4_), channel_id=1, source_target_pairs={{0,224},{16,240},{32,0},{48,16},{64,32},{80,48},{96,64},{112,80},{... | collective-permute-start | bytes 442376 | tf_op jit(solution)/shard_map/ppermute | solution.py:220
  106.4 6.7 %collective-permute-start.9 = (bf16[288,256]{1,0:T(8,128)(2,1)S(1)}, bf16[288,256]{1,0:T(8,128)(2,1)S(1)}, u32[]{:S(2)}, u32[]{:S(2)}) collective-permute-start(bf16[288,256]{1,0:T(8,128)(2,1)S(1)} %collective-permute-done.7.refs_5_), channel_id=1, source_target_pairs={{0,32},{16,48},{32,64},{48,80},{64,96},{80,112},{96,128},{112,144}... | collective-permute-start | bytes 442376 | tf_op jit(solution)/shard_map/ppermute | solution.py:220
  113.8 10.3 %collective-permute-start.10 = (f32[128,256]{1,0:T(8,128)S(1)}, f32[128,256]{1,0:T(8,128)S(1)}, u32[]{:S(2)}, u32[]{:S(2)}) collective-permute-start(f32[128,256]{1,0:T(8,128)S(1)} %get-tuple-element.43), channel_id=1, source_target_pairs={{0,16},{16,0},{32,48},{48,32},{64,80},{80,64},{96,112},{112,96},{1... | collective-permute-start | bytes 393224 | tf_op jit(solution)/shard_map/ppermute | solution.py:229
  120.7 15.8 %all-to-all-start.3 = ((bf16[16,64,128]{2,1,0:T(8,128)(2,1)}), bf16[16,64,128]{2,1,0:T(8,128)(2,1)S(1)}, u32[]{:S(2)}, u32[]{:S(2)}) async-start(bf16[16,64,128]{2,1,0:T(8,128)(2,1)} %sum_dom.1), calls=%async_computation.3 | async-start | bytes 524288 | tf_op jit(solution)/shard_map/all_to_all | solution.py:214
  124.1 8.1 %collective-permute-start.13 = (f32[128,256]{1,0:T(8,128)S(1)}, f32[128,256]{1,0:T(8,128)S(1)}, u32[]{:S(2)}, u32[]{:S(2)}) collective-permute-start(f32[128,256]{1,0:T(8,128)S(1)} %add.21), channel_id=1, source_target_pairs={{0,12},{1,13},{2,14},{3,15},{4,0},{5,1},{6,2},{7,3},{8,4},{9,5},{1... | collective-permute-start | bytes 393224 | tf_op jit(solution)/shard_map/ppermute | solution.py:225
  126.7 6.2 %collective-permute-start.12 = (f32[128,256]{1,0:T(8,128)S(1)}, f32[128,256]{1,0:T(8,128)S(1)}, u32[]{:S(2)}, u32[]{:S(2)}) collective-permute-start(f32[128,256]{1,0:T(8,128)S(1)} %add.21), channel_id=1, source_target_pairs={{0,8},{1,9},{2,10},{3,11},{4,12},{5,13},{6,14},{7,15},{8,0},{9,1},... | collective-permute-start | bytes 393224 | tf_op jit(solution)/shard_map/ppermute | solution.py:225
  127.4 9.0 %collective-permute-start.11 = (f32[128,256]{1,0:T(8,128)S(1)}, f32[128,256]{1,0:T(8,128)S(1)}, u32[]{:S(2)}, u32[]{:S(2)}) collective-permute-start(f32[128,256]{1,0:T(8,128)S(1)} %add.21), channel_id=1, source_target_pairs={{0,4},{1,5},{2,6},{3,7},{4,8},{5,9},{6,10},{7,11},{8,12},{9,13},{1... | collective-permute-start | bytes 393224 | tf_op jit(solution)/shard_map/ppermute | solution.py:225
  136.5 9.9 %collective-permute-start.16 = (f32[128,256]{1,0:T(8,128)S(1)}, f32[128,256]{1,0:T(8,128)S(1)}, u32[]{:S(2)}, u32[]{:S(2)}) collective-permute-start(f32[128,256]{1,0:T(8,128)S(1)} %add_add_fusion.1), channel_id=1, source_target_pairs={{0,3},{1,0},{2,1},{3,2},{4,7},{5,4},{6,5},{7,6},{8,11},{9,8},{10,9... | collective-permute-start | bytes 393224 | tf_op jit(solution)/shard_map/ppermute | solution.py:225
  139.0 7.4 %collective-permute-start.15 = (f32[128,256]{1,0:T(8,128)S(1)}, f32[128,256]{1,0:T(8,128)S(1)}, u32[]{:S(2)}, u32[]{:S(2)}) collective-permute-start(f32[128,256]{1,0:T(8,128)S(1)} %add_add_fusion.1), channel_id=1, source_target_pairs={{0,2},{1,3},{2,0},{3,1},{4,6},{5,7},{6,4},{7,5},{8,10},{9,11},{10,... | collective-permute-start | bytes 393224 | tf_op jit(solution)/shard_map/ppermute | solution.py:225
  139.7 9.0 %collective-permute-start.14 = (f32[128,256]{1,0:T(8,128)S(1)}, f32[128,256]{1,0:T(8,128)S(1)}, u32[]{:S(2)}, u32[]{:S(2)}) collective-permute-start(f32[128,256]{1,0:T(8,128)S(1)} %add_add_fusion.1), channel_id=1, source_target_pairs={{0,1},{1,2},{2,3},{3,0},{4,5},{5,6},{6,7},{7,4},{8,9},{9,10},{10,1... | collective-permute-start | bytes 393224 | tf_op jit(solution)/shard_map/ppermute | solution.py:225
  141.0 13.1 %all-to-all-start.4 = ((bf16[16,64,128]{2,1,0:T(8,128)(2,1)}), bf16[16,64,128]{2,1,0:T(8,128)(2,1)S(1)}, u32[]{:S(2)}, u32[]{:S(2)}) async-start(bf16[16,64,128]{2,1,0:T(8,128)(2,1)} %sum_feat.1), calls=%async_computation.4 | async-start | bytes 524288 | tf_op jit(solution)/shard_map/all_to_all | solution.py:214
  (8 other events, 131.6 us)

commit v10 on v9

--- a/solution.py
+++ b/solution.py
@@ -131,9 +131,9 @@
     return high, low, d, d_hidden
 
 
-def main_body(
+def hidden_body(
     share_ref, in_ref, send_ref, seed_ref, dout_ref, w2s_ref, w2n_ref,
-    out_ref, part_ref, dpre_ref,
+    dpre_ref, hidden_ref, g2_ref,
 ):
     high, low, d, d_hidden = owner_grads(in_ref, send_ref, seed_ref, dout_ref, w2s_ref, w2n_ref)
     pre = share_ref[0].astype(F32)
@@ -142,12 +142,16 @@
     slope = jnp.exp(jnp.minimum(pre, 0.0))
     hidden = jnp.where(pre > 0, pre, slope - 1.0).astype(BF)
     dpre_ref[...] = (d_hidden * slope).astype(BF)
-    g2s = dot(hidden, d, 0, 0).astype(BF)
-    g2n = (dot(hidden, high, 0, 0) + dot(hidden, low, 0, 0)).astype(BF)
+    hidden_ref[...] = hidden
+    g2_ref[0:HID, :] = dot(hidden, d, 0, 0).astype(BF)
+    g2_ref[HID:, :] = (dot(hidden, high, 0, 0) + dot(hidden, low, 0, 0)).astype(BF)
+
+
+def outgoing_body(hidden_ref, g2_ref, send_ref, seed_ref, w2s_ref, out_ref, part_ref):
+    hidden = hidden_ref[...]
     for q in range(ND):
-        g = g2s if q < 8 else g2n
         for h in range(2):
-            piece = g[(q % 8) * 32 : (q % 8) * 32 + 32, h * 128 : (h + 1) * 128]
+            piece = g2_ref[q * 32 : q * 32 + 32, h * 128 : (h + 1) * 128]
             out_ref[q, G2 + h * 32 : G2 + h * 32 + 32, :] = piece
     row = lax.broadcasted_iota(I32, (OWN, SEEDS), 0)
     for q in range(0, ND, 2):
@@ -265,24 +269,26 @@
     )(core, own, other, neigh_one.reshape(-1), w1_self, w1_neigh, ws_other, wn_other)
     share = swap(share, "feat", chips)
 
-    to_dom, part, d_pre = call(
-        main_body,
-        "project",
-        (
-            shape((ND, G2 + 64, 128), BF),
-            shape((SEEDS, HID), F32),
-            shape((OWN, HID), BF),
-        ),
-        [VMEM] * 7,
-        us=4,
+    owned = shape((OWN, HID), BF)
+    d_pre, hidden, g2 = call(
+        hidden_body, "hidden", (owned, owned, shape((2 * HID, HID), BF)), [VMEM] * 7, us=2
     )(share, t_in, send, seeds, grad_out, w2_self, w2_neigh)
 
+    to_dom, part = call(
+        outgoing_body,
+        "outgoing",
+        (shape((ND, G2 + 64, 128), BF), shape((SEEDS, HID), F32)),
+        [VMEM] * 5,
+        us=2,
+    )(hidden, g2, send, seeds, w2_self)
+    ring = {0: d_pre}
+    ring[-1], ring[1] = lax.optimization_barrier((turn(d_pre, 1), turn(d_pre, -1)))
+    to_dom, ring[1] = lax.optimization_barrier((to_dom, ring[1]))
     from_dom = swap(to_dom, "dom")
-    ring = {0: d_pre}
-    for i in range(1, 4):
+    for i in range(2, 4):
         ring[-i], ring[i] = lax.optimization_barrier((turn(ring[1 - i], 1), turn(ring[i - 1], -1)))
-    from_dom, last = lax.optimization_barrier((from_dom, ring[-3]))
-    ring[-4] = turn(last, 1)
+    ring[-4] = turn(ring[-3], 1)
+    from_dom, ring[-4] = lax.optimization_barrier((from_dom, ring[-4]))
     two = call(first_sum_body, "sum_dom", shape((NF, 64, 128), BF), [VMEM])(from_dom)
     layer_out = call(
         layer_body,
@@ -292,7 +298,7 @@
         hot,
         us=5,
     )(counts, names, from_dom, part, w2_neigh)
-    two, ring[-4], layer_out = lax.optimization_barrier((two, ring[-4], layer_out))
+    two, ring[-4] = lax.optimization_barrier((two, ring[-4]))
     two = swap(two, "feat")
     keep, give = call(
         columns_body,
@@ -303,7 +309,7 @@
     )(chip, rows, *[ring[i] for i in RING])
     one = keep + fetch(give, 1)
     one = one + sum(along(one, 4 * i) for i in range(1, 4))
-    one, two = lax.optimization_barrier((one, two))
+    one, two, layer_out = lax.optimization_barrier((one, two, layer_out))
     one = one + sum(along(one, i) for i in range(1, 4))
     done = call(second_sum_body, "sum_feat", shape((ND, 64, 128), BF), [VMEM])(two)
     done = swap(done, "dom")

time: 156 us -> 155 us (level)
  waiting for transfers between devices: 28.4 us -> 25.4 us
  starting transfers between devices: 45.5 us -> 47.4 us
    ppermute x6, waiting for transfers between devices: 10.7 us -> 7.28 us  [along(): return lax.ppermute(x, 'dom', pairs)]
    pallas_call x1 -> x2, Pallas kernels: 3.15 us -> 3.43 us  [the longest x1 1.96 us: per_device(): call(outgoing_body, 'outgoing', (shape((ND, G2 + 64, 128), BF), shape((SE...]
  transfers between devices with their start and end apart: 21 -> 21, of which waited for: 12 -> 10; matrix products, arithmetic and copies ran while one was open for 0% -> 0% of each run, Pallas kernels for 22% -> 23%
where the time goes in v10:
time: 155 us
  starting transfers between devices  47.4 us (31%)
  Pallas kernels  39.4 us (25%)
  blocking collectives  39.1 us (25%)
  waiting for transfers between devices  25.4 us (16%)
  local copies, waits for them, and re-layouts  2.31 us (1%)
    all_to_all x1, blocking collectives, swap(): lax.all_to_all(x, axis, split_axis=0, concat_axis=0, tiled=True, axis_ind...  39.1 us
    pallas_call x1, Pallas kernels, per_device(): call(rows_body, 'node_rows', (rows, rows), [SMEM, VMEM, VMEM, SMEM] + [VM...  25.7 us
    all_to_all x4, starting transfers between devices, swap(): lax.all_to_all(x, axis, split_axis=0, concat_axis=0, tiled=True, axis_ind...  20.6 us
    ppermute x7, waiting for transfers between devices, turn(): lax.ppermute(x, 'feat', [(i, (i + 2 * step) % NF) for i in range(NF)])  13.4 us
    ppermute x4, starting transfers between devices, fetch(): return lax.ppermute(x, 'feat', [(i, i ^ bit) for i in range(NF)])  10.4 us
    ppermute x6, starting transfers between devices, along(): return lax.ppermute(x, 'dom', pairs)  8.34 us
    ppermute x7, starting transfers between devices, turn(): lax.ppermute(x, 'feat', [(i, (i + 2 * step) % NF) for i in range(NF)])  8.06 us
    ppermute x6, waiting for transfers between devices, along(): return lax.ppermute(x, 'dom', pairs)  7.28 us
  transfers between devices with their start and end apart: 21, of which 10 were waited for; matrix products, arithmetic and copies ran while one was open for 0% of the time, Pallas kernels for 23%

profile of v10, /device:TPU:1, one launch (start us, length us, event | category | flops | bytes accessed | tf_op | source)
XLA Modules:
  0.0 154.5 jit_solution(2029049352994000211)
XLA Ops:
  0.6 3.3 %collective-permute-start = (bf16[64,9216]{1,0:T(8,128)(2,1)}, bf16[64,9216]{1,0:T(8,128)(2,1)S(1)}, u32[]{:S(2)}, u32[]{:S(2)}) collective-permute-start(bf16[64,9216]{1,0:T(8,128)(2,1)} %bitcast.22), channel_id=1, source_target_pairs={{0,16},{16,0},{32,48},{48,32},{64,80},{80,64},{96,112},{112,96},{1... | collective-permute-start | bytes 3538952 | tf_op jit(solution)/shard_map/ppermute | solution.py:233
  4.5 3.8 %picks.1 = bf16[16,128,256]{2,1,0:T(8,128)(2,1)} custom-call(s32[16]{0:T(128)} %bitcast.20, s32[15,1,256]{2,1,0:T(1,128)} %bitcast.14, bf16[256,256]{1,0:T(8,128)(2,1)} %bitcast.12), custom_call_target="tpu_custom_call" | custom-call | flops 4000000000 | bytes 4000000 | tf_op jit(solution)/shard_map/picks/pallas_call | solution.py:255
  8.3 5.0 %all-to-all-start.1 = ((bf16[16,128,256]{2,1,0:T(8,128)(2,1)}), bf16[16,128,256]{2,1,0:T(8,128)(2,1)S(1)}, u32[]{:S(2)}, u32[]{:S(2)}) async-start(bf16[16,128,256]{2,1,0:T(8,128)(2,1)} %picks.1), calls=%async_computation.1 | async-start | bytes 2097152 | tf_op jit(solution)/shard_map/all_to_all | solution.py:218
  14.4 25.7 %node_rows.1 = (bf16[8,288,256]{2,1,0:T(8,128)(2,1)}, bf16[8,288,256]{2,1,0:T(8,128)(2,1)}) custom-call(s32[1]{0:T(128)} %bitcast.1.core_ref, bf16[64,9216]{1,0:T(8,128)(2,1)} %bitcast.23, bf16[64,9216]{1,0:T(8,128)(2,1)} %copy-done.8, s32[46080]{0:T(1024)} %bitcast.24, bf16[64,256]{1,0:T(8,128)(2,1)} %ws_ref.1, bf16[64,256]{1,0:T(8,128)(2,1)} %wn_ref.1, ...), custom_call_target="tpu_custom_call" | custom-call | flops 22000001024 | bytes 22000000 | tf_op jit(solution)/shard_map/node_rows/pallas_call | solution.py:261
  40.2 39.1 %all_to_all.25.share_ref = bf16[8,288,256]{2,1,0:T(8,128)(2,1)S(1)} all-to-all(bf16[8,288,256]{2,1,0:T(8,128)(2,1)} %get-tuple-element.32), channel_id=1, replica_groups={{0,32,64,96,128,160,192,224},{16,48,80,112,144,176,208,240},{1,33,65,97..., dimensions={0} | all-to-all | bytes 2359296 | tf_op jit(solution)/shard_map/all_to_all | solution.py:218
  79.3 1.5 hidden.1
  80.9 1.5 collective-permute-start.3
  82.3 2.0 %outgoing.1 = (bf16[16,320,128]{2,1,0:T(8,128)(2,1)}, f32[256,256]{1,0:T(8,128)S(1)}) custom-call(bf16[288,256]{1,0:T(8,128)(2,1)S(1)} %get-tuple-element.35.hidden_ref, bf16[512,256]{1,0:T(8,128)(2,1)S(1)} %get-tuple-element.36.g2_ref, s32[16,128]{1,0:T(8,128)S(1)} %bitcast.17, s32[1,256]{1,0:T(1,128)S(1)} %bitcast.19, bf16[256,256]{1,0:T(8,128)(2,1)S(1)} %copy-done.1), custom_call_target="tpu_custom_call" | custom-call | flops 2000000000 | bytes 2000000 | tf_op jit(solution)/shard_map/outgoing/pallas_call | solution.py:277
  84.9 1.3 collective-permute-done.3.refs_1_
  86.2 6.3 %all-to-all-start.2 = ((bf16[16,320,128]{2,1,0:T(8,128)(2,1)}), bf16[16,320,128]{2,1,0:T(8,128)(2,1)S(1)}, u32[]{:S(2)}, u32[]{:S(2)}) async-start(bf16[16,320,128]{2,1,0:T(8,128)(2,1)} %get-tuple-element.44), calls=%async_computation.2 | async-start | bytes 2621440 | tf_op jit(solution)/shard_map/all_to_all | solution.py:218
  93.0 2.2 %collective-permute-start.6 = (bf16[288,256]{1,0:T(8,128)(2,1)S(1)}, bf16[288,256]{1,0:T(8,128)(2,1)S(1)}, u32[]{:S(2)}, u32[]{:S(2)}) collective-permute-start(bf16[288,256]{1,0:T(8,128)(2,1)S(1)} %collective-permute-done.4.refs_2_), channel_id=1, source_target_pairs={{0,224},{16,240},{32,0},{48,16},{64,32},{80,48},{96,64},{112,80},{... | collective-permute-start | bytes 442376 | tf_op jit(solution)/shard_map/ppermute | solution.py:224
  95.2 2.5 %collective-permute-done.5.refs_3_ = bf16[288,256]{1,0:T(8,128)(2,1)S(1)} collective-permute-done((bf16[288,256]{1,0:T(8,128)(2,1)S(1)}, bf16[288,256]{1,0:T(8,128)(2,1)S(1)}, u32[]{:S(2)}, u32[]{:S(2)}) %collective-permute-start.5) | collective-permute-done | bytes 147488 | tf_op jit(solution)/shard_map/ppermute | solution.py:224
  97.8 3.0 %collective-permute-start.8 = (bf16[288,256]{1,0:T(8,128)(2,1)S(1)}, bf16[288,256]{1,0:T(8,128)(2,1)S(1)}, u32[]{:S(2)}, u32[]{:S(2)}) collective-permute-start(bf16[288,256]{1,0:T(8,128)(2,1)S(1)} %collective-permute-done.6.refs_4_), channel_id=1, source_target_pairs={{0,224},{16,240},{32,0},{48,16},{64,32},{80,48},{96,64},{112,80},{... | collective-permute-start | bytes 442376 | tf_op jit(solution)/shard_map/ppermute | solution.py:224
  100.7 2.8 %collective-permute-done.7.refs_5_ = bf16[288,256]{1,0:T(8,128)(2,1)S(1)} collective-permute-done((bf16[288,256]{1,0:T(8,128)(2,1)S(1)}, bf16[288,256]{1,0:T(8,128)(2,1)S(1)}, u32[]{:S(2)}, u32[]{:S(2)}) %collective-permute-start.7) | collective-permute-done | bytes 147488 | tf_op jit(solution)/shard_map/ppermute | solution.py:224
  104.4 6.2 %collective-permute-done.9.refs_7_ = bf16[288,256]{1,0:T(8,128)(2,1)S(1)} collective-permute-done((bf16[288,256]{1,0:T(8,128)(2,1)S(1)}, bf16[288,256]{1,0:T(8,128)(2,1)S(1)}, u32[]{:S(2)}, u32[]{:S(2)}) %collective-permute-start.9) | collective-permute-done | bytes 147488 | tf_op jit(solution)/shard_map/ppermute | solution.py:224
  112.7 6.5 %collective-permute-start.10 = (f32[128,256]{1,0:T(8,128)S(1)}, f32[128,256]{1,0:T(8,128)S(1)}, u32[]{:S(2)}, u32[]{:S(2)}) collective-permute-start(f32[128,256]{1,0:T(8,128)S(1)} %get-tuple-element.49), channel_id=1, source_target_pairs={{0,16},{16,0},{32,48},{48,32},{64,80},{80,64},{96,112},{112,96},{1... | collective-permute-start | bytes 393224 | tf_op jit(solution)/shard_map/ppermute | solution.py:233
  119.2 3.8 %all-to-all-start.3 = ((bf16[16,64,128]{2,1,0:T(8,128)(2,1)}), bf16[16,64,128]{2,1,0:T(8,128)(2,1)S(1)}, u32[]{:S(2)}, u32[]{:S(2)}) async-start(bf16[16,64,128]{2,1,0:T(8,128)(2,1)} %sum_dom.1), calls=%async_computation.3 | async-start | bytes 524288 | tf_op jit(solution)/shard_map/all_to_all | solution.py:218
  123.0 3.6 %collective-permute-start.13 = (f32[128,256]{1,0:T(8,128)S(1)}, f32[128,256]{1,0:T(8,128)S(1)}, u32[]{:S(2)}, u32[]{:S(2)}) collective-permute-start(f32[128,256]{1,0:T(8,128)S(1)} %add.21), channel_id=1, source_target_pairs={{0,12},{1,13},{2,14},{3,15},{4,0},{5,1},{6,2},{7,3},{8,4},{9,5},{1... | collective-permute-start | bytes 393224 | tf_op jit(solution)/shard_map/ppermute | solution.py:229
  127.7 3.4 %layer_two.1 = bf16[256,256]{1,0:T(8,128)(2,1)} custom-call(s32[16]{0:T(128)S(1)} %bitcast.21, s32[15,1,256]{2,1,0:T(1,128)S(1)} %bitcast.15, bf16[16,320,128]{2,1,0:T(8,128)(2,1)S(1)} %all-to-all-done.2.in_ref, f32[256,256]{1,0:T(8,128)S(1)} %get-tuple-element.51.part_ref, bf16[256,256]{1,0:T(8,128)(2,1)S(1)} %copy-done.2), custom_call_target="tpu_custom_call" | custom-call | flops 5000000000 | bytes 5000000 | tf_op jit(solution)/shard_map/layer_two/pallas_call | solution.py:293
  132.8 3.5 %collective-permute-done.11 = f32[128,256]{1,0:T(8,128)S(1)} collective-permute-done((f32[128,256]{1,0:T(8,128)S(1)}, f32[128,256]{1,0:T(8,128)S(1)}, u32[]{:S(2)}, u32[]{:S(2)}) %collective-permute-start.11) | collective-permute-done | bytes 131104 | tf_op jit(solution)/shard_map/ppermute | solution.py:229
  136.4 2.5 %collective-permute-start.16 = (f32[128,256]{1,0:T(8,128)S(1)}, f32[128,256]{1,0:T(8,128)S(1)}, u32[]{:S(2)}, u32[]{:S(2)}) collective-permute-start(f32[128,256]{1,0:T(8,128)S(1)} %add_add_fusion.1), channel_id=1, source_target_pairs={{0,3},{1,0},{2,1},{3,2},{4,7},{5,4},{6,5},{7,6},{8,11},{9,8},{10,9... | collective-permute-start | bytes 393224 | tf_op jit(solution)/shard_map/ppermute | solution.py:229
  140.7 5.5 %all-to-all-start.4 = ((bf16[16,64,128]{2,1,0:T(8,128)(2,1)}), bf16[16,64,128]{2,1,0:T(8,128)(2,1)S(1)}, u32[]{:S(2)}, u32[]{:S(2)}) async-start(bf16[16,64,128]{2,1,0:T(8,128)(2,1)} %sum_feat.1), calls=%async_computation.4 | async-start | bytes 524288 | tf_op jit(solution)/shard_map/all_to_all | solution.py:218
  146.2 2.1 %collective-permute-done.14 = f32[128,256]{1,0:T(8,128)S(1)} collective-permute-done((f32[128,256]{1,0:T(8,128)S(1)}, f32[128,256]{1,0:T(8,128)S(1)}, u32[]{:S(2)}, u32[]{:S(2)}) %collective-permute-start.14) | collective-permute-done | bytes 131104 | tf_op jit(solution)/shard_map/ppermute | solution.py:229
  149.0 4.7 %all-to-all-done.4.in_ref = bf16[16,64,128]{2,1,0:T(8,128)(2,1)S(1)} async-done(((bf16[16,64,128]{2,1,0:T(8,128)(2,1)}), bf16[16,64,128]{2,1,0:T(8,128)(2,1)S(1)}, u32[]{:S(2)}, u32[]{:S(2)}) %all-to-all-start.4) | async-done | bytes 262176 | tf_op jit(solution)/shard_map/all_to_all | solution.py:218
  (54 shorter events, 12.0 us)
Async XLA Ops:
  0.6 12.8 %collective-permute-start = (bf16[64,9216]{1,0:T(8,128)(2,1)}, bf16[64,9216]{1,0:T(8,128)(2,1)S(1)}, u32[]{:S(2)}, u32[]{:S(2)}) collective-permute-start(bf16[64,9216]{1,0:T(8,128)(2,1)} %bitcast.22), channel_id=1, source_target_pairs={{0,16},{16,0},{32,48},{48,32},{64,80},{80,64},{96,112},{112,96},{1... | collective-permute-start | bytes 3538952 | tf_op jit(solution)/shard_map/ppermute | solution.py:233
  4.0 9.4 %collective-permute-start.1 = (bf16[64,256]{1,0:T(8,128)(2,1)}, bf16[64,256]{1,0:T(8,128)(2,1)S(1)}, u32[]{:S(2)}, u32[]{:S(2)}) collective-permute-start(bf16[64,256]{1,0:T(8,128)(2,1)} %ws_ref.1), channel_id=1, source_target_pairs={{0,16},{16,0},{32,48},{48,32},{64,80},{80,64},{96,112},{112,96},{1... | collective-permute-start | bytes 98312 | tf_op jit(solution)/shard_map/ppermute | solution.py:233
  4.1 9.3 %collective-permute-start.2 = (bf16[64,256]{1,0:T(8,128)(2,1)}, bf16[64,256]{1,0:T(8,128)(2,1)S(1)}, u32[]{:S(2)}, u32[]{:S(2)}) collective-permute-start(bf16[64,256]{1,0:T(8,128)(2,1)} %wn_ref.1), channel_id=1, source_target_pairs={{0,16},{16,0},{32,48},{48,32},{64,80},{80,64},{96,112},{112,96},{1... | collective-permute-start | bytes 98312 | tf_op jit(solution)/shard_map/ppermute | solution.py:233
  8.3 31.8 %all-to-all-start.1 = ((bf16[16,128,256]{2,1,0:T(8,128)(2,1)}), bf16[16,128,256]{2,1,0:T(8,128)(2,1)S(1)}, u32[]{:S(2)}, u32[]{:S(2)}) async-start(bf16[16,128,256]{2,1,0:T(8,128)(2,1)} %picks.1), calls=%async_computation.1 | async-start | bytes 2097152 | tf_op jit(solution)/shard_map/all_to_all | solution.py:218
  40.1 39.2 %copy-start = (bf16[1,1,256,256]{3,2,1,0:T(8,128)(2,1)S(1)}, bf16[1,1,256,256]{3,2,1,0:T(8,128)(2,1)}, u32[]{:S(2)}) copy-start(bf16[1,1,256,256]{3,2,1,0:T(8,128)(2,1)} %param.21) | copy-start | bytes 393220
  40.1 39.2 %copy-start.1 = (bf16[256,256]{1,0:T(8,128)(2,1)S(1)}, bf16[256,256]{1,0:T(8,128)(2,1)}, u32[]{:S(2)}) copy-start(bf16[256,256]{1,0:T(8,128)(2,1)} %w2s_ref.3) | copy-start | bytes 393220
  40.1 39.2 %copy-start.2 = (bf16[256,256]{1,0:T(8,128)(2,1)S(1)}, bf16[256,256]{1,0:T(8,128)(2,1)}, u32[]{:S(2)}) copy-start(bf16[256,256]{1,0:T(8,128)(2,1)} %w2n_ref.3) | copy-start | bytes 393220
  80.8 4.1 %collective-permute-start.4 = (bf16[288,256]{1,0:T(8,128)(2,1)S(1)}, bf16[288,256]{1,0:T(8,128)(2,1)S(1)}, u32[]{:S(2)}, u32[]{:S(2)}) collective-permute-start(bf16[288,256]{1,0:T(8,128)(2,1)S(1)} %get-tuple-element.33.refs_0_), channel_id=1, source_target_pairs={{0,224},{16,240},{32,0},{48,16},{64,32},{80,48},{96,64},{112,80},{... | collective-permute-start | bytes 442376 | tf_op jit(solution)/shard_map/ppermute | solution.py:224
  80.9 5.3 %collective-permute-start.3 = (bf16[288,256]{1,0:T(8,128)(2,1)S(1)}, bf16[288,256]{1,0:T(8,128)(2,1)S(1)}, u32[]{:S(2)}, u32[]{:S(2)}) collective-permute-start(bf16[288,256]{1,0:T(8,128)(2,1)S(1)} %get-tuple-element.33.refs_0_), channel_id=1, source_target_pairs={{0,32},{16,48},{32,64},{48,80},{64,96},{80,112},{96,128},{112,144}... | collective-permute-start | bytes 442376 | tf_op jit(solution)/shard_map/ppermute | solution.py:224
  86.2 24.4 %all-to-all-start.2 = ((bf16[16,320,128]{2,1,0:T(8,128)(2,1)}), bf16[16,320,128]{2,1,0:T(8,128)(2,1)S(1)}, u32[]{:S(2)}, u32[]{:S(2)}) async-start(bf16[16,320,128]{2,1,0:T(8,128)(2,1)} %get-tuple-element.44), calls=%async_computation.2 | async-start | bytes 2621440 | tf_op jit(solution)/shard_map/all_to_all | solution.py:218
  92.5 5.3 %collective-permute-start.5 = (bf16[288,256]{1,0:T(8,128)(2,1)S(1)}, bf16[288,256]{1,0:T(8,128)(2,1)S(1)}, u32[]{:S(2)}, u32[]{:S(2)}) collective-permute-start(bf16[288,256]{1,0:T(8,128)(2,1)S(1)} %collective-permute-done.3.refs_1_), channel_id=1, source_target_pairs={{0,32},{16,48},{32,64},{48,80},{64,96},{80,112},{96,128},{112,144}... | collective-permute-start | bytes 442376 | tf_op jit(solution)/shard_map/ppermute | solution.py:224
  93.0 4.7 %collective-permute-start.6 = (bf16[288,256]{1,0:T(8,128)(2,1)S(1)}, bf16[288,256]{1,0:T(8,128)(2,1)S(1)}, u32[]{:S(2)}, u32[]{:S(2)}) collective-permute-start(bf16[288,256]{1,0:T(8,128)(2,1)S(1)} %collective-permute-done.4.refs_2_), channel_id=1, source_target_pairs={{0,224},{16,240},{32,0},{48,16},{64,32},{80,48},{96,64},{112,80},{... | collective-permute-start | bytes 442376 | tf_op jit(solution)/shard_map/ppermute | solution.py:224
  97.8 5.8 %collective-permute-start.7 = (bf16[288,256]{1,0:T(8,128)(2,1)S(1)}, bf16[288,256]{1,0:T(8,128)(2,1)S(1)}, u32[]{:S(2)}, u32[]{:S(2)}) collective-permute-start(bf16[288,256]{1,0:T(8,128)(2,1)S(1)} %collective-permute-done.5.refs_3_), channel_id=1, source_target_pairs={{0,32},{16,48},{32,64},{48,80},{64,96},{80,112},{96,128},{112,144}... | collective-permute-start | bytes 442376 | tf_op jit(solution)/shard_map/ppermute | solution.py:224
  97.8 5.8 %collective-permute-start.8 = (bf16[288,256]{1,0:T(8,128)(2,1)S(1)}, bf16[288,256]{1,0:T(8,128)(2,1)S(1)}, u32[]{:S(2)}, u32[]{:S(2)}) collective-permute-start(bf16[288,256]{1,0:T(8,128)(2,1)S(1)} %collective-permute-done.6.refs_4_), channel_id=1, source_target_pairs={{0,224},{16,240},{32,0},{48,16},{64,32},{80,48},{96,64},{112,80},{... | collective-permute-start | bytes 442376 | tf_op jit(solution)/shard_map/ppermute | solution.py:224
  103.6 7.0 %collective-permute-start.9 = (bf16[288,256]{1,0:T(8,128)(2,1)S(1)}, bf16[288,256]{1,0:T(8,128)(2,1)S(1)}, u32[]{:S(2)}, u32[]{:S(2)}) collective-permute-start(bf16[288,256]{1,0:T(8,128)(2,1)S(1)} %collective-permute-done.7.refs_5_), channel_id=1, source_target_pairs={{0,32},{16,48},{32,64},{48,80},{64,96},{80,112},{96,128},{112,144}... | collective-permute-start | bytes 442376 | tf_op jit(solution)/shard_map/ppermute | solution.py:224
  112.7 10.3 %collective-permute-start.10 = (f32[128,256]{1,0:T(8,128)S(1)}, f32[128,256]{1,0:T(8,128)S(1)}, u32[]{:S(2)}, u32[]{:S(2)}) collective-permute-start(f32[128,256]{1,0:T(8,128)S(1)} %get-tuple-element.49), channel_id=1, source_target_pairs={{0,16},{16,0},{32,48},{48,32},{64,80},{80,64},{96,112},{112,96},{1... | collective-permute-start | bytes 393224 | tf_op jit(solution)/shard_map/ppermute | solution.py:233
  119.2 17.2 %all-to-all-start.3 = ((bf16[16,64,128]{2,1,0:T(8,128)(2,1)}), bf16[16,64,128]{2,1,0:T(8,128)(2,1)S(1)}, u32[]{:S(2)}, u32[]{:S(2)}) async-start(bf16[16,64,128]{2,1,0:T(8,128)(2,1)} %sum_dom.1), calls=%async_computation.3 | async-start | bytes 524288 | tf_op jit(solution)/shard_map/all_to_all | solution.py:218
  123.0 9.1 %collective-permute-start.13 = (f32[128,256]{1,0:T(8,128)S(1)}, f32[128,256]{1,0:T(8,128)S(1)}, u32[]{:S(2)}, u32[]{:S(2)}) collective-permute-start(f32[128,256]{1,0:T(8,128)S(1)} %add.21), channel_id=1, source_target_pairs={{0,12},{1,13},{2,14},{3,15},{4,0},{5,1},{6,2},{7,3},{8,4},{9,5},{1... | collective-permute-start | bytes 393224 | tf_op jit(solution)/shard_map/ppermute | solution.py:229
  126.6 6.3 %collective-permute-start.12 = (f32[128,256]{1,0:T(8,128)S(1)}, f32[128,256]{1,0:T(8,128)S(1)}, u32[]{:S(2)}, u32[]{:S(2)}) collective-permute-start(f32[128,256]{1,0:T(8,128)S(1)} %add.21), channel_id=1, source_target_pairs={{0,8},{1,9},{2,10},{3,11},{4,12},{5,13},{6,14},{7,15},{8,0},{9,1},... | collective-permute-start | bytes 393224 | tf_op jit(solution)/shard_map/ppermute | solution.py:229
  127.2 9.2 %collective-permute-start.11 = (f32[128,256]{1,0:T(8,128)S(1)}, f32[128,256]{1,0:T(8,128)S(1)}, u32[]{:S(2)}, u32[]{:S(2)}) collective-permute-start(f32[128,256]{1,0:T(8,128)S(1)} %add.21), channel_id=1, source_target_pairs={{0,4},{1,5},{2,6},{3,7},{4,8},{5,9},{6,10},{7,11},{8,12},{9,13},{1... | collective-permute-start | bytes 393224 | tf_op jit(solution)/shard_map/ppermute | solution.py:229
  136.4 9.9 %collective-permute-start.16 = (f32[128,256]{1,0:T(8,128)S(1)}, f32[128,256]{1,0:T(8,128)S(1)}, u32[]{:S(2)}, u32[]{:S(2)}) collective-permute-start(f32[128,256]{1,0:T(8,128)S(1)} %add_add_fusion.1), channel_id=1, source_target_pairs={{0,3},{1,0},{2,1},{3,2},{4,7},{5,4},{6,5},{7,6},{8,11},{9,8},{10,9... | collective-permute-start | bytes 393224 | tf_op jit(solution)/shard_map/ppermute | solution.py:229
  138.8 7.4 %collective-permute-start.15 = (f32[128,256]{1,0:T(8,128)S(1)}, f32[128,256]{1,0:T(8,128)S(1)}, u32[]{:S(2)}, u32[]{:S(2)}) collective-permute-start(f32[128,256]{1,0:T(8,128)S(1)} %add_add_fusion.1), channel_id=1, source_target_pairs={{0,2},{1,3},{2,0},{3,1},{4,6},{5,7},{6,4},{7,5},{8,10},{9,11},{10,... | collective-permute-start | bytes 393224 | tf_op jit(solution)/shard_map/ppermute | solution.py:229
  139.4 8.9 %collective-permute-start.14 = (f32[128,256]{1,0:T(8,128)S(1)}, f32[128,256]{1,0:T(8,128)S(1)}, u32[]{:S(2)}, u32[]{:S(2)}) collective-permute-start(f32[128,256]{1,0:T(8,128)S(1)} %add_add_fusion.1), channel_id=1, source_target_pairs={{0,1},{1,2},{2,3},{3,0},{4,5},{5,6},{6,7},{7,4},{8,9},{9,10},{10,1... | collective-permute-start | bytes 393224 | tf_op jit(solution)/shard_map/ppermute | solution.py:229
  140.7 13.0 %all-to-all-start.4 = ((bf16[16,64,128]{2,1,0:T(8,128)(2,1)}), bf16[16,64,128]{2,1,0:T(8,128)(2,1)S(1)}, u32[]{:S(2)}, u32[]{:S(2)}) async-start(bf16[16,64,128]{2,1,0:T(8,128)(2,1)} %sum_feat.1), calls=%async_computation.4 | async-start | bytes 524288 | tf_op jit(solution)/shard_map/all_to_all | solution.py:218
  (8 other events, 113.5 us)

commit v11 on v10

--- a/solution.py
+++ b/solution.py
@@ -188,21 +188,32 @@
         out_ref[f] = total
 
 
-def second_sum_body(two_ref, out_ref):
+def second_sum_body(x_ref, two_ref, one_ref, out_ref):
     two = two_ref[0].astype(F32)
     for f in range(1, NF):
         two = two + two_ref[f].astype(F32)
     two = two.astype(BF)
+    one = one_ref[pl.ds(pl.multiple_of(x_ref[0] * 32, 32), 32), :].astype(BF)
     for q in range(ND):
-        out_ref[q] = two
-
-
-def place_body(in_ref, g2s_ref, g2n_ref):
-    for q in range(ND):
-        g2 = g2s_ref if q < 8 else g2n_ref
+        out_ref[q, 0:64, :] = two
         for h in range(2):
+            out_ref[q, 64 + h * 32 : 96 + h * 32, :] = one[:, h * 128 : (h + 1) * 128]
+
+
+def place_body(in_ref, g1s_ref, g1n_ref, g2s_ref, g2n_ref):
+    for h in range(2):
+        lanes = slice(h * 128, (h + 1) * 128)
+        for x in range(4):
+            at = 64 + h * 32
+            rows = in_ref[4 * x, at : at + 32, :].astype(F32)
+            for y in range(1, 4):
+                rows = rows + in_ref[4 * x + y, at : at + 32, :].astype(F32)
+            g1 = g1s_ref if x < 2 else g1n_ref
+            g1[x % 2 * 32 : x % 2 * 32 + 32, lanes] = rows
+        for q in range(ND):
+            g2 = g2s_ref if q < 8 else g2n_ref
             piece = in_ref[q, h * 32 : h * 32 + 32, :].astype(F32)
-            g2[(q % 8) * 32 : (q % 8) * 32 + 32, h * 128 : (h + 1) * 128] = piece
+            g2[(q % 8) * 32 : (q % 8) * 32 + 32, lanes] = piece
 
 
 def layer_body(count_ref, neigh_ref, in_ref, part_ref, w2n_ref, layer_ref, hot):
@@ -224,8 +235,8 @@
     return lax.ppermute(x, "feat", [(i, (i + 2 * step) % NF) for i in range(NF)])
 
 
-def along(x, step):
-    pairs = [(i, (i + step) % ND if step % 4 == 0 else i // 4 * 4 + (i + step) % 4) for i in range(ND)]
+def along_x(x, step):
+    pairs = [(i, (i + 4 * step) % ND) for i in range(ND)]
     return lax.ppermute(x, "dom", pairs)
 
 
@@ -308,14 +319,17 @@
         us=2,
     )(chip, rows, *[ring[i] for i in RING])
     one = keep + fetch(give, 1)
-    one = one + sum(along(one, 4 * i) for i in range(1, 4))
+    one = one + sum(along_x(one, i) for i in range(1, 4))
     one, two, layer_out = lax.optimization_barrier((one, two, layer_out))
-    one = one + sum(along(one, i) for i in range(1, 4))
-    done = call(second_sum_body, "sum_feat", shape((ND, 64, 128), BF), [VMEM])(two)
+    x = jnp.right_shift(lax.axis_index("dom"), 2).reshape(1)
+    done = call(
+        second_sum_body, "sum_feat", shape((ND, 128, 128), BF), [SMEM] + [VMEM] * 2
+    )(x, two, one)
     done = swap(done, "dom")
+    first = shape((COLS, HID), F32)
     second = shape((HID, HID), F32)
-    two_self, two_neigh = call(place_body, "place", (second, second), [VMEM])(done)
-    return (layer_out[None, None], one[:COLS], one[COLS:], two_self, two_neigh)
+    grads = call(place_body, "place", (first, first, second, second), [VMEM])(done)
+    return (layer_out[None, None], *grads)
 
 
 def solution(mesh):

time: 155 us -> 155 us (level)
  blocking collectives: 39.1 us -> 56.3 us
  starting transfers between devices: 47.4 us -> 38.3 us
  waiting for transfers between devices: 25.4 us -> 18.6 us
    all_to_all x1 -> x2, blocking collectives: 39.1 us -> 56.3 us  [swap(): lax.all_to_all(x, axis, split_axis=0, concat_axis=0, tiled=True, axis_ind...]
    all_to_all x4 -> x3, starting transfers between devices: 20.6 us -> 15.2 us  [swap(): lax.all_to_all(x, axis, split_axis=0, concat_axis=0, tiled=True, axis_ind...]
    all_to_all x4 -> x3, waiting for transfers between devices: 4.68 us -> 0.01 us  [swap(): lax.all_to_all(x, axis, split_axis=0, concat_axis=0, tiled=True, axis_ind...]
    ppermute x6 -> x3, starting transfers between devices: 8.34 us -> 4.72 us  [along_x(): return lax.ppermute(x, 'dom', pairs)]
    ppermute x6 -> x3, waiting for transfers between devices: 7.28 us -> 5.17 us  [along_x(): return lax.ppermute(x, 'dom', pairs)]
  transfers between devices with their start and end apart: 21 -> 17, of which waited for: 10 -> 8; matrix products, arithmetic and copies ran while one was open for 0% -> 0% of each run, Pallas kernels for 23% -> 23%
where the time goes in v11:
time: 155 us
  blocking collectives  56.3 us (36%)
  Pallas kernels  38.8 us (25%)
  starting transfers between devices  38.3 us (25%)
  waiting for transfers between devices  18.6 us (12%)
  local copies, waits for them, and re-layouts  1.68 us (1%)
    all_to_all x2, blocking collectives, swap(): lax.all_to_all(x, axis, split_axis=0, concat_axis=0, tiled=True, axis_ind...  56.3 us
    pallas_call x1, Pallas kernels, per_device(): call(rows_body, 'node_rows', (rows, rows), [SMEM, VMEM, VMEM, SMEM] + [VM...  25.7 us
    all_to_all x3, starting transfers between devices, swap(): lax.all_to_all(x, axis, split_axis=0, concat_axis=0, tiled=True, axis_ind...  15.2 us
    ppermute x7, waiting for transfers between devices, turn(): lax.ppermute(x, 'feat', [(i, (i + 2 * step) % NF) for i in range(NF)])  13.4 us
    ppermute x4, starting transfers between devices, fetch(): return lax.ppermute(x, 'feat', [(i, i ^ bit) for i in range(NF)])  10.4 us
    ppermute x7, starting transfers between devices, turn(): lax.ppermute(x, 'feat', [(i, (i + 2 * step) % NF) for i in range(NF)])  8.06 us
    ppermute x3, waiting for transfers between devices, along_x(): return lax.ppermute(x, 'dom', pairs)  5.17 us
    ppermute x3, starting transfers between devices, along_x(): return lax.ppermute(x, 'dom', pairs)  4.72 us
  transfers between devices with their start and end apart: 17, of which 8 were waited for; matrix products, arithmetic and copies ran while one was open for 0% of the time, Pallas kernels for 23%

profile of v11, /device:TPU:1, one launch (start us, length us, event | category | flops | bytes accessed | tf_op | source)
XLA Modules:
  0.0 154.6 jit_solution(11062420057880428895)
XLA Ops:
  0.6 3.3 %collective-permute-start = (bf16[64,9216]{1,0:T(8,128)(2,1)}, bf16[64,9216]{1,0:T(8,128)(2,1)S(1)}, u32[]{:S(2)}, u32[]{:S(2)}) collective-permute-start(bf16[64,9216]{1,0:T(8,128)(2,1)} %bitcast.23), channel_id=1, source_target_pairs={{0,16},{16,0},{32,48},{48,32},{64,80},{80,64},{96,112},{112,96},{1... | collective-permute-start | bytes 3538952 | tf_op jit(solution)/shard_map/ppermute | solution.py:244
  4.5 3.8 %picks.1 = bf16[16,128,256]{2,1,0:T(8,128)(2,1)} custom-call(s32[16]{0:T(128)} %bitcast.21, s32[15,1,256]{2,1,0:T(1,128)} %bitcast.15, bf16[256,256]{1,0:T(8,128)(2,1)} %bitcast.13), custom_call_target="tpu_custom_call" | custom-call | flops 4000000000 | bytes 4000000 | tf_op jit(solution)/shard_map/picks/pallas_call | solution.py:266
  8.3 5.0 %all-to-all-start.1 = ((bf16[16,128,256]{2,1,0:T(8,128)(2,1)}), bf16[16,128,256]{2,1,0:T(8,128)(2,1)S(1)}, u32[]{:S(2)}, u32[]{:S(2)}) async-start(bf16[16,128,256]{2,1,0:T(8,128)(2,1)} %picks.1), calls=%async_computation.1 | async-start | bytes 2097152 | tf_op jit(solution)/shard_map/all_to_all | solution.py:229
  14.4 25.7 %node_rows.1 = (bf16[8,288,256]{2,1,0:T(8,128)(2,1)}, bf16[8,288,256]{2,1,0:T(8,128)(2,1)}) custom-call(s32[1]{0:T(128)} %bitcast.1.core_ref, bf16[64,9216]{1,0:T(8,128)(2,1)} %bitcast.24, bf16[64,9216]{1,0:T(8,128)(2,1)} %copy-done.8, s32[46080]{0:T(1024)} %bitcast.25, bf16[64,256]{1,0:T(8,128)(2,1)} %ws_ref.1, bf16[64,256]{1,0:T(8,128)(2,1)} %wn_ref.1, ...), custom_call_target="tpu_custom_call" | custom-call | flops 22000001024 | bytes 22000000 | tf_op jit(solution)/shard_map/node_rows/pallas_call | solution.py:272
  40.2 39.1 %all_to_all.25.share_ref = bf16[8,288,256]{2,1,0:T(8,128)(2,1)S(1)} all-to-all(bf16[8,288,256]{2,1,0:T(8,128)(2,1)} %get-tuple-element.34), channel_id=1, replica_groups={{0,32,64,96,128,160,192,224},{16,48,80,112,144,176,208,240},{1,33,65,97..., dimensions={0} | all-to-all | bytes 2359296 | tf_op jit(solution)/shard_map/all_to_all | solution.py:229
  79.3 1.5 hidden.1
  80.9 1.5 collective-permute-start.3
  82.3 2.0 %outgoing.1 = (bf16[16,320,128]{2,1,0:T(8,128)(2,1)}, f32[256,256]{1,0:T(8,128)S(1)}) custom-call(bf16[288,256]{1,0:T(8,128)(2,1)S(1)} %get-tuple-element.37.hidden_ref, bf16[512,256]{1,0:T(8,128)(2,1)S(1)} %get-tuple-element.38.g2_ref, s32[16,128]{1,0:T(8,128)S(1)} %bitcast.18, s32[1,256]{1,0:T(1,128)S(1)} %bitcast.20, bf16[256,256]{1,0:T(8,128)(2,1)S(1)} %copy-done.1), custom_call_target="tpu_custom_call" | custom-call | flops 2000000000 | bytes 2000000 | tf_op jit(solution)/shard_map/outgoing/pallas_call | solution.py:288
  84.8 1.3 collective-permute-done.3.refs_1_
  86.1 6.3 %all-to-all-start.2 = ((bf16[16,320,128]{2,1,0:T(8,128)(2,1)}), bf16[16,320,128]{2,1,0:T(8,128)(2,1)S(1)}, u32[]{:S(2)}, u32[]{:S(2)}) async-start(bf16[16,320,128]{2,1,0:T(8,128)(2,1)} %get-tuple-element.46), calls=%async_computation.2 | async-start | bytes 2621440 | tf_op jit(solution)/shard_map/all_to_all | solution.py:229
  93.0 2.2 %collective-permute-start.6 = (bf16[288,256]{1,0:T(8,128)(2,1)S(1)}, bf16[288,256]{1,0:T(8,128)(2,1)S(1)}, u32[]{:S(2)}, u32[]{:S(2)}) collective-permute-start(bf16[288,256]{1,0:T(8,128)(2,1)S(1)} %collective-permute-done.4.refs_2_), channel_id=1, source_target_pairs={{0,224},{16,240},{32,0},{48,16},{64,32},{80,48},{96,64},{112,80},{... | collective-permute-start | bytes 442376 | tf_op jit(solution)/shard_map/ppermute | solution.py:235
  95.2 2.5 %collective-permute-done.5.refs_3_ = bf16[288,256]{1,0:T(8,128)(2,1)S(1)} collective-permute-done((bf16[288,256]{1,0:T(8,128)(2,1)S(1)}, bf16[288,256]{1,0:T(8,128)(2,1)S(1)}, u32[]{:S(2)}, u32[]{:S(2)}) %collective-permute-start.5) | collective-permute-done | bytes 147488 | tf_op jit(solution)/shard_map/ppermute | solution.py:235
  97.8 3.0 %collective-permute-start.8 = (bf16[288,256]{1,0:T(8,128)(2,1)S(1)}, bf16[288,256]{1,0:T(8,128)(2,1)S(1)}, u32[]{:S(2)}, u32[]{:S(2)}) collective-permute-start(bf16[288,256]{1,0:T(8,128)(2,1)S(1)} %collective-permute-done.6.refs_4_), channel_id=1, source_target_pairs={{0,224},{16,240},{32,0},{48,16},{64,32},{80,48},{96,64},{112,80},{... | collective-permute-start | bytes 442376 | tf_op jit(solution)/shard_map/ppermute | solution.py:235
  100.7 2.8 %collective-permute-done.7.refs_5_ = bf16[288,256]{1,0:T(8,128)(2,1)S(1)} collective-permute-done((bf16[288,256]{1,0:T(8,128)(2,1)S(1)}, bf16[288,256]{1,0:T(8,128)(2,1)S(1)}, u32[]{:S(2)}, u32[]{:S(2)}) %collective-permute-start.7) | collective-permute-done | bytes 147488 | tf_op jit(solution)/shard_map/ppermute | solution.py:235
  103.6 0.8 collective-permute-start.9
  104.4 6.2 %collective-permute-done.9.refs_7_ = bf16[288,256]{1,0:T(8,128)(2,1)S(1)} collective-permute-done((bf16[288,256]{1,0:T(8,128)(2,1)S(1)}, bf16[288,256]{1,0:T(8,128)(2,1)S(1)}, u32[]{:S(2)}, u32[]{:S(2)}) %collective-permute-start.9) | collective-permute-done | bytes 147488 | tf_op jit(solution)/shard_map/ppermute | solution.py:235
  112.7 6.5 %collective-permute-start.10 = (f32[128,256]{1,0:T(8,128)S(1)}, f32[128,256]{1,0:T(8,128)S(1)}, u32[]{:S(2)}, u32[]{:S(2)}) collective-permute-start(f32[128,256]{1,0:T(8,128)S(1)} %get-tuple-element.51), channel_id=1, source_target_pairs={{0,16},{16,0},{32,48},{48,32},{64,80},{80,64},{96,112},{112,96},{1... | collective-permute-start | bytes 393224 | tf_op jit(solution)/shard_map/ppermute | solution.py:244
  119.2 3.8 %all-to-all-start.3 = ((bf16[16,64,128]{2,1,0:T(8,128)(2,1)}), bf16[16,64,128]{2,1,0:T(8,128)(2,1)S(1)}, u32[]{:S(2)}, u32[]{:S(2)}) async-start(bf16[16,64,128]{2,1,0:T(8,128)(2,1)} %sum_dom.1), calls=%async_computation.3 | async-start | bytes 524288 | tf_op jit(solution)/shard_map/all_to_all | solution.py:229
  123.0 3.6 %collective-permute-start.13 = (f32[128,256]{1,0:T(8,128)S(1)}, f32[128,256]{1,0:T(8,128)S(1)}, u32[]{:S(2)}, u32[]{:S(2)}) collective-permute-start(f32[128,256]{1,0:T(8,128)S(1)} %add.12), channel_id=1, source_target_pairs={{0,12},{1,13},{2,14},{3,15},{4,0},{5,1},{6,2},{7,3},{8,4},{9,5},{1... | collective-permute-start | bytes 393224 | tf_op jit(solution)/shard_map/ppermute | solution.py:240
  127.7 3.4 %layer_two.1 = bf16[256,256]{1,0:T(8,128)(2,1)} custom-call(s32[16]{0:T(128)S(1)} %bitcast.22, s32[15,1,256]{2,1,0:T(1,128)S(1)} %bitcast.16, bf16[16,320,128]{2,1,0:T(8,128)(2,1)S(1)} %all-to-all-done.2.in_ref, f32[256,256]{1,0:T(8,128)S(1)} %get-tuple-element.53.part_ref, bf16[256,256]{1,0:T(8,128)(2,1)S(1)} %copy-done.2), custom_call_target="tpu_custom_call" | custom-call | flops 5000000000 | bytes 5000000 | tf_op jit(solution)/shard_map/layer_two/pallas_call | solution.py:304
  131.1 0.9 collective-permute-done.13
  132.8 3.5 %collective-permute-done.11 = f32[128,256]{1,0:T(8,128)S(1)} collective-permute-done((f32[128,256]{1,0:T(8,128)S(1)}, f32[128,256]{1,0:T(8,128)S(1)}, u32[]{:S(2)}, u32[]{:S(2)}) %collective-permute-start.11) | collective-permute-done | bytes 131104 | tf_op jit(solution)/shard_map/ppermute | solution.py:240
  136.4 17.2 %all_to_all.26.in_ref = bf16[16,128,128]{2,1,0:T(8,128)(2,1)S(1)} all-to-all(bf16[16,128,128]{2,1,0:T(8,128)(2,1)S(1)} %sum_feat.1), channel_id=1, replica_groups=mesh['feat'=16,'dom'=16] {'dom'}, dimensions={0} | all-to-all | bytes 1048576 | tf_op jit(solution)/shard_map/all_to_all | solution.py:229
  153.7 0.9 place.1
  (45 shorter events, 6.9 us)
Async XLA Ops:
  0.6 12.7 %collective-permute-start = (bf16[64,9216]{1,0:T(8,128)(2,1)}, bf16[64,9216]{1,0:T(8,128)(2,1)S(1)}, u32[]{:S(2)}, u32[]{:S(2)}) collective-permute-start(bf16[64,9216]{1,0:T(8,128)(2,1)} %bitcast.23), channel_id=1, source_target_pairs={{0,16},{16,0},{32,48},{48,32},{64,80},{80,64},{96,112},{112,96},{1... | collective-permute-start | bytes 3538952 | tf_op jit(solution)/shard_map/ppermute | solution.py:244
  4.0 9.4 %collective-permute-start.1 = (bf16[64,256]{1,0:T(8,128)(2,1)}, bf16[64,256]{1,0:T(8,128)(2,1)S(1)}, u32[]{:S(2)}, u32[]{:S(2)}) collective-permute-start(bf16[64,256]{1,0:T(8,128)(2,1)} %ws_ref.1), channel_id=1, source_target_pairs={{0,16},{16,0},{32,48},{48,32},{64,80},{80,64},{96,112},{112,96},{1... | collective-permute-start | bytes 98312 | tf_op jit(solution)/shard_map/ppermute | solution.py:244
  4.1 9.3 %collective-permute-start.2 = (bf16[64,256]{1,0:T(8,128)(2,1)}, bf16[64,256]{1,0:T(8,128)(2,1)S(1)}, u32[]{:S(2)}, u32[]{:S(2)}) collective-permute-start(bf16[64,256]{1,0:T(8,128)(2,1)} %wn_ref.1), channel_id=1, source_target_pairs={{0,16},{16,0},{32,48},{48,32},{64,80},{80,64},{96,112},{112,96},{1... | collective-permute-start | bytes 98312 | tf_op jit(solution)/shard_map/ppermute | solution.py:244
  8.3 31.9 %all-to-all-start.1 = ((bf16[16,128,256]{2,1,0:T(8,128)(2,1)}), bf16[16,128,256]{2,1,0:T(8,128)(2,1)S(1)}, u32[]{:S(2)}, u32[]{:S(2)}) async-start(bf16[16,128,256]{2,1,0:T(8,128)(2,1)} %picks.1), calls=%async_computation.1 | async-start | bytes 2097152 | tf_op jit(solution)/shard_map/all_to_all | solution.py:229
  40.1 39.1 %copy-start = (bf16[1,1,256,256]{3,2,1,0:T(8,128)(2,1)S(1)}, bf16[1,1,256,256]{3,2,1,0:T(8,128)(2,1)}, u32[]{:S(2)}) copy-start(bf16[1,1,256,256]{3,2,1,0:T(8,128)(2,1)} %param.21) | copy-start | bytes 393220
  40.1 39.1 %copy-start.1 = (bf16[256,256]{1,0:T(8,128)(2,1)S(1)}, bf16[256,256]{1,0:T(8,128)(2,1)}, u32[]{:S(2)}) copy-start(bf16[256,256]{1,0:T(8,128)(2,1)} %w2s_ref.3) | copy-start | bytes 393220
  40.1 39.1 %copy-start.2 = (bf16[256,256]{1,0:T(8,128)(2,1)S(1)}, bf16[256,256]{1,0:T(8,128)(2,1)}, u32[]{:S(2)}) copy-start(bf16[256,256]{1,0:T(8,128)(2,1)} %w2n_ref.3) | copy-start | bytes 393220
  40.2 39.1 %copy-start.4 = (s32[1,1,16,128]{3,2,1,0:T(8,128)S(1)}, s32[1,1,16,128]{3,2,1,0:T(8,128)}, u32[]{:S(2)}) copy-start(s32[1,1,16,128]{3,2,1,0:T(8,128)} %param.17) | copy-start | bytes 24580
  40.2 39.1 %copy-start.5 = (s32[1,1,256]{2,1,0:T(1,128)S(1)}, s32[1,1,256]{2,1,0:T(1,128)}, u32[]{:S(2)}) copy-start(s32[1,1,256]{2,1,0:T(1,128)} %param.20) | copy-start | bytes 3076
  80.8 4.1 %collective-permute-start.4 = (bf16[288,256]{1,0:T(8,128)(2,1)S(1)}, bf16[288,256]{1,0:T(8,128)(2,1)S(1)}, u32[]{:S(2)}, u32[]{:S(2)}) collective-permute-start(bf16[288,256]{1,0:T(8,128)(2,1)S(1)} %get-tuple-element.35.refs_0_), channel_id=1, source_target_pairs={{0,224},{16,240},{32,0},{48,16},{64,32},{80,48},{96,64},{112,80},{... | collective-permute-start | bytes 442376 | tf_op jit(solution)/shard_map/ppermute | solution.py:235
  80.9 5.3 %collective-permute-start.3 = (bf16[288,256]{1,0:T(8,128)(2,1)S(1)}, bf16[288,256]{1,0:T(8,128)(2,1)S(1)}, u32[]{:S(2)}, u32[]{:S(2)}) collective-permute-start(bf16[288,256]{1,0:T(8,128)(2,1)S(1)} %get-tuple-element.35.refs_0_), channel_id=1, source_target_pairs={{0,32},{16,48},{32,64},{48,80},{64,96},{80,112},{96,128},{112,144}... | collective-permute-start | bytes 442376 | tf_op jit(solution)/shard_map/ppermute | solution.py:235
  86.1 24.4 %all-to-all-start.2 = ((bf16[16,320,128]{2,1,0:T(8,128)(2,1)}), bf16[16,320,128]{2,1,0:T(8,128)(2,1)S(1)}, u32[]{:S(2)}, u32[]{:S(2)}) async-start(bf16[16,320,128]{2,1,0:T(8,128)(2,1)} %get-tuple-element.46), calls=%async_computation.2 | async-start | bytes 2621440 | tf_op jit(solution)/shard_map/all_to_all | solution.py:229
  92.5 5.3 %collective-permute-start.5 = (bf16[288,256]{1,0:T(8,128)(2,1)S(1)}, bf16[288,256]{1,0:T(8,128)(2,1)S(1)}, u32[]{:S(2)}, u32[]{:S(2)}) collective-permute-start(bf16[288,256]{1,0:T(8,128)(2,1)S(1)} %collective-permute-done.3.refs_1_), channel_id=1, source_target_pairs={{0,32},{16,48},{32,64},{48,80},{64,96},{80,112},{96,128},{112,144}... | collective-permute-start | bytes 442376 | tf_op jit(solution)/shard_map/ppermute | solution.py:235
  93.0 4.7 %collective-permute-start.6 = (bf16[288,256]{1,0:T(8,128)(2,1)S(1)}, bf16[288,256]{1,0:T(8,128)(2,1)S(1)}, u32[]{:S(2)}, u32[]{:S(2)}) collective-permute-start(bf16[288,256]{1,0:T(8,128)(2,1)S(1)} %collective-permute-done.4.refs_2_), channel_id=1, source_target_pairs={{0,224},{16,240},{32,0},{48,16},{64,32},{80,48},{96,64},{112,80},{... | collective-permute-start | bytes 442376 | tf_op jit(solution)/shard_map/ppermute | solution.py:235
  97.8 5.8 %collective-permute-start.7 = (bf16[288,256]{1,0:T(8,128)(2,1)S(1)}, bf16[288,256]{1,0:T(8,128)(2,1)S(1)}, u32[]{:S(2)}, u32[]{:S(2)}) collective-permute-start(bf16[288,256]{1,0:T(8,128)(2,1)S(1)} %collective-permute-done.5.refs_3_), channel_id=1, source_target_pairs={{0,32},{16,48},{32,64},{48,80},{64,96},{80,112},{96,128},{112,144}... | collective-permute-start | bytes 442376 | tf_op jit(solution)/shard_map/ppermute | solution.py:235
  97.8 5.8 %collective-permute-start.8 = (bf16[288,256]{1,0:T(8,128)(2,1)S(1)}, bf16[288,256]{1,0:T(8,128)(2,1)S(1)}, u32[]{:S(2)}, u32[]{:S(2)}) collective-permute-start(bf16[288,256]{1,0:T(8,128)(2,1)S(1)} %collective-permute-done.6.refs_4_), channel_id=1, source_target_pairs={{0,224},{16,240},{32,0},{48,16},{64,32},{80,48},{96,64},{112,80},{... | collective-permute-start | bytes 442376 | tf_op jit(solution)/shard_map/ppermute | solution.py:235
  103.6 7.0 %collective-permute-start.9 = (bf16[288,256]{1,0:T(8,128)(2,1)S(1)}, bf16[288,256]{1,0:T(8,128)(2,1)S(1)}, u32[]{:S(2)}, u32[]{:S(2)}) collective-permute-start(bf16[288,256]{1,0:T(8,128)(2,1)S(1)} %collective-permute-done.7.refs_5_), channel_id=1, source_target_pairs={{0,32},{16,48},{32,64},{48,80},{64,96},{80,112},{96,128},{112,144}... | collective-permute-start | bytes 442376 | tf_op jit(solution)/shard_map/ppermute | solution.py:235
  111.9 15.8 %copy-start.3 = (s32[1,1,256,15]{2,1,3,0:T(1,128)S(1)}, s32[1,1,256,15]{2,1,3,0:T(1,128)}, u32[]{:S(2)}) copy-start(s32[1,1,256,15]{2,1,3,0:T(1,128)} %param.19) | copy-start | bytes 46084
  111.9 15.8 %copy-start.6 = (s32[16,1,1]{0,2,1:T(1,128)S(1)}, s32[16,1,1]{0,2,1:T(1,128)}, u32[]{:S(2)}) copy-start(s32[16,1,1]{0,2,1:T(1,128)} %param.18) | copy-start | bytes 196
  112.7 10.3 %collective-permute-start.10 = (f32[128,256]{1,0:T(8,128)S(1)}, f32[128,256]{1,0:T(8,128)S(1)}, u32[]{:S(2)}, u32[]{:S(2)}) collective-permute-start(f32[128,256]{1,0:T(8,128)S(1)} %get-tuple-element.51), channel_id=1, source_target_pairs={{0,16},{16,0},{32,48},{48,32},{64,80},{80,64},{96,112},{112,96},{1... | collective-permute-start | bytes 393224 | tf_op jit(solution)/shard_map/ppermute | solution.py:244
  119.2 17.2 %all-to-all-start.3 = ((bf16[16,64,128]{2,1,0:T(8,128)(2,1)}), bf16[16,64,128]{2,1,0:T(8,128)(2,1)S(1)}, u32[]{:S(2)}, u32[]{:S(2)}) async-start(bf16[16,64,128]{2,1,0:T(8,128)(2,1)} %sum_dom.1), calls=%async_computation.3 | async-start | bytes 524288 | tf_op jit(solution)/shard_map/all_to_all | solution.py:229
  123.0 9.1 %collective-permute-start.13 = (f32[128,256]{1,0:T(8,128)S(1)}, f32[128,256]{1,0:T(8,128)S(1)}, u32[]{:S(2)}, u32[]{:S(2)}) collective-permute-start(f32[128,256]{1,0:T(8,128)S(1)} %add.12), channel_id=1, source_target_pairs={{0,12},{1,13},{2,14},{3,15},{4,0},{5,1},{6,2},{7,3},{8,4},{9,5},{1... | collective-permute-start | bytes 393224 | tf_op jit(solution)/shard_map/ppermute | solution.py:240
  126.6 6.3 %collective-permute-start.12 = (f32[128,256]{1,0:T(8,128)S(1)}, f32[128,256]{1,0:T(8,128)S(1)}, u32[]{:S(2)}, u32[]{:S(2)}) collective-permute-start(f32[128,256]{1,0:T(8,128)S(1)} %add.12), channel_id=1, source_target_pairs={{0,8},{1,9},{2,10},{3,11},{4,12},{5,13},{6,14},{7,15},{8,0},{9,1},... | collective-permute-start | bytes 393224 | tf_op jit(solution)/shard_map/ppermute | solution.py:240
  127.2 9.2 %collective-permute-start.11 = (f32[128,256]{1,0:T(8,128)S(1)}, f32[128,256]{1,0:T(8,128)S(1)}, u32[]{:S(2)}, u32[]{:S(2)}) collective-permute-start(f32[128,256]{1,0:T(8,128)S(1)} %add.12), channel_id=1, source_target_pairs={{0,4},{1,5},{2,6},{3,7},{4,8},{5,9},{6,10},{7,11},{8,12},{9,13},{1... | collective-permute-start | bytes 393224 | tf_op jit(solution)/shard_map/ppermute | solution.py:240
  (4 other events, 3.6 us)

commit v12 on v11

--- a/solution.py
+++ b/solution.py
@@ -319,7 +319,8 @@
         us=2,
     )(chip, rows, *[ring[i] for i in RING])
     one = keep + fetch(give, 1)
-    one = one + sum(along_x(one, i) for i in range(1, 4))
+    rounded = one.astype(BF)
+    one = one + sum(along_x(rounded, i).astype(F32) for i in range(1, 4))
     one, two, layer_out = lax.optimization_barrier((one, two, layer_out))
     x = jnp.right_shift(lax.axis_index("dom"), 2).reshape(1)
     done = call(

time: 155 us -> 155 us (level)
  blocking collectives: 56.3 us -> 58 us
  waiting for transfers between devices: 18.6 us -> 16.9 us
    ppermute x3, waiting for transfers between devices: 5.17 us -> 2.05 us  [along_x(): return lax.ppermute(x, 'dom', pairs)]
    all_to_all x2, blocking collectives: 56.3 us -> 58 us  [swap(): lax.all_to_all(x, axis, split_axis=0, concat_axis=0, tiled=True, axis_ind...]
where the time goes in v12:
time: 155 us
  blocking collectives  58 us (37%)
  Pallas kernels  38.8 us (25%)
  starting transfers between devices  38.3 us (25%)
  waiting for transfers between devices  16.9 us (11%)
  local copies, waits for them, and re-layouts  1.68 us (1%)
    all_to_all x2, blocking collectives, swap(): lax.all_to_all(x, axis, split_axis=0, concat_axis=0, tiled=True, axis_ind...  58 us
    pallas_call x1, Pallas kernels, per_device(): call(rows_body, 'node_rows', (rows, rows), [SMEM, VMEM, VMEM, SMEM] + [VM...  25.7 us
    all_to_all x3, starting transfers between devices, swap(): lax.all_to_all(x, axis, split_axis=0, concat_axis=0, tiled=True, axis_ind...  15.1 us
    ppermute x7, waiting for transfers between devices, turn(): lax.ppermute(x, 'feat', [(i, (i + 2 * step) % NF) for i in range(NF)])  13.4 us
    ppermute x4, starting transfers between devices, fetch(): return lax.ppermute(x, 'feat', [(i, i ^ bit) for i in range(NF)])  10.4 us
    ppermute x7, starting transfers between devices, turn(): lax.ppermute(x, 'feat', [(i, (i + 2 * step) % NF) for i in range(NF)])  8.06 us
    ppermute x3, starting transfers between devices, along_x(): return lax.ppermute(x, 'dom', pairs)  4.72 us
    pallas_call x1, Pallas kernels, per_device(): call(pick_body, 'picks', shape((ND, SLOTS, HID), BF), [SMEM, VMEM, VMEM],...  3.8 us
  transfers between devices with their start and end apart: 17, of which 8 were waited for; matrix products, arithmetic and copies ran while one was open for 0% of the time, Pallas kernels for 23%

profile of v12, /device:TPU:1, one launch (start us, length us, event | category | flops | bytes accessed | tf_op | source)
XLA Modules:
  0.0 154.6 jit_solution(1263762765518173804)
XLA Ops:
  0.6 3.3 %collective-permute-start = (bf16[64,9216]{1,0:T(8,128)(2,1)}, bf16[64,9216]{1,0:T(8,128)(2,1)S(1)}, u32[]{:S(2)}, u32[]{:S(2)}) collective-permute-start(bf16[64,9216]{1,0:T(8,128)(2,1)} %bitcast.23), channel_id=1, source_target_pairs={{0,16},{16,0},{32,48},{48,32},{64,80},{80,64},{96,112},{112,96},{1... | collective-permute-start | bytes 3538952 | tf_op jit(solution)/shard_map/ppermute | solution.py:244
  4.5 3.8 %picks.1 = bf16[16,128,256]{2,1,0:T(8,128)(2,1)} custom-call(s32[16]{0:T(128)} %bitcast.21, s32[15,1,256]{2,1,0:T(1,128)} %bitcast.15, bf16[256,256]{1,0:T(8,128)(2,1)} %bitcast.13), custom_call_target="tpu_custom_call" | custom-call | flops 4000000000 | bytes 4000000 | tf_op jit(solution)/shard_map/picks/pallas_call | solution.py:266
  8.3 5.0 %all-to-all-start.1 = ((bf16[16,128,256]{2,1,0:T(8,128)(2,1)}), bf16[16,128,256]{2,1,0:T(8,128)(2,1)S(1)}, u32[]{:S(2)}, u32[]{:S(2)}) async-start(bf16[16,128,256]{2,1,0:T(8,128)(2,1)} %picks.1), calls=%async_computation.1 | async-start | bytes 2097152 | tf_op jit(solution)/shard_map/all_to_all | solution.py:229
  14.4 25.7 %node_rows.1 = (bf16[8,288,256]{2,1,0:T(8,128)(2,1)}, bf16[8,288,256]{2,1,0:T(8,128)(2,1)}) custom-call(s32[1]{0:T(128)} %bitcast.1.core_ref, bf16[64,9216]{1,0:T(8,128)(2,1)} %bitcast.24, bf16[64,9216]{1,0:T(8,128)(2,1)} %copy-done.8, s32[46080]{0:T(1024)} %bitcast.25, bf16[64,256]{1,0:T(8,128)(2,1)} %ws_ref.1, bf16[64,256]{1,0:T(8,128)(2,1)} %wn_ref.1, ...), custom_call_target="tpu_custom_call" | custom-call | flops 22000001024 | bytes 22000000 | tf_op jit(solution)/shard_map/node_rows/pallas_call | solution.py:272
  40.2 39.1 %all_to_all.25.share_ref = bf16[8,288,256]{2,1,0:T(8,128)(2,1)S(1)} all-to-all(bf16[8,288,256]{2,1,0:T(8,128)(2,1)} %get-tuple-element.34), channel_id=1, replica_groups={{0,32,64,96,128,160,192,224},{16,48,80,112,144,176,208,240},{1,33,65,97..., dimensions={0} | all-to-all | bytes 2359296 | tf_op jit(solution)/shard_map/all_to_all | solution.py:229
  79.3 1.5 hidden.1
  80.9 1.5 collective-permute-start.3
  82.3 2.0 %outgoing.1 = (bf16[16,320,128]{2,1,0:T(8,128)(2,1)}, f32[256,256]{1,0:T(8,128)S(1)}) custom-call(bf16[288,256]{1,0:T(8,128)(2,1)S(1)} %get-tuple-element.37.hidden_ref, bf16[512,256]{1,0:T(8,128)(2,1)S(1)} %get-tuple-element.38.g2_ref, s32[16,128]{1,0:T(8,128)S(1)} %bitcast.18, s32[1,256]{1,0:T(1,128)S(1)} %bitcast.20, bf16[256,256]{1,0:T(8,128)(2,1)S(1)} %copy-done.1), custom_call_target="tpu_custom_call" | custom-call | flops 2000000000 | bytes 2000000 | tf_op jit(solution)/shard_map/outgoing/pallas_call | solution.py:288
  84.9 1.3 collective-permute-done.3.refs_1_
  86.2 6.3 %all-to-all-start.2 = ((bf16[16,320,128]{2,1,0:T(8,128)(2,1)}), bf16[16,320,128]{2,1,0:T(8,128)(2,1)S(1)}, u32[]{:S(2)}, u32[]{:S(2)}) async-start(bf16[16,320,128]{2,1,0:T(8,128)(2,1)} %get-tuple-element.46), calls=%async_computation.2 | async-start | bytes 2621440 | tf_op jit(solution)/shard_map/all_to_all | solution.py:229
  93.0 2.2 %collective-permute-start.6 = (bf16[288,256]{1,0:T(8,128)(2,1)S(1)}, bf16[288,256]{1,0:T(8,128)(2,1)S(1)}, u32[]{:S(2)}, u32[]{:S(2)}) collective-permute-start(bf16[288,256]{1,0:T(8,128)(2,1)S(1)} %collective-permute-done.4.refs_2_), channel_id=1, source_target_pairs={{0,224},{16,240},{32,0},{48,16},{64,32},{80,48},{96,64},{112,80},{... | collective-permute-start | bytes 442376 | tf_op jit(solution)/shard_map/ppermute | solution.py:235
  95.2 2.5 %collective-permute-done.5.refs_3_ = bf16[288,256]{1,0:T(8,128)(2,1)S(1)} collective-permute-done((bf16[288,256]{1,0:T(8,128)(2,1)S(1)}, bf16[288,256]{1,0:T(8,128)(2,1)S(1)}, u32[]{:S(2)}, u32[]{:S(2)}) %collective-permute-start.5) | collective-permute-done | bytes 147488 | tf_op jit(solution)/shard_map/ppermute | solution.py:235
  97.8 3.0 %collective-permute-start.8 = (bf16[288,256]{1,0:T(8,128)(2,1)S(1)}, bf16[288,256]{1,0:T(8,128)(2,1)S(1)}, u32[]{:S(2)}, u32[]{:S(2)}) collective-permute-start(bf16[288,256]{1,0:T(8,128)(2,1)S(1)} %collective-permute-done.6.refs_4_), channel_id=1, source_target_pairs={{0,224},{16,240},{32,0},{48,16},{64,32},{80,48},{96,64},{112,80},{... | collective-permute-start | bytes 442376 | tf_op jit(solution)/shard_map/ppermute | solution.py:235
  100.7 2.8 %collective-permute-done.7.refs_5_ = bf16[288,256]{1,0:T(8,128)(2,1)S(1)} collective-permute-done((bf16[288,256]{1,0:T(8,128)(2,1)S(1)}, bf16[288,256]{1,0:T(8,128)(2,1)S(1)}, u32[]{:S(2)}, u32[]{:S(2)}) %collective-permute-start.7) | collective-permute-done | bytes 147488 | tf_op jit(solution)/shard_map/ppermute | solution.py:235
  103.6 0.8 collective-permute-start.9
  104.4 6.2 %collective-permute-done.9.refs_7_ = bf16[288,256]{1,0:T(8,128)(2,1)S(1)} collective-permute-done((bf16[288,256]{1,0:T(8,128)(2,1)S(1)}, bf16[288,256]{1,0:T(8,128)(2,1)S(1)}, u32[]{:S(2)}, u32[]{:S(2)}) %collective-permute-start.9) | collective-permute-done | bytes 147488 | tf_op jit(solution)/shard_map/ppermute | solution.py:235
  112.7 6.5 %collective-permute-start.10 = (f32[128,256]{1,0:T(8,128)S(1)}, f32[128,256]{1,0:T(8,128)S(1)}, u32[]{:S(2)}, u32[]{:S(2)}) collective-permute-start(f32[128,256]{1,0:T(8,128)S(1)} %get-tuple-element.51), channel_id=1, source_target_pairs={{0,16},{16,0},{32,48},{48,32},{64,80},{80,64},{96,112},{112,96},{1... | collective-permute-start | bytes 393224 | tf_op jit(solution)/shard_map/ppermute | solution.py:244
  119.2 3.8 %all-to-all-start.3 = ((bf16[16,64,128]{2,1,0:T(8,128)(2,1)}), bf16[16,64,128]{2,1,0:T(8,128)(2,1)S(1)}, u32[]{:S(2)}, u32[]{:S(2)}) async-start(bf16[16,64,128]{2,1,0:T(8,128)(2,1)} %sum_dom.1), calls=%async_computation.3 | async-start | bytes 524288 | tf_op jit(solution)/shard_map/all_to_all | solution.py:229
  123.0 3.6 %collective-permute-start.13 = (bf16[128,256]{1,0:T(8,128)(2,1)S(1)}, bf16[128,256]{1,0:T(8,128)(2,1)S(1)}, u32[]{:S(2)}, u32[]{:S(2)}) collective-permute-start(bf16[128,256]{1,0:T(8,128)(2,1)S(1)} %get-tuple-element.61), channel_id=1, source_target_pairs={{0,12},{1,13},{2,14},{3,15},{4,0},{5,1},{6,2},{7,3},{8,4},{9,5},{1... | collective-permute-start | bytes 196616 | tf_op jit(solution)/shard_map/ppermute | solution.py:240
  127.7 3.4 %layer_two.1 = bf16[256,256]{1,0:T(8,128)(2,1)} custom-call(s32[16]{0:T(128)S(1)} %bitcast.22, s32[15,1,256]{2,1,0:T(1,128)S(1)} %bitcast.16, bf16[16,320,128]{2,1,0:T(8,128)(2,1)S(1)} %all-to-all-done.2.in_ref, f32[256,256]{1,0:T(8,128)S(1)} %get-tuple-element.53.part_ref, bf16[256,256]{1,0:T(8,128)(2,1)S(1)} %copy-done.2), custom_call_target="tpu_custom_call" | custom-call | flops 5000000000 | bytes 5000000 | tf_op jit(solution)/shard_map/layer_two/pallas_call | solution.py:304
  131.5 1.7 %collective-permute-done.11 = bf16[128,256]{1,0:T(8,128)(2,1)S(1)} collective-permute-done((bf16[128,256]{1,0:T(8,128)(2,1)S(1)}, bf16[128,256]{1,0:T(8,128)(2,1)S(1)}, u32[]{:S(2)}, u32[]{:S(2)}) %collective-permute-start.11) | collective-permute-done | bytes 65568 | tf_op jit(solution)/shard_map/ppermute | solution.py:240
  133.2 1.5 all-to-all-done.3.two_ref
  134.8 18.9 %all_to_all.26.in_ref = bf16[16,128,128]{2,1,0:T(8,128)(2,1)S(1)} all-to-all(bf16[16,128,128]{2,1,0:T(8,128)(2,1)S(1)} %sum_feat.1), channel_id=1, replica_groups=mesh['feat'=16,'dom'=16] {'dom'}, dimensions={0} | all-to-all | bytes 1048576 | tf_op jit(solution)/shard_map/all_to_all | solution.py:229
  153.7 0.9 place.1
  (45 shorter events, 6.5 us)
Async XLA Ops:
  0.6 12.7 %collective-permute-start = (bf16[64,9216]{1,0:T(8,128)(2,1)}, bf16[64,9216]{1,0:T(8,128)(2,1)S(1)}, u32[]{:S(2)}, u32[]{:S(2)}) collective-permute-start(bf16[64,9216]{1,0:T(8,128)(2,1)} %bitcast.23), channel_id=1, source_target_pairs={{0,16},{16,0},{32,48},{48,32},{64,80},{80,64},{96,112},{112,96},{1... | collective-permute-start | bytes 3538952 | tf_op jit(solution)/shard_map/ppermute | solution.py:244
  4.0 9.4 %collective-permute-start.1 = (bf16[64,256]{1,0:T(8,128)(2,1)}, bf16[64,256]{1,0:T(8,128)(2,1)S(1)}, u32[]{:S(2)}, u32[]{:S(2)}) collective-permute-start(bf16[64,256]{1,0:T(8,128)(2,1)} %ws_ref.1), channel_id=1, source_target_pairs={{0,16},{16,0},{32,48},{48,32},{64,80},{80,64},{96,112},{112,96},{1... | collective-permute-start | bytes 98312 | tf_op jit(solution)/shard_map/ppermute | solution.py:244
  4.1 9.3 %collective-permute-start.2 = (bf16[64,256]{1,0:T(8,128)(2,1)}, bf16[64,256]{1,0:T(8,128)(2,1)S(1)}, u32[]{:S(2)}, u32[]{:S(2)}) collective-permute-start(bf16[64,256]{1,0:T(8,128)(2,1)} %wn_ref.1), channel_id=1, source_target_pairs={{0,16},{16,0},{32,48},{48,32},{64,80},{80,64},{96,112},{112,96},{1... | collective-permute-start | bytes 98312 | tf_op jit(solution)/shard_map/ppermute | solution.py:244
  8.3 31.9 %all-to-all-start.1 = ((bf16[16,128,256]{2,1,0:T(8,128)(2,1)}), bf16[16,128,256]{2,1,0:T(8,128)(2,1)S(1)}, u32[]{:S(2)}, u32[]{:S(2)}) async-start(bf16[16,128,256]{2,1,0:T(8,128)(2,1)} %picks.1), calls=%async_computation.1 | async-start | bytes 2097152 | tf_op jit(solution)/shard_map/all_to_all | solution.py:229
  40.1 39.2 %copy-start = (bf16[1,1,256,256]{3,2,1,0:T(8,128)(2,1)S(1)}, bf16[1,1,256,256]{3,2,1,0:T(8,128)(2,1)}, u32[]{:S(2)}) copy-start(bf16[1,1,256,256]{3,2,1,0:T(8,128)(2,1)} %param.21) | copy-start | bytes 393220
  40.1 39.2 %copy-start.1 = (bf16[256,256]{1,0:T(8,128)(2,1)S(1)}, bf16[256,256]{1,0:T(8,128)(2,1)}, u32[]{:S(2)}) copy-start(bf16[256,256]{1,0:T(8,128)(2,1)} %w2s_ref.3) | copy-start | bytes 393220
  40.1 39.2 %copy-start.2 = (bf16[256,256]{1,0:T(8,128)(2,1)S(1)}, bf16[256,256]{1,0:T(8,128)(2,1)}, u32[]{:S(2)}) copy-start(bf16[256,256]{1,0:T(8,128)(2,1)} %w2n_ref.3) | copy-start | bytes 393220
  40.2 39.1 %copy-start.4 = (s32[1,1,16,128]{3,2,1,0:T(8,128)S(1)}, s32[1,1,16,128]{3,2,1,0:T(8,128)}, u32[]{:S(2)}) copy-start(s32[1,1,16,128]{3,2,1,0:T(8,128)} %param.17) | copy-start | bytes 24580
  40.2 39.1 %copy-start.5 = (s32[1,1,256]{2,1,0:T(1,128)S(1)}, s32[1,1,256]{2,1,0:T(1,128)}, u32[]{:S(2)}) copy-start(s32[1,1,256]{2,1,0:T(1,128)} %param.20) | copy-start | bytes 3076
  80.8 4.1 %collective-permute-start.4 = (bf16[288,256]{1,0:T(8,128)(2,1)S(1)}, bf16[288,256]{1,0:T(8,128)(2,1)S(1)}, u32[]{:S(2)}, u32[]{:S(2)}) collective-permute-start(bf16[288,256]{1,0:T(8,128)(2,1)S(1)} %get-tuple-element.35.refs_0_), channel_id=1, source_target_pairs={{0,224},{16,240},{32,0},{48,16},{64,32},{80,48},{96,64},{112,80},{... | collective-permute-start | bytes 442376 | tf_op jit(solution)/shard_map/ppermute | solution.py:235
  80.9 5.3 %collective-permute-start.3 = (bf16[288,256]{1,0:T(8,128)(2,1)S(1)}, bf16[288,256]{1,0:T(8,128)(2,1)S(1)}, u32[]{:S(2)}, u32[]{:S(2)}) collective-permute-start(bf16[288,256]{1,0:T(8,128)(2,1)S(1)} %get-tuple-element.35.refs_0_), channel_id=1, source_target_pairs={{0,32},{16,48},{32,64},{48,80},{64,96},{80,112},{96,128},{112,144}... | collective-permute-start | bytes 442376 | tf_op jit(solution)/shard_map/ppermute | solution.py:235
  86.2 24.4 %all-to-all-start.2 = ((bf16[16,320,128]{2,1,0:T(8,128)(2,1)}), bf16[16,320,128]{2,1,0:T(8,128)(2,1)S(1)}, u32[]{:S(2)}, u32[]{:S(2)}) async-start(bf16[16,320,128]{2,1,0:T(8,128)(2,1)} %get-tuple-element.46), calls=%async_computation.2 | async-start | bytes 2621440 | tf_op jit(solution)/shard_map/all_to_all | solution.py:229
  92.5 5.3 %collective-permute-start.5 = (bf16[288,256]{1,0:T(8,128)(2,1)S(1)}, bf16[288,256]{1,0:T(8,128)(2,1)S(1)}, u32[]{:S(2)}, u32[]{:S(2)}) collective-permute-start(bf16[288,256]{1,0:T(8,128)(2,1)S(1)} %collective-permute-done.3.refs_1_), channel_id=1, source_target_pairs={{0,32},{16,48},{32,64},{48,80},{64,96},{80,112},{96,128},{112,144}... | collective-permute-start | bytes 442376 | tf_op jit(solution)/shard_map/ppermute | solution.py:235
  93.0 4.7 %collective-permute-start.6 = (bf16[288,256]{1,0:T(8,128)(2,1)S(1)}, bf16[288,256]{1,0:T(8,128)(2,1)S(1)}, u32[]{:S(2)}, u32[]{:S(2)}) collective-permute-start(bf16[288,256]{1,0:T(8,128)(2,1)S(1)} %collective-permute-done.4.refs_2_), channel_id=1, source_target_pairs={{0,224},{16,240},{32,0},{48,16},{64,32},{80,48},{96,64},{112,80},{... | collective-permute-start | bytes 442376 | tf_op jit(solution)/shard_map/ppermute | solution.py:235
  97.8 5.8 %collective-permute-start.7 = (bf16[288,256]{1,0:T(8,128)(2,1)S(1)}, bf16[288,256]{1,0:T(8,128)(2,1)S(1)}, u32[]{:S(2)}, u32[]{:S(2)}) collective-permute-start(bf16[288,256]{1,0:T(8,128)(2,1)S(1)} %collective-permute-done.5.refs_3_), channel_id=1, source_target_pairs={{0,32},{16,48},{32,64},{48,80},{64,96},{80,112},{96,128},{112,144}... | collective-permute-start | bytes 442376 | tf_op jit(solution)/shard_map/ppermute | solution.py:235
  97.8 5.8 %collective-permute-start.8 = (bf16[288,256]{1,0:T(8,128)(2,1)S(1)}, bf16[288,256]{1,0:T(8,128)(2,1)S(1)}, u32[]{:S(2)}, u32[]{:S(2)}) collective-permute-start(bf16[288,256]{1,0:T(8,128)(2,1)S(1)} %collective-permute-done.6.refs_4_), channel_id=1, source_target_pairs={{0,224},{16,240},{32,0},{48,16},{64,32},{80,48},{96,64},{112,80},{... | collective-permute-start | bytes 442376 | tf_op jit(solution)/shard_map/ppermute | solution.py:235
  103.6 7.0 %collective-permute-start.9 = (bf16[288,256]{1,0:T(8,128)(2,1)S(1)}, bf16[288,256]{1,0:T(8,128)(2,1)S(1)}, u32[]{:S(2)}, u32[]{:S(2)}) collective-permute-start(bf16[288,256]{1,0:T(8,128)(2,1)S(1)} %collective-permute-done.7.refs_5_), channel_id=1, source_target_pairs={{0,32},{16,48},{32,64},{48,80},{64,96},{80,112},{96,128},{112,144}... | collective-permute-start | bytes 442376 | tf_op jit(solution)/shard_map/ppermute | solution.py:235
  111.9 15.8 %copy-start.3 = (s32[1,1,256,15]{2,1,3,0:T(1,128)S(1)}, s32[1,1,256,15]{2,1,3,0:T(1,128)}, u32[]{:S(2)}) copy-start(s32[1,1,256,15]{2,1,3,0:T(1,128)} %param.19) | copy-start | bytes 46084
  111.9 15.8 %copy-start.6 = (s32[16,1,1]{0,2,1:T(1,128)S(1)}, s32[16,1,1]{0,2,1:T(1,128)}, u32[]{:S(2)}) copy-start(s32[16,1,1]{0,2,1:T(1,128)} %param.18) | copy-start | bytes 196
  112.7 10.3 %collective-permute-start.10 = (f32[128,256]{1,0:T(8,128)S(1)}, f32[128,256]{1,0:T(8,128)S(1)}, u32[]{:S(2)}, u32[]{:S(2)}) collective-permute-start(f32[128,256]{1,0:T(8,128)S(1)} %get-tuple-element.51), channel_id=1, source_target_pairs={{0,16},{16,0},{32,48},{48,32},{64,80},{80,64},{96,112},{112,96},{1... | collective-permute-start | bytes 393224 | tf_op jit(solution)/shard_map/ppermute | solution.py:244
  119.2 15.5 %all-to-all-start.3 = ((bf16[16,64,128]{2,1,0:T(8,128)(2,1)}), bf16[16,64,128]{2,1,0:T(8,128)(2,1)S(1)}, u32[]{:S(2)}, u32[]{:S(2)}) async-start(bf16[16,64,128]{2,1,0:T(8,128)(2,1)} %sum_dom.1), calls=%async_computation.3 | async-start | bytes 524288 | tf_op jit(solution)/shard_map/all_to_all | solution.py:229
  123.0 8.1 %collective-permute-start.13 = (bf16[128,256]{1,0:T(8,128)(2,1)S(1)}, bf16[128,256]{1,0:T(8,128)(2,1)S(1)}, u32[]{:S(2)}, u32[]{:S(2)}) collective-permute-start(bf16[128,256]{1,0:T(8,128)(2,1)S(1)} %get-tuple-element.61), channel_id=1, source_target_pairs={{0,12},{1,13},{2,14},{3,15},{4,0},{5,1},{6,2},{7,3},{8,4},{9,5},{1... | collective-permute-start | bytes 196616 | tf_op jit(solution)/shard_map/ppermute | solution.py:240
  126.6 4.9 %collective-permute-start.12 = (bf16[128,256]{1,0:T(8,128)(2,1)S(1)}, bf16[128,256]{1,0:T(8,128)(2,1)S(1)}, u32[]{:S(2)}, u32[]{:S(2)}) collective-permute-start(bf16[128,256]{1,0:T(8,128)(2,1)S(1)} %get-tuple-element.61), channel_id=1, source_target_pairs={{0,8},{1,9},{2,10},{3,11},{4,12},{5,13},{6,14},{7,15},{8,0},{9,1},... | collective-permute-start | bytes 196616 | tf_op jit(solution)/shard_map/ppermute | solution.py:240
  127.2 6.0 %collective-permute-start.11 = (bf16[128,256]{1,0:T(8,128)(2,1)S(1)}, bf16[128,256]{1,0:T(8,128)(2,1)S(1)}, u32[]{:S(2)}, u32[]{:S(2)}) collective-permute-start(bf16[128,256]{1,0:T(8,128)(2,1)S(1)} %get-tuple-element.61), channel_id=1, source_target_pairs={{0,4},{1,5},{2,6},{3,7},{4,8},{5,9},{6,10},{7,11},{8,12},{9,13},{1... | collective-permute-start | bytes 196616 | tf_op jit(solution)/shard_map/ppermute | solution.py:240
  (4 other events, 3.6 us)
